TPU v7x, 32 devices: a whole 2x2x4 slice. The times are simulated.
32 devices in a mesh: worker: 8 (over z, x), tok: 4 (over y, core).
Axes of the slice: x: 2, y: 2, z: 4, core: 2. Of those that a mesh axis runs over, the one named last changes fastest.
Arguments:
- inputs: bfloat16 [8, 6144, 2048], P('worker', 'tok'), may hold values from -6 to 6
- cotangent: bfloat16 [8, 6144, 1024], P('worker', 'tok'), may hold values from -0.076171875 to 0.076171875
- weights: float32 [8, 2048, 1024], P('worker', 'tok'), may hold values from -12 to 12
- momentum: float32 [8, 2048, 1024], P('worker', 'tok'), may hold values from -6 to 6
- mix_weights: int32 [8, 5], P('worker'), may hold values from 1 to 5
- clip_radius: int32 [2], replicated, may hold values from 700 to 2299
Outputs:
- new_weights: float32 [8, 2048, 1024], P('worker', 'tok')
- new_momentum: float32 [8, 2048, 1024], P('worker', 'tok')
All inputs are finite; a program needn't handle non-finite values.
Results may differ from a plain program's by a relative error of at most 0.0003.
Values sent between devices are 32-bit elements; how exact they have to be, the bound alone decides.
No kernel may reach another device: no remote copies, remote signals or barrier semaphores. Data moves between devices by JAX's collectives and lax.ppermute only.
A program may use at most 64 MiB of HBM per device.

v0:
```python
import math

import jax
import jax.numpy as jnp
from jax import lax
from jax.sharding import PartitionSpec as P

D = 2048
KV_WIDTH = 512
ROUNDS = 2


LEARNING_RATE = 0.25


def partner(value, axis, apart):
    mask = 2**apart
    pairs = [(source, source ^ mask) for source in range(lax.axis_size(axis))]
    return lax.ppermute(value, axis, pairs)


def shifted(block, axis, distance):
    devices = range(lax.axis_size(axis))
    route = [((i - distance) % len(devices), i) for i in devices]
    return lax.ppermute(block, axis, route)


def gradient_rows(features, columns):
    return lax.dot_general(
        features, columns, (((0,), (0,)), ((), ())), preferred_element_type=jnp.float32
    )


def per_device(inputs, cotangent, weights, momentum, mix_weights, clip_radius):
    features = inputs[0]
    upstream = cotangent[0]
    current = weights[0]
    previous = momentum[0]
    half_width = upstream.shape[1] // 2
    local_rows = current.shape[0]
    gradient = lax.psum_scatter(
        gradient_rows(features, upstream), "tok", scatter_dimension=0, tiled=True
    )
    velocity = 0.5 * previous + gradient
    current = current - LEARNING_RATE * velocity
    mixing = mix_weights[0].astype(jnp.float32)
    shares = mixing / jnp.sum(mixing)
    radius_all = clip_radius.astype(jnp.float32) * (math.sqrt(D * KV_WIDTH) / 1000.0)
    for round_index in range(ROUNDS):
        radius = radius_all[round_index]
        neighbours = (
            partner(current, "worker", 0),
            partner(current, "worker", 1),
            shifted(current, "worker", 4),
            shifted(current, "worker", -4),
        )
        halves_list = [
            (neighbour - current).reshape(local_rows, 2, half_width) for neighbour in neighbours
        ]
        squares = jnp.stack([jnp.sum(halves * halves, axis=(0, 2)) for halves in halves_list])
        totals = lax.psum(squares, "tok")
        distance_rows = [totals[position] for position in range(4)]
        mixed_step = jnp.zeros((local_rows, 2, half_width), jnp.float32)
        for position in range(4):
            factor = radius / jnp.maximum(jnp.sqrt(distance_rows[position]), radius)
            mixed_step = (
                mixed_step + halves_list[position] * (shares[position + 1] * factor)[None, :, None]
            )
        current = current + mixed_step.reshape(current.shape)
    return (current[None], velocity[None])


def solution(mesh):
    placed = (
        P("worker", "tok", None),
        P("worker", "tok", None),
        P("worker", "tok", None),
        P("worker", "tok", None),
        P("worker", None),
        P(),
    )
    return jax.shard_map(
        per_device,
        mesh=mesh,
        in_specs=placed,
        out_specs=(P("worker", "tok", None), P("worker", "tok", None)),
        check_vma=False,
    )
```

profile of v0, /device:TPU:0, one launch (start us, length us, event | category | flops | bytes accessed | tf_op | source)
XLA Modules:
  0.0 334.0 jit_solution(2159878431121370692)
XLA Ops:
  7.2 1.8 copy-done
  9.1 10.8 %fusion = f32[2048,1024]{1,0:T(8,128)} fusion(bf16[1,1536,2048]{2,1,0:T(8,128)(2,1)} %param.6, bf16[1,1536,1024]{2,1,0:T(8,128)(2,1)S(1)} %copy-done), kind=kOutput, calls=%fused_computation | convolution fusion | flops 6442450944 | bytes 17825792 | tf_op jit(solution)/shard_map/dot_general | solution.py:29
  19.9 74.2 %reduce-scatter.2.cloned.1.call-done = f32[512,1024]{1,0:T(8,128)} async-done(((f32[2048,1024]{1,0:T(8,128)}), f32[512,1024]{1,0:T(8,128)}) %reduce-scatter.2.cloned.1.call-update) | async-done | bytes 2097168 | tf_op jit(solution)/shard_map/reduce_scatter | solution.py:41
  94.2 5.3 %fusion.3 = (f32[1,512,1024]{2,1,0:T(8,128)}, f32[512,1024]{1,0:T(8,128)S(1)}) fusion(f32[512,1024]{1,0:T(8,128)} %reduce-scatter.2.cloned.1.call-done, f32[1,512,1024]{2,1,0:T(8,128)} %param.9, f32[1,512,1024]{2,1,0:T(8,128)} %param.8), kind=kLoop, calls=%fused_computation.13 | loop fusion | flops 2097152 | bytes 10485760 | tf_op jit(solution)/shard_map/broadcast_in_dim | solution.py:70
  99.5 1.5 collective-permute-start
  101.0 1.5 collective-permute-start.1
  102.5 2.4 collective-permute-start.2
  104.9 0.7 convert_reduce_fusion
  105.6 0.7 convert_divide_fusion
  106.9 39.8 %collective-permute-done = f32[512,1024]{1,0:T(8,128)S(1)} collective-permute-done((f32[512,1024]{1,0:T(8,128)S(1)}, f32[512,1024]{1,0:T(8,128)S(1)}, u32[]{:S(2)}, u32[]{:S(2)}) %collective-permute-start) | collective-permute-done | bytes 2097184 | tf_op jit(solution)/shard_map/ppermute | solution.py:19
  146.7 45.9 %collective-permute-done.1 = f32[512,1024]{1,0:T(8,128)S(1)} collective-permute-done((f32[512,1024]{1,0:T(8,128)S(1)}, f32[512,1024]{1,0:T(8,128)S(1)}, u32[]{:S(2)}, u32[]{:S(2)}) %collective-permute-start.1) | collective-permute-done | bytes 2097184 | tf_op jit(solution)/shard_map/ppermute | solution.py:19
  192.6 2.4 collective-permute-done.2
  195.0 4.0 %multiply_reduce_fusion.5 = (f32[1024]{0:T(1024)S(1)}, f32[512,1024]{1,0:T(8,128)}, f32[1024]{0:T(1024)S(1)}, f32[512,1024]{1,0:T(8,128)}, f32[1024]{0:T(1024)S(1)}, /*index=5*/f32[512,1024]{1,0:T(8,128)}) fusion(f32[512,1024]{1,0:T(8,128)S(1)} %collective-permute-done, f32[512,1024]{1,0:T(8,128)S(1)} %get-tuple-element.15, ...), kind=kLoop, calls=%fused_computation.12 | loop fusion | flops 4715520 | bytes 14692352 | tf_op jit(solution)/shard_map/reduce_sum | solution.py:60
  200.0 5.9 %psum.14 = f32[4,2]{1,0:T(4,128)S(1)} all-reduce(f32[4,2]{1,0:T(4,128)S(1)} %pad_maximum_fusion), channel_id=1, replica_groups=mesh['worker'=8,'tok'=4] {'tok'}, use_global_device_ids=true, to_apply=%region_8.0 | all-reduce | flops 8 | bytes 64 | tf_op jit(solution)/shard_map/psum | solution.py:61
  205.9 3.2 multiply_bitcast_fusion.7
  209.2 4.7 %add_add_fusion = f32[512,1024]{1,0:T(8,128)S(1)} fusion(f32[512,1024]{1,0:T(8,128)} %copy-done.1, f32[512,1024]{1,0:T(8,128)} %get-tuple-element.21, f32[512,1024]{1,0:T(8,128)} %get-tuple-element.23, f32[512,1024]{1,0:T(8,128)} %get-tuple-element.9, f32[1024]{0:T(1024)S(1)} %bitcast.76, f32[1024]{0:T(1024)S(1)} %bitcast.75, f32[1024]{0:T(1024)S(1)} %bitcast.72, ...), kind=kLoop, calls=%fused_computation.9 | loop fusion | flops 4194304 | bytes 10502144 | tf_op jit(solution)/shard_map/add | solution.py:69
  214.9 2.6 collective-permute-start.5
  217.5 43.6 %collective-permute-done.3 = f32[512,1024]{1,0:T(8,128)S(1)} collective-permute-done((f32[512,1024]{1,0:T(8,128)S(1)}, f32[512,1024]{1,0:T(8,128)S(1)}, u32[]{:S(2)}, u32[]{:S(2)}) %collective-permute-start.3) | collective-permute-done | bytes 2097184 | tf_op jit(solution)/shard_map/ppermute | solution.py:19
  261.1 44.9 %collective-permute-done.4 = f32[512,1024]{1,0:T(8,128)S(1)} collective-permute-done((f32[512,1024]{1,0:T(8,128)S(1)}, f32[512,1024]{1,0:T(8,128)S(1)}, u32[]{:S(2)}, u32[]{:S(2)}) %collective-permute-start.4) | collective-permute-done | bytes 2097184 | tf_op jit(solution)/shard_map/ppermute | solution.py:19
  306.1 1.3 collective-permute-done.5
  307.4 4.0 %multiply_reduce_fusion.2 = (f32[1024]{0:T(1024)S(1)}, f32[512,1024]{1,0:T(8,128)}, f32[1024]{0:T(1024)S(1)}, f32[512,1024]{1,0:T(8,128)}, f32[1024]{0:T(1024)S(1)}, /*index=5*/f32[512,1024]{1,0:T(8,128)}) fusion(f32[512,1024]{1,0:T(8,128)S(1)} %collective-permute-done.3, f32[512,1024]{1,0:T(8,128)S(1)} %add_add_fusion, ...), kind=kLoop, calls=%fused_computation.8 | loop fusion | flops 4715520 | bytes 14692352 | tf_op jit(solution)/shard_map/reduce_sum | solution.py:60
  311.8 6.0 %psum.15 = f32[4,2]{1,0:T(4,128)S(1)} all-reduce(f32[4,2]{1,0:T(4,128)S(1)} %pad_maximum_fusion.1), channel_id=1, replica_groups=mesh['worker'=8,'tok'=4] {'tok'}, use_global_device_ids=true, to_apply=%region_15.16 | all-reduce | flops 8 | bytes 64 | tf_op jit(solution)/shard_map/psum | solution.py:61
  317.7 3.1 multiply_bitcast_fusion.3
  321.1 6.0 %add_bitcast_fusion = f32[1,512,1024]{2,1,0:T(8,128)} fusion(f32[512,1024]{1,0:T(8,128)} %copy-done.2, f32[512,1024]{1,0:T(8,128)} %get-tuple-element.17, f32[512,1024]{1,0:T(8,128)} %get-tuple-element.19, f32[512,1024]{1,0:T(8,128)} %get-tuple-element.3, f32[1024]{0:T(1024)S(1)} %bitcast.77, f32[1024]{0:T(1024)S(1)} %bitcast.74, f32[1024]{0:T(1024)S(1)} %bitcast.73, ...), kind=kLoop, calls=%fused_computation.5 | loop fusion | flops 4194304 | bytes 10502144 | tf_op jit(solution)/shard_map/broadcast_in_dim | solution.py:70
  (44 shorter events, 3.6 us)
Async XLA Ops:
  7.2 1.9 copy-start
  7.2 87.0 %reduce-scatter.2.cloned.1.call-start = ((), (), s32[]{:S(2)}) async-start(), calls=%async_computation.1 | async-start | bytes 10485760 | tf_op jit(solution)/shard_map/reduce_scatter | solution.py:41
  19.9 85.0 %copy-start.3 = (s32[1,5]{1,0:T(1,128)S(1)}, s32[1,5]{1,0:T(1,128)}, u32[]{:S(2)}) copy-start(s32[1,5]{1,0:T(1,128)} %param.10) | copy-start | bytes 64
  19.9 87.0 %copy-start.4 = (s32[2]{0:T(128)S(1)}, s32[2]{0:T(128)}, u32[]{:S(2)}) copy-start(s32[2]{0:T(128)} %param.11) | copy-start | bytes 28
  99.5 99.5 %copy-start.1 = (f32[512,1024]{1,0:T(8,128)}, f32[512,1024]{1,0:T(8,128)S(1)}, u32[]{:S(2)}) copy-start(f32[512,1024]{1,0:T(8,128)S(1)} %get-tuple-element.15) | copy-start | bytes 6291460
  99.5 47.2 %collective-permute-start = (f32[512,1024]{1,0:T(8,128)S(1)}, f32[512,1024]{1,0:T(8,128)S(1)}, u32[]{:S(2)}, u32[]{:S(2)}) collective-permute-start(f32[512,1024]{1,0:T(8,128)S(1)} %get-tuple-element.15), channel_id=1, source_target_pairs={{0,4},{4,0},{8,12},{12,8},{16,20},{20,16},{24,28},{28,24},{1,5},{5... | collective-permute-start | bytes 6291464 | tf_op jit(solution)/shard_map/ppermute | solution.py:19
  101.0 91.6 %collective-permute-start.1 = (f32[512,1024]{1,0:T(8,128)S(1)}, f32[512,1024]{1,0:T(8,128)S(1)}, u32[]{:S(2)}, u32[]{:S(2)}) collective-permute-start(f32[512,1024]{1,0:T(8,128)S(1)} %get-tuple-element.15), channel_id=1, source_target_pairs={{0,8},{4,12},{8,0},{12,4},{16,24},{20,28},{24,16},{28,20},{1,9},{5... | collective-permute-start | bytes 6291464 | tf_op jit(solution)/shard_map/ppermute | solution.py:19
  102.5 92.6 %collective-permute-start.2 = (f32[512,1024]{1,0:T(8,128)S(1)}, f32[512,1024]{1,0:T(8,128)S(1)}, u32[]{:S(2)}, u32[]{:S(2)}) collective-permute-start(f32[512,1024]{1,0:T(8,128)S(1)} %get-tuple-element.15), channel_id=1, source_target_pairs={{16,0},{20,4},{24,8},{28,12},{0,16},{4,20},{8,24},{12,28},{17,1},{... | collective-permute-start | bytes 6291464 | tf_op jit(solution)/shard_map/ppermute | solution.py:25
  213.9 97.4 %copy-start.2 = (f32[512,1024]{1,0:T(8,128)}, f32[512,1024]{1,0:T(8,128)S(1)}, u32[]{:S(2)}) copy-start(f32[512,1024]{1,0:T(8,128)S(1)} %add_add_fusion) | copy-start | bytes 6291460
  213.9 47.2 %collective-permute-start.3 = (f32[512,1024]{1,0:T(8,128)S(1)}, f32[512,1024]{1,0:T(8,128)S(1)}, u32[]{:S(2)}, u32[]{:S(2)}) collective-permute-start(f32[512,1024]{1,0:T(8,128)S(1)} %add_add_fusion), channel_id=1, source_target_pairs={{0,4},{4,0},{8,12},{12,8},{16,20},{20,16},{24,28},{28,24},{1,5},{5... | collective-permute-start | bytes 6291464 | tf_op jit(solution)/shard_map/ppermute | solution.py:19
  214.6 91.5 %collective-permute-start.4 = (f32[512,1024]{1,0:T(8,128)S(1)}, f32[512,1024]{1,0:T(8,128)S(1)}, u32[]{:S(2)}, u32[]{:S(2)}) collective-permute-start(f32[512,1024]{1,0:T(8,128)S(1)} %add_add_fusion), channel_id=1, source_target_pairs={{0,8},{4,12},{8,0},{12,4},{16,24},{20,28},{24,16},{28,20},{1,9},{5... | collective-permute-start | bytes 6291464 | tf_op jit(solution)/shard_map/ppermute | solution.py:19
  214.9 92.4 %collective-permute-start.5 = (f32[512,1024]{1,0:T(8,128)S(1)}, f32[512,1024]{1,0:T(8,128)S(1)}, u32[]{:S(2)}, u32[]{:S(2)}) collective-permute-start(f32[512,1024]{1,0:T(8,128)S(1)} %add_add_fusion), channel_id=1, source_target_pairs={{16,0},{20,4},{24,8},{28,12},{0,16},{4,20},{8,24},{12,28},{17,1},{... | collective-permute-start | bytes 6291464 | tf_op jit(solution)/shard_map/ppermute | solution.py:25
Sparse Core Ops, SparseCore 0:
  20.0 74.1 reduce-scatter.1
where the time goes:
time: 334 us
  waiting for transfers between devices  252 us (75%)
  other arithmetic  32.3 us (10%)
  between operations  14.1 us (4%)
  blocking collectives  11.9 us (4%)
  matrix products  10.8 us (3%)
  starting transfers between devices  9.01 us (3%)
  local copies, waits for them, and re-layouts  3.61 us (1%)
    ppermute x4, waiting for transfers between devices, partner(): return lax.ppermute(value, axis, pairs)  174 us
    reduce_scatter x1, waiting for transfers between devices, per_device(): lax.psum_scatter(gradient_rows(features, upstream), 'tok', scatter_dimens...  74.2 us
    psum x2, blocking collectives, per_device(): totals = lax.psum(squares, 'tok')  11.9 us
    broadcast_in_dim x2, other arithmetic, per_device(): return (current[None], velocity[None])  11.4 us
    dot_general x1, matrix products, gradient_rows(): lax.dot_general(features, columns, (((0,), (0,)), ((), ())), preferred_el...  10.8 us
    reduce_sum x8, other arithmetic, per_device(): jnp.sum(halves * halves, axis=(0, 2))  8.67 us
  transfers between devices with their start and end apart: 7, of which 7 were waited for; matrix products, arithmetic and copies ran while one was open for 1% of the time, Pallas kernels for 0%

commit v1 on v0

v1 whole, which is shorter than its diff:
```python
import math

import jax
import jax.numpy as jnp
from jax import lax
from jax.sharding import PartitionSpec as P

D = 2048
KV_WIDTH = 512
ROUNDS = 2
LEARNING_RATE = 0.25
HIGH = lax.Precision.HIGHEST


def flip(value, axis, mask):
    pairs = [(source, source ^ mask) for source in range(lax.axis_size(axis))]
    return lax.ppermute(value, axis, pairs)


def chunk_units(rows, workers):
    units = rows // (8 * workers)
    count = min(4, units)
    return [units // count * 8 * workers] * count


def neighbour_table(workers):
    table = []
    for w in range(workers):
        table.append([w ^ 1, w ^ 2, (w - 4) % workers, (w + 4) % workers])
    return table


def mixing_matrices(squares, mixing, radius_all):
    workers = squares.shape[1]
    shares = mixing / jnp.sum(mixing, axis=1, keepdims=True)
    select = jnp.zeros((workers, workers), jnp.float32)
    table = jnp.array(neighbour_table(workers), jnp.int32)
    columns = jnp.arange(workers, dtype=jnp.int32)
    for k in range(4):
        hit = (table[:, k][:, None] == columns[None, :]).astype(jnp.float32)
        select = select + hit * shares[:, k + 1][:, None]
    eye = (columns[:, None] == columns[None, :]).astype(jnp.float32)[None]
    total = jnp.broadcast_to(eye, squares.shape)
    now = squares
    for r in range(ROUNDS):
        radius = radius_all[r]
        factor = radius / jnp.maximum(jnp.sqrt(jnp.maximum(now, 0.0)), radius)
        step = select[None] * factor
        step = step + eye * (1.0 - jnp.sum(step, axis=2, keepdims=True))
        total = jnp.einsum("hij,hjk->hik", step, total, precision=HIGH)
        if r + 1 < ROUNDS:
            inner = jnp.einsum("hij,hjk->hik", total, squares, precision=HIGH)
            inner = jnp.einsum("hik,hlk->hil", inner, total, precision=HIGH)
            diag = jnp.sum(inner * eye, axis=2)
            now = inner - 0.5 * (diag[:, :, None] + diag[:, None, :])
    return total


def per_device(inputs, cotangent, weights, momentum, mix_weights, clip_radius):
    features, upstream = inputs[0], cotangent[0]
    tokens = lax.axis_size("tok")
    workers = lax.axis_size("worker")
    tok, me = lax.axis_index("tok"), lax.axis_index("worker")
    rows, width = weights.shape[1:]
    half = width // 2

    def partial_rows(offset, start, size):
        block = lax.dynamic_slice_in_dim(features, (tok ^ offset) * rows + start, size, axis=1)
        return lax.dot_general(block, upstream, (((0,), (0,)), ((), ())), preferred_element_type=jnp.float32)

    def reduced(offset, level, start, size):
        if level == 0:
            return partial_rows(offset, start, size)
        mask = 1 << (level - 1)
        away = reduced(offset ^ mask, level - 1, start, size)
        return reduced(offset, level - 1, start, size) + flip(away, "tok", mask)

    levels = tokens.bit_length() - 1
    start = 0
    velocities, gathered = [], []
    for size in chunk_units(rows, workers):
        gradient = reduced(0, levels, start, size)
        velocity = 0.5 * momentum[0, start : start + size] + gradient
        current = weights[0, start : start + size] - LEARNING_RATE * velocity
        velocities.append(velocity)
        gathered.append(
            lax.all_to_all(current.reshape(workers, size // workers, width), "worker", 0, 0, tiled=True)
        )
        start += size
    squares = jnp.zeros((2, workers, workers), jnp.float32)
    pairs = {}
    for block in gathered:
        for a in range(workers):
            for b in range(a + 1, workers):
                gap = block[a] - block[b]
                gap = jnp.sum((gap * gap).reshape(-1, 2, half), axis=(0, 2))
                pairs[a, b] = pairs[a, b] + gap if (a, b) in pairs else gap
    zero = jnp.zeros((2,), jnp.float32)
    squares = jnp.stack(
        [jnp.stack([zero if a == b else pairs[min(a, b), max(a, b)] for b in range(workers)], 1) for a in range(workers)], 1
    )
    mine = (jnp.arange(workers) == me).astype(jnp.float32)[:, None]
    mixing = mine * mix_weights.astype(jnp.float32) * (1.0 / tokens)
    packed = jnp.concatenate([squares.reshape(-1), mixing.reshape(-1)])
    packed = jnp.pad(packed, (0, -packed.size % 1024)).reshape(-1, 128)
    for axis, size in (("tok", tokens), ("worker", workers)):
        mask = 1
        while mask < size:
            packed = packed + flip(packed, axis, mask)
            mask *= 2
    packed = packed.reshape(-1)
    squares = packed[: 2 * workers * workers].reshape(2, workers, workers)
    mixing = packed[2 * workers * workers :][: workers * 5].reshape(workers, 5)
    radius_all = clip_radius.astype(jnp.float32) * (math.sqrt(D * KV_WIDTH) / 1000.0)
    matrix = mixing_matrices(squares, mixing, radius_all)
    news = []
    for block in gathered:
        mixed = []
        for w in range(workers):
            total = 0.0
            for j in range(workers):
                scale = jnp.repeat(matrix[:, w, j], half)
                total = total + block[j] * scale[None, :]
            mixed.append(total)
        news.append(jnp.stack(mixed))
    news = jnp.concatenate(news, axis=1)
    news = lax.all_to_all(news, "worker", 0, 0, tiled=True)
    out, start = [], 0
    for block in gathered:
        size = block.shape[1]
        out.append(news[:, start : start + size].reshape(-1, width))
        start += size
    return jnp.concatenate(out)[None], jnp.concatenate(velocities)[None]


def solution(mesh):
    placed = (
        P("worker", "tok", None),
        P("worker", "tok", None),
        P("worker", "tok", None),
        P("worker", "tok", None),
        P("worker", None),
        P(),
    )
    return jax.shard_map(
        per_device,
        mesh=mesh,
        in_specs=placed,
        out_specs=(P("worker", "tok", None), P("worker", "tok", None)),
        check_vma=False,
    )
```

time: 334 us -> 275 us (0.82)
  waiting for transfers between devices: 252 us -> 107 us
  blocking collectives: 11.9 us -> 37.9 us
  matrix products: 10.8 us -> 35.6 us
  other arithmetic: 32.3 us -> 53.1 us
  starting transfers between devices: 9.01 us -> 24.7 us
  between operations: 14.1 us -> 1.38 us
  local copies, waits for them, and re-layouts: 3.61 us -> 12.8 us
    ppermute x6 -> x17, waiting for transfers between devices: 178 us -> 46.4 us  [flip(): return lax.ppermute(value, axis, pairs)]
    reduce_scatter x1 -> x0, waiting for transfers between devices: 74.2 us -> none  [per_device(): lax.psum_scatter(gradient_rows(features, upstream), 'tok', scatter_dimens...]
    all_to_all x0 -> x3, waiting for transfers between devices: none -> 60.8 us  [the longest x1 41.3 us: per_device(): news = lax.all_to_all(news, 'worker', 0, 0, tiled=True)]
    all_to_all x0 -> x2, blocking collectives: none -> 37.9 us  [per_device(): lax.all_to_all(current.reshape(workers, size // workers, width), 'worker'...]
    dot_general x1 -> x20, matrix products: 10.8 us -> 35.6 us  [the longest x16 33.5 us: partial_rows(): lax.dot_general(block, upstream, (((0,), (0,)), ((), ())), preferred_elem...]
    unnamed x0 -> x28, other arithmetic: none -> 18.6 us
    reduce_sum x9 -> x123, other arithmetic: 9.36 us -> 25.4 us  [the longest x120 23.8 us: per_device(): gap = jnp.sum((gap * gap).reshape(-1, 2, half), axis=(0, 2))]
    all_to_all x0 -> x3, starting transfers between devices: none -> 12.8 us  [the longest x2 8.47 us: per_device(): lax.all_to_all(current.reshape(workers, size // workers, width), 'worker'...]
  transfers between devices with their start and end apart: 7 -> 20, of which waited for: 7 -> 12; matrix products, arithmetic and copies ran while one was open for 1% -> 14% of each run, Pallas kernels for 0% -> 0%
where the time goes in v1:
time: 275 us; the launch traced here: 273 us
  waiting for transfers between devices  107 us (39%)
  other arithmetic  53.1 us (19%)
  blocking collectives  37.9 us (14%)
  matrix products  35.6 us (13%)
  starting transfers between devices  24.7 us (9%)
  local copies, waits for them, and re-layouts  12.8 us (5%)
    ppermute x17, waiting for transfers between devices, flip(): return lax.ppermute(value, axis, pairs)  46.4 us
    all_to_all x1, waiting for transfers between devices, per_device(): news = lax.all_to_all(news, 'worker', 0, 0, tiled=True)  41.3 us
    all_to_all x2, blocking collectives, per_device(): lax.all_to_all(current.reshape(workers, size // workers, width), 'worker'...  37.9 us
    dot_general x16, matrix products, partial_rows(): lax.dot_general(block, upstream, (((0,), (0,)), ((), ())), preferred_elem...  33.5 us
    reduce_sum x120, other arithmetic, per_device(): gap = jnp.sum((gap * gap).reshape(-1, 2, half), axis=(0, 2))  23.8 us
    all_to_all x2, waiting for transfers between devices, per_device(): lax.all_to_all(current.reshape(workers, size // workers, width), 'worker'...  19.5 us
    unnamed x28, other arithmetic  18.6 us
    ppermute x17, starting transfers between devices, flip(): return lax.ppermute(value, axis, pairs)  11.9 us
  transfers between devices with their start and end apart: 20, of which 12 were waited for; matrix products, arithmetic and copies ran while one was open for 14% of the time, Pallas kernels for 0%

profile of v1, /device:TPU:0, one launch (start us, length us, event | category | flops | bytes accessed | tf_op | source)
XLA Modules:
  0.0 272.7 jit_solution(10125063713962569551)
XLA Ops:
  2.5 2.4 fusion
  5.4 2.4 fusion.28
  7.8 2.4 fusion.24
  10.7 2.4 fusion.20
  13.2 2.4 fusion.16
  16.1 2.4 fusion.4
  25.9 2.6 collective-permute-start.2
  32.5 8.8 %collective-permute-done.2 = f32[128,1024]{1,0:T(8,128)S(1)} collective-permute-done((f32[128,1024]{1,0:T(8,128)S(1)}, f32[128,1024]{1,0:T(8,128)S(1)}, u32[]{:S(2)}, u32[]{:S(2)}) %collective-permute-start.2) | collective-permute-done | bytes 524320 | tf_op jit(solution)/shard_map/ppermute | solution.py:17
  45.3 7.3 %collective-permute-done.8 = f32[128,1024]{1,0:T(8,128)S(1)} collective-permute-done((f32[128,1024]{1,0:T(8,128)S(1)}, f32[128,1024]{1,0:T(8,128)S(1)}, u32[]{:S(2)}, u32[]{:S(2)}) %collective-permute-start.8) | collective-permute-done | bytes 524320 | tf_op jit(solution)/shard_map/ppermute | solution.py:17
  54.2 9.6 %collective-permute-done.11 = f32[128,1024]{1,0:T(8,128)S(1)} collective-permute-done((f32[128,1024]{1,0:T(8,128)S(1)}, f32[128,1024]{1,0:T(8,128)S(1)}, u32[]{:S(2)}, u32[]{:S(2)}) %collective-permute-start.11) | collective-permute-done | bytes 524320 | tf_op jit(solution)/shard_map/ppermute | solution.py:17
  65.4 9.4 %collective-permute-done.5 = f32[128,1024]{1,0:T(8,128)S(1)} collective-permute-done((f32[128,1024]{1,0:T(8,128)S(1)}, f32[128,1024]{1,0:T(8,128)S(1)}, u32[]{:S(2)}, u32[]{:S(2)}) %collective-permute-start.5) | collective-permute-done | bytes 524320 | tf_op jit(solution)/shard_map/ppermute | solution.py:17
  74.8 3.7 %bitcast_subtract_fusion.2 = (f32[128,1024]{1,0:T(8,128)S(1)}, f32[128,1024]{1,0:T(8,128)}, f32[128,1024]{1,0:T(8,128)S(1)}, f32[128,1024]{1,0:T(8,128)}, f32[128,1024]{1,0:T(8,128)}) fusion(f32[1,512,1024]{2,1,0:T(8,128)} %param.9, f32[128,1024]{1,0:T(8,128)S(1)} %fusion.68, f32[128,1024]{1,0:T(8,128)S(1)} %fusion.77, f32[128,1024]{1,0:T(8,128)S(1)} %fusion.74, ...), kind=kOutput, calls=%fused_computation.53 | convolution fusion | flops 404226048 | bytes 11403268 | tf_op jit(solution)/shard_map/dot_general | solution.py:69
  78.5 20.2 %all_to_all.25 = f32[8,16,1024]{2,1,0:T(8,128)} all-to-all(f32[8,16,1024]{2,1,0:T(8,128)S(1)} %bitcast.429), channel_id=1, replica_groups=mesh['worker'=8,'tok'=4] {'worker'}, dimensions={0} | all-to-all | bytes 1048576 | tf_op jit(solution)/shard_map/all_to_all | solution.py:87
  98.7 17.7 %all_to_all.26 = f32[8,16,1024]{2,1,0:T(8,128)} all-to-all(f32[8,16,1024]{2,1,0:T(8,128)S(1)} %bitcast.428), channel_id=1, replica_groups=mesh['worker'=8,'tok'=4] {'worker'}, dimensions={0} | all-to-all | bytes 1048576 | tf_op jit(solution)/shard_map/all_to_all | solution.py:87
  116.4 4.1 %all-to-all-start.2 = ((f32[8,16,1024]{2,1,0:T(8,128)}), f32[8,16,1024]{2,1,0:T(8,128)}, u32[]{:S(2)}, u32[]{:S(2)}) async-start(f32[8,16,1024]{2,1,0:T(8,128)} %bitcast.427), calls=%async_computation.2 | async-start | bytes 1048576 | tf_op jit(solution)/shard_map/all_to_all | solution.py:87
  120.5 13.7 %all-to-all-done.2 = f32[8,16,1024]{2,1,0:T(8,128)} async-done(((f32[8,16,1024]{2,1,0:T(8,128)}), f32[8,16,1024]{2,1,0:T(8,128)}, u32[]{:S(2)}, u32[]{:S(2)}) %all-to-all-start.2) | async-done | bytes 524320 | tf_op jit(solution)/shard_map/all_to_all | solution.py:87
  134.2 4.3 %all-to-all-start = ((f32[8,16,1024]{2,1,0:T(8,128)}), f32[8,16,1024]{2,1,0:T(8,128)}, u32[]{:S(2)}, u32[]{:S(2)}) async-start(f32[8,16,1024]{2,1,0:T(8,128)} %bitcast.426), calls=%async_computation | async-start | bytes 1048576 | tf_op jit(solution)/shard_map/all_to_all | solution.py:87
  145.9 5.9 %all-to-all-done = f32[8,16,1024]{2,1,0:T(8,128)} async-done(((f32[8,16,1024]{2,1,0:T(8,128)}), f32[8,16,1024]{2,1,0:T(8,128)}, u32[]{:S(2)}, u32[]{:S(2)}) %all-to-all-start) | async-done | bytes 524320 | tf_op jit(solution)/shard_map/all_to_all | solution.py:87
  179.9 2.1 collective-permute-done.14
  183.3 2.3 collective-permute-done.15
  186.4 3.7 %collective-permute-done.16 = f32[8,128]{1,0:T(8,128)S(1)} collective-permute-done((f32[8,128]{1,0:T(8,128)S(1)}, f32[8,128]{1,0:T(8,128)S(1)}, u32[]{:S(2)}, u32[]{:S(2)}) %collective-permute-start.16) | collective-permute-done | bytes 4128 | tf_op jit(solution)/shard_map/ppermute | solution.py:17
  220.6 4.3 %all-to-all-start.4 = ((f32[8,64,1024]{2,1,0:T(8,128)}), f32[8,64,1024]{2,1,0:T(8,128)}, u32[]{:S(2)}, u32[]{:S(2)}) async-start(f32[8,64,1024]{2,1,0:T(8,128)} %pad_maximum_fusion), calls=%async_computation.4 | async-start | bytes 4194304 | tf_op jit(solution)/shard_map/all_to_all | solution.py:127
  224.9 3.1 %maximum_bitcast_fusion.1 = f32[1,512,1024]{2,1,0:T(8,128)} fusion(f32[128,1024]{1,0:T(8,128)} %copy-done.5, f32[128,1024]{1,0:T(8,128)} %copy-done.4, f32[128,1024]{1,0:T(8,128)} %get-tuple-element.228, f32[128,1024]{1,0:T(8,128)} %copy-done.3), kind=kLoop, calls=%fused_computation.34 | loop fusion | flops 1572864 | bytes 4194304 | tf_op jit(solution)/shard_map/broadcast_in_dim | solution.py:133
  228.0 41.3 %all-to-all-done.4 = f32[8,64,1024]{2,1,0:T(8,128)} async-done(((f32[8,64,1024]{2,1,0:T(8,128)}), f32[8,64,1024]{2,1,0:T(8,128)}, u32[]{:S(2)}, u32[]{:S(2)}) %all-to-all-start.4) | async-done | bytes 2097184 | tf_op jit(solution)/shard_map/all_to_all | solution.py:127
  (536 shorter events, 92.9 us)
Async XLA Ops:
  4.9 16.8 %collective-permute-start.10 = (f32[128,1024]{1,0:T(8,128)}, f32[128,1024]{1,0:T(8,128)}, u32[]{:S(2)}, u32[]{:S(2)}) collective-permute-start(f32[128,1024]{1,0:T(8,128)} %fusion), channel_id=1, source_target_pairs={{0,1},{1,0},{2,3},{3,2},{4,5},{5,4},{6,7},{7,6},{8,9},{9,8},{10,11... | collective-permute-start | bytes 1572872 | tf_op jit(solution)/shard_map/ppermute | solution.py:17
  7.8 24.4 %collective-permute-start = (f32[128,1024]{1,0:T(8,128)}, f32[128,1024]{1,0:T(8,128)}, u32[]{:S(2)}, u32[]{:S(2)}) collective-permute-start(f32[128,1024]{1,0:T(8,128)} %fusion.28), channel_id=1, source_target_pairs={{0,1},{1,0},{2,3},{3,2},{4,5},{5,4},{6,7},{7,6},{8,9},{9,8},{10,11... | collective-permute-start | bytes 1572872 | tf_op jit(solution)/shard_map/ppermute | solution.py:17
  10.2 13.3 %collective-permute-start.1 = (f32[128,1024]{1,0:T(8,128)}, f32[128,1024]{1,0:T(8,128)}, u32[]{:S(2)}, u32[]{:S(2)}) collective-permute-start(f32[128,1024]{1,0:T(8,128)} %fusion.24), channel_id=1, source_target_pairs={{0,1},{1,0},{2,3},{3,2},{4,5},{5,4},{6,7},{7,6},{8,9},{9,8},{10,11... | collective-permute-start | bytes 1572872 | tf_op jit(solution)/shard_map/ppermute | solution.py:17
  13.2 52.3 %collective-permute-start.3 = (f32[128,1024]{1,0:T(8,128)}, f32[128,1024]{1,0:T(8,128)}, u32[]{:S(2)}, u32[]{:S(2)}) collective-permute-start(f32[128,1024]{1,0:T(8,128)} %fusion.20), channel_id=1, source_target_pairs={{0,1},{1,0},{2,3},{3,2},{4,5},{5,4},{6,7},{7,6},{8,9},{9,8},{10,11... | collective-permute-start | bytes 1572872 | tf_op jit(solution)/shard_map/ppermute | solution.py:17
  15.6 14.6 %collective-permute-start.4 = (f32[128,1024]{1,0:T(8,128)}, f32[128,1024]{1,0:T(8,128)}, u32[]{:S(2)}, u32[]{:S(2)}) collective-permute-start(f32[128,1024]{1,0:T(8,128)} %fusion.16), channel_id=1, source_target_pairs={{0,1},{1,0},{2,3},{3,2},{4,5},{5,4},{6,7},{7,6},{8,9},{9,8},{10,11... | collective-permute-start | bytes 1572872 | tf_op jit(solution)/shard_map/ppermute | solution.py:17
  21.7 4.2 %collective-permute-start.7 = (f32[128,1024]{1,0:T(8,128)S(1)}, f32[128,1024]{1,0:T(8,128)S(1)}, u32[]{:S(2)}, u32[]{:S(2)}) collective-permute-start(f32[128,1024]{1,0:T(8,128)S(1)} %fusion.8), channel_id=1, source_target_pairs={{0,1},{1,0},{2,3},{3,2},{4,5},{5,4},{6,7},{7,6},{8,9},{9,8},{10,11... | collective-permute-start | bytes 1572872 | tf_op jit(solution)/shard_map/ppermute | solution.py:17
  23.6 21.6 %collective-permute-start.6 = (f32[128,1024]{1,0:T(8,128)S(1)}, f32[128,1024]{1,0:T(8,128)S(1)}, u32[]{:S(2)}, u32[]{:S(2)}) collective-permute-start(f32[128,1024]{1,0:T(8,128)S(1)} %fusion.12), channel_id=1, source_target_pairs={{0,1},{1,0},{2,3},{3,2},{4,5},{5,4},{6,7},{7,6},{8,9},{9,8},{10,11... | collective-permute-start | bytes 1572872 | tf_op jit(solution)/shard_map/ppermute | solution.py:17
  25.9 15.4 %collective-permute-start.2 = (f32[128,1024]{1,0:T(8,128)S(1)}, f32[128,1024]{1,0:T(8,128)S(1)}, u32[]{:S(2)}, u32[]{:S(2)}) collective-permute-start(f32[128,1024]{1,0:T(8,128)S(1)} %fusion.35), channel_id=1, source_target_pairs={{0,2},{1,3},{2,0},{3,1},{4,6},{5,7},{6,4},{7,5},{8,10},{9,11},{10,... | collective-permute-start | bytes 1572872 | tf_op jit(solution)/shard_map/ppermute | solution.py:17
  30.2 22.4 %collective-permute-start.8 = (f32[128,1024]{1,0:T(8,128)S(1)}, f32[128,1024]{1,0:T(8,128)S(1)}, u32[]{:S(2)}, u32[]{:S(2)}) collective-permute-start(f32[128,1024]{1,0:T(8,128)S(1)} %fusion.47), channel_id=1, source_target_pairs={{0,2},{1,3},{2,0},{3,1},{4,6},{5,7},{6,4},{7,5},{8,10},{9,11},{10,... | collective-permute-start | bytes 1572872 | tf_op jit(solution)/shard_map/ppermute | solution.py:17
  32.2 22.0 %collective-permute-start.9 = (f32[128,1024]{1,0:T(8,128)S(1)}, f32[128,1024]{1,0:T(8,128)S(1)}, u32[]{:S(2)}, u32[]{:S(2)}) collective-permute-start(f32[128,1024]{1,0:T(8,128)S(1)} %copy-done.7), channel_id=1, source_target_pairs={{0,1},{1,0},{2,3},{3,2},{4,5},{5,4},{6,7},{7,6},{8,9},{9,8},{10,11... | collective-permute-start | bytes 1572872 | tf_op jit(solution)/shard_map/ppermute | solution.py:17
  41.3 22.5 %collective-permute-start.11 = (f32[128,1024]{1,0:T(8,128)S(1)}, f32[128,1024]{1,0:T(8,128)S(1)}, u32[]{:S(2)}, u32[]{:S(2)}) collective-permute-start(f32[128,1024]{1,0:T(8,128)S(1)} %fusion.53), channel_id=1, source_target_pairs={{0,2},{1,3},{2,0},{3,1},{4,6},{5,7},{6,4},{7,5},{8,10},{9,11},{10,... | collective-permute-start | bytes 1572872 | tf_op jit(solution)/shard_map/ppermute | solution.py:17
  45.2 29.6 %collective-permute-start.5 = (f32[128,1024]{1,0:T(8,128)S(1)}, f32[128,1024]{1,0:T(8,128)S(1)}, u32[]{:S(2)}, u32[]{:S(2)}) collective-permute-start(f32[128,1024]{1,0:T(8,128)S(1)} %fusion.41), channel_id=1, source_target_pairs={{0,2},{1,3},{2,0},{3,1},{4,6},{5,7},{6,4},{7,5},{8,10},{9,11},{10,... | collective-permute-start | bytes 1572872 | tf_op jit(solution)/shard_map/ppermute | solution.py:17
  78.5 60.1 %copy-start.11 = (s32[1,5]{1,0:T(1,128)S(1)}, s32[1,5]{1,0:T(1,128)}, u32[]{:S(2)}) copy-start(s32[1,5]{1,0:T(1,128)} %param.11) | copy-start | bytes 64
  116.4 17.9 %all-to-all-start.2 = ((f32[8,16,1024]{2,1,0:T(8,128)}), f32[8,16,1024]{2,1,0:T(8,128)}, u32[]{:S(2)}, u32[]{:S(2)}) async-start(f32[8,16,1024]{2,1,0:T(8,128)} %bitcast.427), calls=%async_computation.2 | async-start | bytes 1048576 | tf_op jit(solution)/shard_map/all_to_all | solution.py:87
  134.2 17.5 %all-to-all-start = ((f32[8,16,1024]{2,1,0:T(8,128)}), f32[8,16,1024]{2,1,0:T(8,128)}, u32[]{:S(2)}, u32[]{:S(2)}) async-start(f32[8,16,1024]{2,1,0:T(8,128)} %bitcast.426), calls=%async_computation | async-start | bytes 1048576 | tf_op jit(solution)/shard_map/all_to_all | solution.py:87
  138.7 52.1 %copy-start.8 = (s32[8]{0:T(128)S(1)}, s32[8]{0:T(128)}, u32[]{:S(2)}) copy-start(s32[8]{0:T(128)} %constant.92) | copy-start | bytes 100
  138.7 52.1 %copy-start.9 = (s32[8]{0:T(128)S(1)}, s32[8]{0:T(128)}, u32[]{:S(2)}) copy-start(s32[8]{0:T(128)} %constant.90) | copy-start | bytes 100
  138.8 52.1 %copy-start.10 = (s32[8]{0:T(128)S(1)}, s32[8]{0:T(128)}, u32[]{:S(2)}) copy-start(s32[8]{0:T(128)} %constant.88) | copy-start | bytes 100
  173.4 1.2 collective-permute-start.12
  174.6 3.7 %collective-permute-start.13 = (f32[8,128]{1,0:T(8,128)S(1)}, f32[8,128]{1,0:T(8,128)S(1)}, u32[]{:S(2)}, u32[]{:S(2)}) collective-permute-start(f32[8,128]{1,0:T(8,128)S(1)} %fusion.140), channel_id=1, source_target_pairs={{0,2},{1,3},{2,0},{3,1},{4,6},{5,7},{6,4},{7,5},{8,10},{9,11},{10,... | collective-permute-start | bytes 12296 | tf_op jit(solution)/shard_map/ppermute | solution.py:17
  178.3 3.7 %collective-permute-start.14 = (f32[8,128]{1,0:T(8,128)S(1)}, f32[8,128]{1,0:T(8,128)S(1)}, u32[]{:S(2)}, u32[]{:S(2)}) collective-permute-start(f32[8,128]{1,0:T(8,128)S(1)} %fusion.151), channel_id=1, source_target_pairs={{0,4},{4,0},{8,12},{12,8},{16,20},{20,16},{24,28},{28,24},{1,5},{5... | collective-permute-start | bytes 12296 | tf_op jit(solution)/shard_map/ppermute | solution.py:17
  182.0 3.6 %collective-permute-start.15 = (f32[8,128]{1,0:T(8,128)S(1)}, f32[8,128]{1,0:T(8,128)S(1)}, u32[]{:S(2)}, u32[]{:S(2)}) collective-permute-start(f32[8,128]{1,0:T(8,128)S(1)} %add.2247), channel_id=1, source_target_pairs={{0,8},{4,12},{8,0},{12,4},{16,24},{20,28},{24,16},{28,20},{1,9},{5... | collective-permute-start | bytes 12296 | tf_op jit(solution)/shard_map/ppermute | solution.py:17
  185.6 4.5 %collective-permute-start.16 = (f32[8,128]{1,0:T(8,128)S(1)}, f32[8,128]{1,0:T(8,128)S(1)}, u32[]{:S(2)}, u32[]{:S(2)}) collective-permute-start(f32[8,128]{1,0:T(8,128)S(1)} %add.2248), channel_id=1, source_target_pairs={{0,16},{4,20},{8,24},{12,28},{16,0},{20,4},{24,8},{28,12},{1,17},{... | collective-permute-start | bytes 12296 | tf_op jit(solution)/shard_map/ppermute | solution.py:17
  220.6 48.7 %all-to-all-start.4 = ((f32[8,64,1024]{2,1,0:T(8,128)}), f32[8,64,1024]{2,1,0:T(8,128)}, u32[]{:S(2)}, u32[]{:S(2)}) async-start(f32[8,64,1024]{2,1,0:T(8,128)} %pad_maximum_fusion), calls=%async_computation.4 | async-start | bytes 4194304 | tf_op jit(solution)/shard_map/all_to_all | solution.py:127
  (9 other events, 142.9 us)

commit v2 on v0

v2 whole, which is shorter than its diff:
```python
import functools
import math

import jax
import jax.numpy as jnp
import numpy as np
from jax import lax
from jax.experimental import pallas as pl
from jax.experimental.pallas import tpu as pltpu
from jax.sharding import PartitionSpec as P


D = 2048
KV_WIDTH = 512
ROUNDS = 2
LEARNING_RATE = 0.25
HIGH = lax.Precision.HIGHEST
LANES = 128
CHUNKS = (256, 256, 256, 256)


def flip(value, axis, mask):
    pairs = [(source, source ^ mask) for source in range(lax.axis_size(axis))]
    return lax.ppermute(value, axis, pairs)


def after(value, *others):
    return lax.optimization_barrier((value, *others))[0]


def neighbours(w, workers):
    return (w ^ 1, w ^ 2, (w - 4) % workers, (w + 4) % workers)


def pair_list(workers):
    return [(a, b) for a in range(workers) for b in range(a + 1, workers)]


def update(mine, other, momentum, weights, start):
    cut = slice(start, start + mine.shape[1])
    velocity = 0.5 * momentum[:, cut] + (mine + other)
    return velocity, weights[:, cut] - LEARNING_RATE * velocity


def squares_kernel(workers, block_ref, sums_ref):
    sums_ref[...] = jnp.zeros_like(sums_ref)
    lanes = block_ref.shape[2] // LANES
    for index, (a, b) in enumerate(pair_list(workers)):
        total = None
        for lane in range(lanes):
            cut = slice(lane * LANES, (lane + 1) * LANES)
            gap = block_ref[a, :, cut] - block_ref[b, :, cut]
            part = jnp.sum(gap * gap, axis=0, keepdims=True)
            total = part if total is None else total + part
        sums_ref[index : index + 1, :] = total


def squares(block):
    workers = block.shape[0]
    rows = -(-len(pair_list(workers)) // 8) * 8
    return pl.pallas_call(
        functools.partial(squares_kernel, workers),
        out_shape=jax.ShapeDtypeStruct((rows, LANES), jnp.float32),
        name="squares",
    )(block)


def lane_sums(sums):
    ones = jnp.ones((8, LANES), jnp.float32)
    return lax.dot_general(ones, sums, (((1,), (1,)), ((), ())), precision=HIGH, preferred_element_type=jnp.float32)


def pack_kernel(tokens, owners, me_ref, mix_ref, *rest):
    parts, packed_ref = rest[:-1], rest[-1]
    packed_ref[...] = jnp.zeros_like(packed_ref)
    count = parts[0].shape[0]
    for h in range(2):
        total = None
        for part, owner in zip(parts, owners):
            if owner == h:
                total = part[...] if total is None else total + part[...]
        packed_ref[h : h + 1, 0:count] = lane_sums(total)[0:1]
    lane = lax.broadcasted_iota(jnp.int32, (1, LANES), 1)
    row = jnp.zeros((1, LANES), jnp.float32)
    for k in range(5):
        weight = mix_ref[0, k].astype(jnp.float32) * (1.0 / tokens)
        row = row + jnp.where(lane == me_ref[0] * 5 + k, weight, 0.0)
    packed_ref[2:3, :] = row


def pack(parts, owners, mix_weights, me, tokens):
    smem = pl.BlockSpec(memory_space=pltpu.SMEM)
    vmem = pl.BlockSpec(memory_space=pltpu.VMEM)
    return pl.pallas_call(
        functools.partial(pack_kernel, tokens, owners),
        in_specs=[smem, smem] + [vmem] * len(parts),
        out_specs=vmem,
        out_shape=jax.ShapeDtypeStruct((8, LANES), jnp.float32),
        name="pack",
    )(me.reshape(1), mix_weights, *parts)


def selectors(workers):
    table = np.zeros((5, workers, workers, LANES), np.float32)
    for place, (a, b) in enumerate(pair_list(workers)):
        table[0, a, b, place] = table[0, b, a, place] = 1.0
    for w in range(workers):
        for k, j in enumerate(neighbours(w, workers)):
            table[1, w, j, w * 5 + k + 1] += 1.0
            table[3, j, w, w * 5 + k + 1] += 1.0
        table[2, w, :, w * 5 : w * 5 + 5] = 1.0
        table[4, :, w, w * 5 : w * 5 + 5] = 1.0
    return table.reshape(-1, LANES)


def spread(select, row):
    wide = jnp.broadcast_to(row, (LANES, LANES))
    return lax.dot_general(select, wide, (((1,), (1,)), ((), ())), precision=HIGH, preferred_element_type=jnp.float32)


def mix_kernel(workers, h, starts, clip_ref, packed_ref, select_ref, *rest):
    blocks, out_ref = rest[:-1], rest[-1]
    size = workers * workers
    table = lambda k: select_ref[k * size : (k + 1) * size, :]
    rows_of = lambda flat: [flat[w * workers : (w + 1) * workers] for w in range(workers)]
    mixing = packed_ref[2:3, :]
    share = rows_of(spread(table(1), mixing) / spread(table(2), mixing))
    share_t = rows_of(spread(table(3), mixing) / spread(table(4), mixing))
    place = lax.broadcasted_iota(jnp.int32, (workers, LANES), 0)
    eye = [jnp.where(place == w, 1.0, 0.0) for w in range(workers)]
    radius = [clip_ref[r].astype(jnp.float32) * (math.sqrt(D * KV_WIDTH) / 1000.0) for r in range(ROUNDS)]

    def times(left, right):
        out = []
        for w in range(workers):
            total = None
            for j in range(workers):
                term = left[w][j : j + 1, :] * right[j]
                total = term if total is None else total + term
            out.append(total)
        return out

    first = rows_of(spread(table(0), packed_ref[h : h + 1, :]))
    now, total, total_t = first, None, None
    for r in range(ROUNDS):
        factor = [radius[r] / jnp.maximum(jnp.sqrt(d), radius[r]) for d in now]
        step = [s * f for s, f in zip(share, factor)]
        step = [a + e * (1.0 - jnp.sum(a, axis=0, keepdims=True)) for a, e in zip(step, eye)]
        total = step if total is None else times(step, total)
        if r + 1 < ROUNDS:
            step_t = [s * f for s, f in zip(share_t, factor)]
            keep = 1.0 - functools.reduce(lambda a, b: a + b, step_t)
            step_t = [a + e * keep for a, e in zip(step_t, eye)]
            total_t = step_t if total_t is None else times(total_t, step_t)
            inner = times(times(total, first), total_t)
            diag = functools.reduce(lambda a, b: a + b, [i * e for i, e in zip(inner, eye)])
            now = [
                jnp.maximum(i - 0.5 * (diag + diag[w : w + 1, :]), 0.0) for w, i in enumerate(inner)
            ]
    for block, start in zip(blocks, starts):
        for lane in range(block.shape[2] // LANES):
            cut = slice(lane * LANES, (lane + 1) * LANES)
            into = slice(start + lane * LANES, start + (lane + 1) * LANES)
            old = [block[j, :, cut] for j in range(workers)]
            for w in range(workers):
                value = None
                for j in range(workers):
                    term = total[w][j : j + 1, :] * old[j]
                    value = term if value is None else value + term
                out_ref[w, :, into] = value


def mix(packed, clip_radius, blocks, h, starts, width):
    workers, rows = blocks[0].shape[:2]
    vmem = pl.BlockSpec(memory_space=pltpu.VMEM)
    return pl.pallas_call(
        functools.partial(mix_kernel, workers, h, starts),
        in_specs=[pl.BlockSpec(memory_space=pltpu.SMEM)] + [vmem] * (2 + len(blocks)),
        out_specs=vmem,
        out_shape=jax.ShapeDtypeStruct((workers, rows, width), jnp.float32),
        name="mix",
    )(clip_radius, packed, selectors(workers), *blocks)


def per_device(inputs, cotangent, weights, momentum, mix_weights, clip_radius):
    features, upstream = inputs[0], cotangent[0]
    tokens = lax.axis_size("tok")
    workers = lax.axis_size("worker")
    tok, me = lax.axis_index("tok"), lax.axis_index("worker")
    rows, width = weights.shape[1:]
    half = width // 2
    starts = [sum(CHUNKS[:k]) for k in range(len(CHUNKS))]
    owners = tuple(start // half for start in starts)
    levels = tokens.bit_length() - 1
    count = len(CHUNKS)
    order = [None]

    def partial_rows(offset, k):
        left, right = features, upstream
        if order[0] is not None:
            left, right = lax.optimization_barrier((features, upstream, order[0]))[:2]
        left = lax.dynamic_slice_in_dim(left, (tok ^ offset) * rows, rows, axis=1)
        right = right[:, starts[k] : starts[k] + CHUNKS[k]]
        out = lax.dot_general(left, right, (((0,), (0,)), ((), ())), preferred_element_type=jnp.float32)
        order[0] = out
        return out

    leaves = {}
    last = 1 << (levels - 1)
    for lead in (last, 0):
        for k in range(count + 1):
            for near in (1, 0):
                chunk = k - 1 + near
                if 0 <= chunk < count:
                    for offset in range(lead, lead + last):
                        if offset & 1 == near:
                            leaves[offset, chunk] = partial_rows(offset, chunk)

    def reduced(offset, level, k):
        if level == 0:
            return leaves[offset, k]
        mask = 1 << (level - 1)
        away = reduced(offset ^ mask, level - 1, k)
        away = flip(away, "tok", mask)
        return reduced(offset, level - 1, k) + away

    aways = []
    for k in range(count):
        away = reduced(last, levels - 1, k)
        aways.append(flip(away, "tok", last))
    mines = [reduced(0, levels - 1, k) for k in range(count)]
    mines = [lax.optimization_barrier(mine) for mine in mines]
    velocities, gathered = [], []
    for k in range(count):
        away = after(aways[k], current) if k else after(aways[k], *mines)
        velocity, current = update(mines[k], away, momentum[0], weights[0], starts[k])
        velocities.append(velocity)
        block = current.reshape(workers, rows // workers, CHUNKS[k])
        gathered.append(lax.all_to_all(block, "worker", 0, 0, tiled=True))
    parts = []
    for k in range(count):
        parts.append(squares(gathered[k]))
    packed = pack(parts, owners, mix_weights, me, tokens)
    for axis, size in (("tok", tokens), ("worker", workers)):
        mask = 1
        while mask < size:
            packed = packed + flip(packed, axis, mask)
            mask *= 2
    news = []
    for h in range(2):
        mine = [k for k in range(count) if owners[k] == h]
        blocks, places = [gathered[k] for k in mine], [starts[k] - h * half for k in mine]
        mixed = mix(packed, clip_radius, blocks, h, places, half)
        mixed = lax.all_to_all(mixed, "worker", 0, 0, tiled=True)
        news.append(mixed.reshape(rows, half))
    new, velocity = jnp.concatenate(news, axis=1), jnp.concatenate(velocities, axis=1)
    return new[None], velocity[None]


def solution(mesh):
    placed = (
        P("worker", "tok", None),
        P("worker", "tok", None),
        P("worker", "tok", None),
        P("worker", "tok", None),
        P("worker", None),
        P(),
    )

    return jax.shard_map(
        per_device,
        mesh=mesh,
        in_specs=placed,
        out_specs=(P("worker", "tok", None), P("worker", "tok", None)),
        check_vma=False,
    )
```

time: 334 us -> 230 us (0.69)
  waiting for transfers between devices: 252 us -> 98.2 us
  blocking collectives: 11.9 us -> 37.5 us
  matrix products: 10.8 us -> 34.5 us
  other arithmetic: 32.3 us -> 10.9 us
  starting transfers between devices: 9.01 us -> 29.7 us
  Pallas kernels: 0 us -> 16.4 us
  between operations: 14.1 us -> 0.85 us
    ppermute x6 -> x17, waiting for transfers between devices: 178 us -> 51.2 us  [flip(): return lax.ppermute(value, axis, pairs)]
    reduce_scatter x1 -> x0, waiting for transfers between devices: 74.2 us -> none  [per_device(): lax.psum_scatter(gradient_rows(features, upstream), 'tok', scatter_dimens...]
    all_to_all x0 -> x4, waiting for transfers between devices: none -> 47 us  [the longest x2 39.9 us: per_device(): mixed = lax.all_to_all(mixed, 'worker', 0, 0, tiled=True)]
    all_to_all x0 -> x2, blocking collectives: none -> 37.5 us  [per_device(): gathered.append(lax.all_to_all(block, 'worker', 0, 0, tiled=True))]
    dot_general x1 -> x16, matrix products: 10.8 us -> 34.5 us  [partial_rows(): lax.dot_general(left, right, (((0,), (0,)), ((), ())), preferred_element_...]
    all_to_all x0 -> x4, starting transfers between devices: none -> 16.7 us  [the longest x2 9.36 us: per_device(): gathered.append(lax.all_to_all(block, 'worker', 0, 0, tiled=True))]
    pallas_call x0 -> x7, Pallas kernels: none -> 16.4 us  [the longest x4 7.48 us: squares(): pl.pallas_call(functools.partial(squares_kernel, workers), out_shape=jax....]
    psum x2 -> x0, blocking collectives: 11.9 us -> none  [per_device(): totals = lax.psum(squares, 'tok')]
  transfers between devices with their start and end apart: 7 -> 21, of which waited for: 7 -> 11; matrix products, arithmetic and copies ran while one was open for 1% -> 14% of each run, Pallas kernels for 0% -> 4%
where the time goes in v2:
time: 230 us; the launch traced here: 229 us
  waiting for transfers between devices  98.2 us (43%)
  blocking collectives  37.5 us (16%)
  matrix products  34.5 us (15%)
  starting transfers between devices  29.7 us (13%)
  Pallas kernels  16.4 us (7%)
  other arithmetic  10.9 us (5%)
    ppermute x17, waiting for transfers between devices, flip(): return lax.ppermute(value, axis, pairs)  51.2 us
    all_to_all x2, waiting for transfers between devices, per_device(): mixed = lax.all_to_all(mixed, 'worker', 0, 0, tiled=True)  39.9 us
    all_to_all x2, blocking collectives, per_device(): gathered.append(lax.all_to_all(block, 'worker', 0, 0, tiled=True))  37.5 us
    dot_general x16, matrix products, partial_rows(): lax.dot_general(left, right, (((0,), (0,)), ((), ())), preferred_element_...  34.5 us
    ppermute x17, starting transfers between devices, flip(): return lax.ppermute(value, axis, pairs)  13 us
    all_to_all x2, starting transfers between devices, per_device(): gathered.append(lax.all_to_all(block, 'worker', 0, 0, tiled=True))  9.36 us
    pallas_call x4, Pallas kernels, squares(): pl.pallas_call(functools.partial(squares_kernel, workers), out_shape=jax....  7.48 us
    pallas_call x2, Pallas kernels, mix(): pl.pallas_call(functools.partial(mix_kernel, workers, h, starts), in_spec...  7.4 us
  transfers between devices with their start and end apart: 21, of which 11 were waited for; matrix products, arithmetic and copies ran while one was open for 14% of the time, Pallas kernels for 4%

profile of v2, /device:TPU:0, one launch (start us, length us, event | category | flops | bytes accessed | tf_op | source)
XLA Modules:
  0.0 229.2 jit_solution(9036526335912589623)
XLA Ops:
  3.4 3.2 %fusion.30 = f32[512,256]{1,0:T(8,128)} fusion(bf16[1536,2048]{1,0:T(8,128)(2,1)} %bitcast.30, s32[]{:T(128)S(6)} %select_n.8, bf16[1536,1024]{1,0:T(8,128)(2,1)} %bitcast.50), kind=kOutput, calls=%fused_computation.32 | convolution fusion | flops 402653184 | bytes 2883588 | tf_op jit(solution)/shard_map/dot_general | solution.py:204
  9.0 3.2 %fusion.26 = f32[512,256]{1,0:T(8,128)} fusion(bf16[1536,2048]{1,0:T(8,128)(2,1)} %bitcast.32, s32[]{:T(128)S(6)} %select_n.8, bf16[1536,1024]{1,0:T(8,128)(2,1)} %bitcast.52), kind=kOutput, calls=%fused_computation.28 | convolution fusion | flops 402653184 | bytes 2883588 | tf_op jit(solution)/shard_map/dot_general | solution.py:204
  16.7 3.0 %fusion.81 = f32[512,256]{1,0:T(8,128)} fusion(f32[512,256]{1,0:T(8,128)S(1)} %collective-permute-done.8, bf16[1536,1024]{1,0:T(8,128)(2,1)} %bitcast.53, bf16[1536,2048]{1,0:T(8,128)(2,1)} %bitcast.33, s32[]{:T(128)S(6)} %select_n.9), kind=kOutput, calls=%fused_computation.85 | convolution fusion | flops 402784256 | bytes 3407876 | tf_op jit(solution)/shard_map/dot_general | solution.py:204
  19.7 3.0 %fusion.82 = f32[512,256]{1,0:T(8,128)} fusion(f32[512,256]{1,0:T(8,128)S(1)} %collective-permute-done.10, bf16[1536,1024]{1,0:T(8,128)(2,1)} %bitcast.54, bf16[1536,2048]{1,0:T(8,128)(2,1)} %bitcast.34, s32[]{:T(128)S(6)} %select_n.9), kind=kOutput, calls=%fused_computation.86 | convolution fusion | flops 402784256 | bytes 3407876 | tf_op jit(solution)/shard_map/dot_general | solution.py:204
  22.8 3.2 %fusion.16 = f32[512,256]{1,0:T(8,128)} fusion(bf16[1536,2048]{1,0:T(8,128)(2,1)} %bitcast.35, s32[]{:T(128)S(6)} %select_n.10, bf16[1536,1024]{1,0:T(8,128)(2,1)} %bitcast.55), kind=kOutput, calls=%fused_computation.18 | convolution fusion | flops 402653184 | bytes 2883588 | tf_op jit(solution)/shard_map/dot_general | solution.py:204
  34.2 2.8 %collective-permute-start.7 = (f32[512,256]{1,0:T(8,128)}, f32[512,256]{1,0:T(8,128)S(1)}, u32[]{:S(2)}, u32[]{:S(2)}) collective-permute-start(f32[512,256]{1,0:T(8,128)} %fusion.80), channel_id=1, source_target_pairs={{0,2},{1,3},{2,0},{3,1},{4,6},{5,7},{6,4},{7,5},{8,10},{9,11},{10,... | collective-permute-start | bytes 1572872 | tf_op jit(solution)/shard_map/ppermute | solution.py:24
  39.7 3.0 %fusion.33 = f32[512,256]{1,0:T(8,128)} fusion(f32[512,256]{1,0:T(8,128)S(1)} %collective-permute-done.5, bf16[1536,2048]{1,0:T(8,128)(2,1)} %bitcast.38, s32[]{:T(128)S(6)} %select_n.11, bf16[1536,1024]{1,0:T(8,128)(2,1)S(1)} %bitcast.64), kind=kOutput, calls=%fused_computation.35 | convolution fusion | flops 402784256 | bytes 3407876 | tf_op jit(solution)/shard_map/dot_general | solution.py:204
  42.7 18.5 %collective-permute-done.2 = f32[512,256]{1,0:T(8,128)S(1)} collective-permute-done((f32[512,256]{1,0:T(8,128)S(1)}, f32[512,256]{1,0:T(8,128)S(1)}, u32[]{:S(2)}, u32[]{:S(2)}) %collective-permute-start.2) | collective-permute-done | bytes 524320 | tf_op jit(solution)/shard_map/ppermute | solution.py:24
  63.2 8.8 %collective-permute-done.9 = f32[512,256]{1,0:T(8,128)S(1)} collective-permute-done((f32[512,256]{1,0:T(8,128)}, f32[512,256]{1,0:T(8,128)S(1)}, u32[]{:S(2)}, u32[]{:S(2)}) %collective-permute-start.9) | collective-permute-done | bytes 524320 | tf_op jit(solution)/shard_map/ppermute | solution.py:24
  72.9 19.9 %all_to_all.30.block_ref.rest_0_ = f32[8,64,256]{2,1,0:T(8,128)} all-to-all(f32[8,64,256]{2,1,0:T(8,128)S(1)} %bitcast.21), channel_id=1, replica_groups=mesh['worker'=8,'tok'=4] {'worker'}, dimensions={0} | all-to-all | bytes 1048576 | tf_op jit(solution)/shard_map/all_to_all | solution.py:239
  92.8 17.6 %all_to_all.31.block_ref.rest_1_ = f32[8,64,256]{2,1,0:T(8,128)} all-to-all(f32[8,64,256]{2,1,0:T(8,128)S(1)} %bitcast.20), channel_id=1, replica_groups=mesh['worker'=8,'tok'=4] {'worker'}, dimensions={0} | all-to-all | bytes 1048576 | tf_op jit(solution)/shard_map/all_to_all | solution.py:239
  110.4 3.6 %all-to-all-start = ((f32[8,64,256]{2,1,0:T(8,128)}), f32[8,64,256]{2,1,0:T(8,128)S(1)}, u32[]{:S(2)}, u32[]{:S(2)}) async-start(f32[8,64,256]{2,1,0:T(8,128)} %bitcast.6), calls=%async_computation | async-start | bytes 1048576 | tf_op jit(solution)/shard_map/all_to_all | solution.py:239
  115.6 11.7 %collective-permute-done.11 = f32[512,256]{1,0:T(8,128)S(1)} collective-permute-done((f32[512,256]{1,0:T(8,128)}, f32[512,256]{1,0:T(8,128)S(1)}, u32[]{:S(2)}, u32[]{:S(2)}) %collective-permute-start.11) | collective-permute-done | bytes 524320 | tf_op jit(solution)/shard_map/ppermute | solution.py:24
  129.6 5.7 %all-to-all-start.3 = ((f32[8,64,256]{2,1,0:T(8,128)}), f32[8,64,256]{2,1,0:T(8,128)S(1)}, u32[]{:S(2)}, u32[]{:S(2)}) async-start(f32[8,64,256]{2,1,0:T(8,128)} %bitcast.9), calls=%async_computation.3 | async-start | bytes 1048576 | tf_op jit(solution)/shard_map/all_to_all | solution.py:239
  140.9 7.1 %all-to-all-done.3.block_ref.rest_1_ = f32[8,64,256]{2,1,0:T(8,128)S(1)} async-done(((f32[8,64,256]{2,1,0:T(8,128)}), f32[8,64,256]{2,1,0:T(8,128)S(1)}, u32[]{:S(2)}, u32[]{:S(2)}) %all-to-all-start.3) | async-done | bytes 524320 | tf_op jit(solution)/shard_map/all_to_all | solution.py:239
  162.2 2.9 %collective-permute-done.15 = f32[8,128]{1,0:T(8,128)S(1)} collective-permute-done((f32[8,128]{1,0:T(8,128)S(1)}, f32[8,128]{1,0:T(8,128)S(1)}, u32[]{:S(2)}, u32[]{:S(2)}) %collective-permute-start.15) | collective-permute-done | bytes 4128 | tf_op jit(solution)/shard_map/ppermute | solution.py:24
  165.9 3.7 %collective-permute-done.16 = f32[8,128]{1,0:T(8,128)S(1)} collective-permute-done((f32[8,128]{1,0:T(8,128)S(1)}, f32[8,128]{1,0:T(8,128)S(1)}, u32[]{:S(2)}, u32[]{:S(2)}) %collective-permute-start.16) | collective-permute-done | bytes 4128 | tf_op jit(solution)/shard_map/ppermute | solution.py:24
  170.2 3.7 %mix.2 = f32[8,64,512]{2,1,0:T(8,128)} custom-call(s32[2]{0:T(128)} %clip_ref.3, f32[8,128]{1,0:T(8,128)} %add.111.packed_ref, f32[320,128]{1,0:T(8,128)} %constant.28.clone.select_ref, f32[8,64,256]{2,1,0:T(8,128)} %copy-done, f32[8,64,256]{2,1,0:T(8,128)} %all_to_all.31.block_ref.rest_1_), custom_call_target="tpu_custom_call" | custom-call | tf_op jit(solution)/shard_map/mix/pallas_call | solution.py:176
  173.9 3.8 %all-to-all-start.4 = ((f32[8,64,512]{2,1,0:T(8,128)}), f32[8,64,512]{2,1,0:T(8,128)S(1)}, u32[]{:S(2)}, u32[]{:S(2)}) async-start(f32[8,64,512]{2,1,0:T(8,128)} %mix.2), calls=%async_computation.4 | async-start | bytes 2097152 | tf_op jit(solution)/shard_map/all_to_all | solution.py:254
  177.7 3.7 %mix.3 = f32[8,64,512]{2,1,0:T(8,128)} custom-call(s32[2]{0:T(128)} %clip_ref.3, f32[8,128]{1,0:T(8,128)} %add.111.packed_ref, f32[320,128]{1,0:T(8,128)} %constant.28.clone.select_ref, f32[8,64,256]{2,1,0:T(8,128)} %all_to_all.30.block_ref.rest_0_, f32[8,64,256]{2,1,0:T(8,128)} %copy-done.1), custom_call_target="tpu_custom_call" | custom-call | tf_op jit(solution)/shard_map/mix/pallas_call | solution.py:176
  181.4 18.1 %all-to-all-done.4 = f32[8,64,512]{2,1,0:T(8,128)S(1)} async-done(((f32[8,64,512]{2,1,0:T(8,128)}), f32[8,64,512]{2,1,0:T(8,128)S(1)}, u32[]{:S(2)}, u32[]{:S(2)}) %all-to-all-start.4) | async-done | bytes 1048608 | tf_op jit(solution)/shard_map/all_to_all | solution.py:254
  199.5 3.6 %all-to-all-start.5 = ((f32[8,64,512]{2,1,0:T(8,128)}), f32[8,64,512]{2,1,0:T(8,128)S(1)}, u32[]{:S(2)}, u32[]{:S(2)}) async-start(f32[8,64,512]{2,1,0:T(8,128)} %mix.3), calls=%async_computation.5 | async-start | bytes 2097152 | tf_op jit(solution)/shard_map/all_to_all | solution.py:254
  203.1 2.8 %maximum_bitcast_fusion.1 = f32[1,512,1024]{2,1,0:T(8,128)} fusion(f32[512,256]{1,0:T(8,128)} %get-tuple-element.71, f32[512,256]{1,0:T(8,128)} %get-tuple-element.73, f32[512,256]{1,0:T(8,128)S(1)} %copy-done.4, f32[512,256]{1,0:T(8,128)S(1)} %get-tuple-element.77), kind=kLoop, calls=%fused_computation.1 | loop fusion | flops 1572864 | bytes 4194304 | tf_op jit(solution)/shard_map/broadcast_in_dim | solution.py:257
  205.9 21.8 %all-to-all-done.5 = f32[8,64,512]{2,1,0:T(8,128)S(1)} async-done(((f32[8,64,512]{2,1,0:T(8,128)}), f32[8,64,512]{2,1,0:T(8,128)S(1)}, u32[]{:S(2)}, u32[]{:S(2)}) %all-to-all-start.5) | async-done | bytes 1048608 | tf_op jit(solution)/shard_map/all_to_all | solution.py:254
  (78 shorter events, 50.0 us)
Async XLA Ops:
  2.9 3.8 %collective-permute-start.1 = (f32[512,256]{1,0:T(8,128)S(1)}, f32[512,256]{1,0:T(8,128)S(1)}, u32[]{:S(2)}, u32[]{:S(2)}) collective-permute-start(f32[512,256]{1,0:T(8,128)S(1)} %fusion), channel_id=1, source_target_pairs={{0,1},{1,0},{2,3},{3,2},{4,5},{5,4},{6,7},{7,6},{8,9},{9,8},{10,11... | collective-permute-start | bytes 1572872 | tf_op jit(solution)/shard_map/ppermute | solution.py:24
  6.6 6.1 %collective-permute-start.6 = (f32[512,256]{1,0:T(8,128)}, f32[512,256]{1,0:T(8,128)}, u32[]{:S(2)}, u32[]{:S(2)}) collective-permute-start(f32[512,256]{1,0:T(8,128)} %fusion.30), channel_id=1, source_target_pairs={{0,1},{1,0},{2,3},{3,2},{4,5},{5,4},{6,7},{7,6},{8,9},{9,8},{10,11... | collective-permute-start | bytes 1572872 | tf_op jit(solution)/shard_map/ppermute | solution.py:24
  12.3 4.4 %collective-permute-start.8 = (f32[512,256]{1,0:T(8,128)}, f32[512,256]{1,0:T(8,128)S(1)}, u32[]{:S(2)}, u32[]{:S(2)}) collective-permute-start(f32[512,256]{1,0:T(8,128)} %fusion.26), channel_id=1, source_target_pairs={{0,1},{1,0},{2,3},{3,2},{4,5},{5,4},{6,7},{7,6},{8,9},{9,8},{10,11... | collective-permute-start | bytes 1572872 | tf_op jit(solution)/shard_map/ppermute | solution.py:24
  16.7 3.0 %collective-permute-start.10 = (f32[512,256]{1,0:T(8,128)}, f32[512,256]{1,0:T(8,128)S(1)}, u32[]{:S(2)}, u32[]{:S(2)}) collective-permute-start(f32[512,256]{1,0:T(8,128)} %fusion.22), channel_id=1, source_target_pairs={{0,1},{1,0},{2,3},{3,2},{4,5},{5,4},{6,7},{7,6},{8,9},{9,8},{10,11... | collective-permute-start | bytes 1572872 | tf_op jit(solution)/shard_map/ppermute | solution.py:24
  25.9 3.0 %collective-permute-start = (f32[512,256]{1,0:T(8,128)}, f32[512,256]{1,0:T(8,128)S(1)}, u32[]{:S(2)}, u32[]{:S(2)}) collective-permute-start(f32[512,256]{1,0:T(8,128)} %fusion.16), channel_id=1, source_target_pairs={{0,1},{1,0},{2,3},{3,2},{4,5},{5,4},{6,7},{7,6},{8,9},{9,8},{10,11... | collective-permute-start | bytes 1572872 | tf_op jit(solution)/shard_map/ppermute | solution.py:24
  28.8 3.8 %collective-permute-start.3 = (f32[512,256]{1,0:T(8,128)S(1)}, f32[512,256]{1,0:T(8,128)S(1)}, u32[]{:S(2)}, u32[]{:S(2)}) collective-permute-start(f32[512,256]{1,0:T(8,128)S(1)} %fusion.14), channel_id=1, source_target_pairs={{0,1},{1,0},{2,3},{3,2},{4,5},{5,4},{6,7},{7,6},{8,9},{9,8},{10,11... | collective-permute-start | bytes 1572872 | tf_op jit(solution)/shard_map/ppermute | solution.py:24
  32.2 6.8 %collective-permute-start.4 = (f32[512,256]{1,0:T(8,128)S(1)}, f32[512,256]{1,0:T(8,128)S(1)}, u32[]{:S(2)}, u32[]{:S(2)}) collective-permute-start(f32[512,256]{1,0:T(8,128)S(1)} %fusion.10), channel_id=1, source_target_pairs={{0,1},{1,0},{2,3},{3,2},{4,5},{5,4},{6,7},{7,6},{8,9},{9,8},{10,11... | collective-permute-start | bytes 1572872 | tf_op jit(solution)/shard_map/ppermute | solution.py:24
  33.9 5.7 %collective-permute-start.5 = (f32[512,256]{1,0:T(8,128)S(1)}, f32[512,256]{1,0:T(8,128)S(1)}, u32[]{:S(2)}, u32[]{:S(2)}) collective-permute-start(f32[512,256]{1,0:T(8,128)S(1)} %fusion.6), channel_id=1, source_target_pairs={{0,1},{1,0},{2,3},{3,2},{4,5},{5,4},{6,7},{7,6},{8,9},{9,8},{10,11... | collective-permute-start | bytes 1572872 | tf_op jit(solution)/shard_map/ppermute | solution.py:24
  34.2 28.0 %collective-permute-start.7 = (f32[512,256]{1,0:T(8,128)}, f32[512,256]{1,0:T(8,128)S(1)}, u32[]{:S(2)}, u32[]{:S(2)}) collective-permute-start(f32[512,256]{1,0:T(8,128)} %fusion.80), channel_id=1, source_target_pairs={{0,2},{1,3},{2,0},{3,1},{4,6},{5,7},{6,4},{7,5},{8,10},{9,11},{10,... | collective-permute-start | bytes 1572872 | tf_op jit(solution)/shard_map/ppermute | solution.py:24
  37.0 24.2 %collective-permute-start.2 = (f32[512,256]{1,0:T(8,128)S(1)}, f32[512,256]{1,0:T(8,128)S(1)}, u32[]{:S(2)}, u32[]{:S(2)}) collective-permute-start(f32[512,256]{1,0:T(8,128)S(1)} %fusion.77), channel_id=1, source_target_pairs={{0,2},{1,3},{2,0},{3,1},{4,6},{5,7},{6,4},{7,5},{8,10},{9,11},{10,... | collective-permute-start | bytes 1572872 | tf_op jit(solution)/shard_map/ppermute | solution.py:24
  37.0 34.9 %collective-permute-start.9 = (f32[512,256]{1,0:T(8,128)}, f32[512,256]{1,0:T(8,128)S(1)}, u32[]{:S(2)}, u32[]{:S(2)}) collective-permute-start(f32[512,256]{1,0:T(8,128)} %fusion.81), channel_id=1, source_target_pairs={{0,2},{1,3},{2,0},{3,1},{4,6},{5,7},{6,4},{7,5},{8,10},{9,11},{10,... | collective-permute-start | bytes 1572872 | tf_op jit(solution)/shard_map/ppermute | solution.py:24
  39.6 21.6 %copy-start.2 = (f32[1,512,1024]{2,1,0:T(8,128)S(1)}, f32[1,512,1024]{2,1,0:T(8,128)}, u32[]{:S(2)}) copy-start(f32[1,512,1024]{2,1,0:T(8,128)} %param.10) | copy-start | bytes 6291460
  39.6 21.5 %copy-start.3 = (f32[1,512,1024]{2,1,0:T(8,128)S(1)}, f32[1,512,1024]{2,1,0:T(8,128)}, u32[]{:S(2)}) copy-start(f32[1,512,1024]{2,1,0:T(8,128)} %param.11) | copy-start | bytes 6291460
  110.4 19.2 %all-to-all-start = ((f32[8,64,256]{2,1,0:T(8,128)}), f32[8,64,256]{2,1,0:T(8,128)S(1)}, u32[]{:S(2)}, u32[]{:S(2)}) async-start(f32[8,64,256]{2,1,0:T(8,128)} %bitcast.6), calls=%async_computation | async-start | bytes 1048576 | tf_op jit(solution)/shard_map/all_to_all | solution.py:239
  114.0 13.2 %collective-permute-start.11 = (f32[512,256]{1,0:T(8,128)}, f32[512,256]{1,0:T(8,128)S(1)}, u32[]{:S(2)}, u32[]{:S(2)}) collective-permute-start(f32[512,256]{1,0:T(8,128)} %fusion.82), channel_id=1, source_target_pairs={{0,2},{1,3},{2,0},{3,1},{4,6},{5,7},{6,4},{7,5},{8,10},{9,11},{10,... | collective-permute-start | bytes 1572872 | tf_op jit(solution)/shard_map/ppermute | solution.py:24
  129.6 18.4 %all-to-all-start.3 = ((f32[8,64,256]{2,1,0:T(8,128)}), f32[8,64,256]{2,1,0:T(8,128)S(1)}, u32[]{:S(2)}, u32[]{:S(2)}) async-start(f32[8,64,256]{2,1,0:T(8,128)} %bitcast.9), calls=%async_computation.3 | async-start | bytes 1048576 | tf_op jit(solution)/shard_map/all_to_all | solution.py:239
  152.2 1.4 collective-permute-start.12
  154.3 3.6 %collective-permute-start.13 = (f32[8,128]{1,0:T(8,128)S(1)}, f32[8,128]{1,0:T(8,128)S(1)}, u32[]{:S(2)}, u32[]{:S(2)}) collective-permute-start(f32[8,128]{1,0:T(8,128)S(1)} %add.107), channel_id=1, source_target_pairs={{0,2},{1,3},{2,0},{3,1},{4,6},{5,7},{6,4},{7,5},{8,10},{9,11},{10,... | collective-permute-start | bytes 12296 | tf_op jit(solution)/shard_map/ppermute | solution.py:24
  157.9 3.6 %collective-permute-start.14 = (f32[8,128]{1,0:T(8,128)S(1)}, f32[8,128]{1,0:T(8,128)S(1)}, u32[]{:S(2)}, u32[]{:S(2)}) collective-permute-start(f32[8,128]{1,0:T(8,128)S(1)} %add.108), channel_id=1, source_target_pairs={{0,4},{4,0},{8,12},{12,8},{16,20},{20,16},{24,28},{28,24},{1,5},{5... | collective-permute-start | bytes 12296 | tf_op jit(solution)/shard_map/ppermute | solution.py:24
  161.5 3.6 %collective-permute-start.15 = (f32[8,128]{1,0:T(8,128)S(1)}, f32[8,128]{1,0:T(8,128)S(1)}, u32[]{:S(2)}, u32[]{:S(2)}) collective-permute-start(f32[8,128]{1,0:T(8,128)S(1)} %add.109), channel_id=1, source_target_pairs={{0,8},{4,12},{8,0},{12,4},{16,24},{20,28},{24,16},{28,20},{1,9},{5... | collective-permute-start | bytes 12296 | tf_op jit(solution)/shard_map/ppermute | solution.py:24
  165.1 4.5 %collective-permute-start.16 = (f32[8,128]{1,0:T(8,128)S(1)}, f32[8,128]{1,0:T(8,128)S(1)}, u32[]{:S(2)}, u32[]{:S(2)}) collective-permute-start(f32[8,128]{1,0:T(8,128)S(1)} %add.110), channel_id=1, source_target_pairs={{0,16},{4,20},{8,24},{12,28},{16,0},{20,4},{24,8},{28,12},{1,17},{... | collective-permute-start | bytes 12296 | tf_op jit(solution)/shard_map/ppermute | solution.py:24
  173.9 29.2 %copy-start.4 = (f32[512,256]{1,0:T(8,128)S(1)}, f32[512,256]{1,0:T(8,128)}, u32[]{:S(2)}) copy-start(f32[512,256]{1,0:T(8,128)} %get-tuple-element.75) | copy-start | bytes 1572868
  173.9 25.6 %all-to-all-start.4 = ((f32[8,64,512]{2,1,0:T(8,128)}), f32[8,64,512]{2,1,0:T(8,128)S(1)}, u32[]{:S(2)}, u32[]{:S(2)}) async-start(f32[8,64,512]{2,1,0:T(8,128)} %mix.2), calls=%async_computation.4 | async-start | bytes 2097152 | tf_op jit(solution)/shard_map/all_to_all | solution.py:254
  199.5 28.2 %all-to-all-start.5 = ((f32[8,64,512]{2,1,0:T(8,128)}), f32[8,64,512]{2,1,0:T(8,128)S(1)}, u32[]{:S(2)}, u32[]{:S(2)}) async-start(f32[8,64,512]{2,1,0:T(8,128)} %mix.3), calls=%async_computation.5 | async-start | bytes 2097152 | tf_op jit(solution)/shard_map/all_to_all | solution.py:254
  (8 other events, 41.9 us)

commit v3 on v0

v3 whole, which is shorter than its diff:
```python
import functools
import math

import jax
import jax.numpy as jnp
import numpy as np
from jax import lax
from jax.experimental import pallas as pl
from jax.experimental.pallas import tpu as pltpu
from jax.sharding import PartitionSpec as P


D = 2048
KV_WIDTH = 512
ROUNDS = 2
LEARNING_RATE = 0.25
HIGH = lax.Precision.HIGHEST
LANES = 128
CHUNKS = (256, 256, 256, 256)
STARTS = tuple(sum(CHUNKS[:k]) for k in range(len(CHUNKS)))
COUNT = len(CHUNKS)
EARLY = 2


SMEM = pl.BlockSpec(memory_space=pltpu.SMEM)
VMEM = pl.BlockSpec(memory_space=pltpu.VMEM)


def flip(value, axis, mask):
    pairs = [(source, source ^ mask) for source in range(lax.axis_size(axis))]
    return lax.ppermute(value, axis, pairs)


def after(value, *others):
    return lax.optimization_barrier((value, *others))[0]


def neighbours(w, workers):
    return (w ^ 1, w ^ 2, (w - 4) % workers, (w + 4) % workers)


def pair_list(workers):
    return [(a, b) for a in range(workers) for b in range(a + 1, workers)]


def pair_rows(workers):
    return -(-len(pair_list(workers)) // 8) * 8


def product(left, right):
    return lax.dot_general(left, right, (((0,), (0,)), ((), ())), preferred_element_type=jnp.float32)


def blocks_of(left_ref, upstream_ref, rows, places, outs):
    for i, place in enumerate(places):
        left = left_ref[:, pl.ds(pl.multiple_of(place * rows, LANES), rows)]
        for k in range(COUNT):
            right = upstream_ref[:, STARTS[k] : STARTS[k] + CHUNKS[k]]
            outs[i * COUNT + k][...] = product(left, right)


def first_kernel(rows, cuts, at_ref, features_hbm, upstream_hbm, *rest):
    outs, (left_ref, upstream_ref, sems) = rest[: 2 * COUNT], rest[2 * COUNT :]
    at = at_ref[0]
    columns = pl.ds(pl.multiple_of(at // 2 * (2 * rows), LANES), 2 * rows)
    copies = []
    for i, cut in enumerate(cuts):
        copies.append(pltpu.make_async_copy(features_hbm.at[0, cut, columns], left_ref.at[cut], sems.at[2 * i]))
        copies.append(pltpu.make_async_copy(upstream_hbm.at[0, cut], upstream_ref.at[cut], sems.at[2 * i + 1]))
    for copy in copies:
        copy.start()
    for copy in copies:
        copy.wait()
    side = at % 2
    blocks_of(left_ref, upstream_ref, rows, (1 - side, side), outs)


def second_kernel(rows, at_ref, features_ref, upstream_ref, *outs):
    at = at_ref[0]
    side = at % 2
    blocks_of(features_ref, upstream_ref, rows, (at + 1 - 2 * side, at), outs)


def multiply(at, features, upstream, rows, first):
    outs = [jax.ShapeDtypeStruct((rows, size), jnp.float32) for size in CHUNKS] * 2
    if not first:
        outs = pl.pallas_call(
            functools.partial(second_kernel, rows),
            in_specs=[SMEM, VMEM, VMEM],
            out_specs=[VMEM] * len(outs),
            out_shape=outs,
            compiler_params=pltpu.CompilerParams(vmem_limit_bytes=24 << 20),
            name="second",
        )(at, features[0], upstream[0])
        return list(outs[:COUNT]), list(outs[COUNT:])
    hbm = pl.BlockSpec(memory_space=pltpu.HBM)
    tokens = features.shape[1]
    step = tokens // 6 if tokens % 96 == 0 else tokens
    cuts = [slice(start, start + step) for start in range(0, tokens, step)]
    outs = pl.pallas_call(
        functools.partial(first_kernel, rows, cuts),
        in_specs=[SMEM, hbm, hbm],
        out_specs=[VMEM] * len(outs),
        out_shape=outs,
        scratch_shapes=[
            pltpu.VMEM((tokens, 2 * rows), features.dtype),
            pltpu.VMEM(upstream.shape[1:], upstream.dtype),
            pltpu.SemaphoreType.DMA((2 * len(cuts),)),
        ],
        compiler_params=pltpu.CompilerParams(vmem_limit_bytes=60 << 20),
        name="first",
    )(at, features, upstream)
    return list(outs[:COUNT]), list(outs[COUNT:])


def velocity_kernel(gradient_ref, momentum_ref, *rest):
    rest[-1][...] = 0.5 * momentum_ref[...] + gradient_ref[...]


def velocity_chunk(gradient, momentum, velocity, k):
    rows, width = gradient.shape
    narrow = pl.BlockSpec((rows, width), lambda i: (0, 0))
    wide = pl.BlockSpec((rows, width), lambda i: (0, STARTS[k] // width))
    args, specs, alias = [gradient, momentum], [narrow, wide], {}
    if velocity is not None:
        args.append(velocity)
        specs.append(pl.BlockSpec(memory_space=pl.ANY))
        alias = {2: 0}
    return pl.pallas_call(
        velocity_kernel,
        grid=(1,),
        in_specs=specs,
        out_specs=wide,
        out_shape=jax.ShapeDtypeStruct(momentum.shape, jnp.float32),
        input_output_aliases=alias,
        compiler_params=pltpu.CompilerParams(vmem_limit_bytes=8 << 20),
        name="velocity",
    )(*args)


def update_kernel(k, count, grouped, me_ref, *rest):
    terms, (momentum_ref, weights_ref, gradient_ref, *outs) = rest[:count], rest[count:]
    me = me_ref[0]
    rows = gradient_ref.shape[0]
    cut = slice(STARTS[k], STARTS[k] + CHUNKS[k])
    gradient = terms[0][...]
    for term in terms[1:]:
        gradient = gradient + term[...]
    gradient_ref[...] = gradient
    current = weights_ref[:, cut] - LEARNING_RATE * (0.5 * momentum_ref[:, cut] + gradient)
    size = outs[0].shape[0]
    parts = rows // size
    for place in range(parts):
        if grouped:
            for mask, out in enumerate(outs):

                @pl.when((me >= grouped) == ((place ^ mask) == 1))
                def _(out=out, place=place):
                    out[...] = current[place * size : (place + 1) * size]

        else:
            for mask, out in enumerate(outs):

                @pl.when((me ^ mask) == place)
                def _(out=out, place=place):
                    out[...] = current[place * size : (place + 1) * size]


def update(me, terms, momentum, weights, k, group, grouped):
    rows = terms[0].shape[0]
    parts = 2 if grouped else 2 * group
    full = jax.ShapeDtypeStruct(terms[0].shape, jnp.float32)
    cut = jax.ShapeDtypeStruct((rows // parts, CHUNKS[k]), jnp.float32)
    gradient, *outs = pl.pallas_call(
        functools.partial(update_kernel, k, len(terms), group if grouped else 0),
        in_specs=[SMEM] + [VMEM] * (len(terms) + 2),
        out_specs=[VMEM] * (1 + parts),
        out_shape=[full] + [cut] * parts,
        compiler_params=pltpu.CompilerParams(vmem_limit_bytes=8 << 20),
        name="update",
    )(me, *terms, momentum, weights)
    return gradient, outs


def regroup_kernel(group, me_ref, keep_ref, got_ref, *outs):
    rank = me_ref[0] % group
    size = outs[0].shape[1]
    for mask, out in enumerate(outs):
        cut = pl.ds(pl.multiple_of((rank ^ mask) * size, 8), size)
        out[0] = keep_ref[cut, :]
        out[1] = got_ref[cut, :]


def regroup(me, keep, got, group):
    rows, width = keep.shape
    return pl.pallas_call(
        functools.partial(regroup_kernel, group),
        in_specs=[SMEM, VMEM, VMEM],
        out_specs=[VMEM] * group,
        out_shape=[jax.ShapeDtypeStruct((2, rows // group, width), jnp.float32)] * group,
        compiler_params=pltpu.CompilerParams(vmem_limit_bytes=8 << 20),
        name="regroup",
    )(me, keep, got)


def pieces_of(refs, cut):
    if len(refs[0].shape) == 2:
        return [ref[:, cut] for ref in refs]
    return [ref[half, :, cut] for half in range(2) for ref in refs]


def gap_row(left, right):
    gap = left - right
    return jnp.sum(gap * gap, axis=0, keepdims=True)


def add_squares(refs, h_of, rows, sums_ref):
    for lane, h in enumerate(h_of):
        old = pieces_of(refs, slice(lane * LANES, (lane + 1) * LANES))
        for place, (a, b) in enumerate(pair_list(len(old))):
            at = slice(h * rows + place, h * rows + place + 1)
            sums_ref[at, :] = sums_ref[at, :] + gap_row(old[a], old[b])


def squares_kernel(h_of, *rest):
    refs, sums_ref = rest[:-1], rest[-1]
    sums_ref[...] = jnp.zeros_like(sums_ref)
    add_squares(refs, h_of, sums_ref.shape[0] // 2, sums_ref)


def squares(pieces, workers, h_of):
    return pl.pallas_call(
        functools.partial(squares_kernel, h_of),
        in_specs=[VMEM] * len(pieces),
        out_specs=VMEM,
        out_shape=jax.ShapeDtypeStruct((2 * pair_rows(workers), LANES), jnp.float32),
        compiler_params=pltpu.CompilerParams(vmem_limit_bytes=4 << 20),
        name="squares",
    )(*pieces)


def lane_sums(sums):
    ones = jnp.ones((8, LANES), jnp.float32)
    return lax.dot_general(ones, sums, (((1,), (1,)), ((), ())), precision=HIGH, preferred_element_type=jnp.float32)


def pack_kernel(workers, tokens, parts, h_of, me_ref, mix_ref, *rest):
    rows = pair_rows(workers)
    sums, refs = rest[:parts], rest[parts:-3]
    packed_ref, table_ref, total_ref = rest[-3:]
    me = me_ref[0]
    total = sums[0][...]
    for part in sums[1:]:
        total = total + part[...]
    total_ref[...] = total
    add_squares(refs, h_of, rows, total_ref)
    packed_ref[...] = jnp.zeros_like(packed_ref)
    for h in range(2):
        for place, (a, b) in enumerate(pair_list(workers)):
            row = total_ref[h * rows + place : h * rows + place + 1, :]
            table_ref[a * workers + b : a * workers + b + 1, :] = row
            table_ref[b * workers + a : b * workers + a + 1, :] = row
        for place, (a, b) in enumerate(pair_list(workers)):
            row = table_ref[pl.ds((a ^ me) * workers + (b ^ me), 1), :]
            total_ref[h * rows + place : h * rows + place + 1, :] = row
        packed_ref[h : h + 1, 0:rows] = lane_sums(total_ref[h * rows : (h + 1) * rows, :])[0:1]
    lane = lax.broadcasted_iota(jnp.int32, (1, LANES), 1)
    row = jnp.zeros((1, LANES), jnp.float32)
    for k in range(5):
        weight = mix_ref[0, k].astype(jnp.float32) * (1.0 / tokens)
        row = row + jnp.where(lane == me * 5 + k, weight, 0.0)
    packed_ref[2:3, :] = row


def pack(sums, pieces, mix_weights, me, workers, tokens, h_of):
    return pl.pallas_call(
        functools.partial(pack_kernel, workers, tokens, len(sums), h_of),
        in_specs=[SMEM, SMEM] + [VMEM] * (len(sums) + len(pieces)),
        out_specs=VMEM,
        out_shape=jax.ShapeDtypeStruct((8, LANES), jnp.float32),
        scratch_shapes=[
            pltpu.VMEM((workers * workers, LANES), jnp.float32),
            pltpu.VMEM((2 * pair_rows(workers), LANES), jnp.float32),
        ],
        compiler_params=pltpu.CompilerParams(vmem_limit_bytes=4 << 20),
        name="pack",
    )(me, mix_weights, *sums, *pieces)


def selectors(workers):
    table = np.zeros((5, workers, workers, LANES), np.float32)
    for place, (a, b) in enumerate(pair_list(workers)):
        table[0, a, b, place] = table[0, b, a, place] = 1.0
    for w in range(workers):
        for k, j in enumerate(neighbours(w, workers)):
            table[1, w, j, w * 5 + k + 1] += 1.0
            table[3, j, w, w * 5 + k + 1] += 1.0
        table[2, w, :, w * 5 : w * 5 + 5] = 1.0
        table[4, :, w, w * 5 : w * 5 + 5] = 1.0
    return table.reshape(-1, LANES)


def spread(select, row):
    wide = jnp.broadcast_to(row, (LANES, LANES))
    return lax.dot_general(select, wide, (((1,), (1,)), ((), ())), precision=HIGH, preferred_element_type=jnp.float32)


def fill_matrices(workers, clip_ref, packed_ref, select_ref, matrix_ref):
    size = workers * workers
    table = lambda k: select_ref[k * size : (k + 1) * size, :]
    rows_of = lambda flat: [flat[w * workers : (w + 1) * workers] for w in range(workers)]
    mixing = packed_ref[2:3, :]
    share = rows_of(spread(table(1), mixing) / spread(table(2), mixing))
    share_t = rows_of(spread(table(3), mixing) / spread(table(4), mixing))
    place = lax.broadcasted_iota(jnp.int32, (workers, LANES), 0)
    eye = [jnp.where(place == w, 1.0, 0.0) for w in range(workers)]
    radius = [clip_ref[r].astype(jnp.float32) * (math.sqrt(D * KV_WIDTH) / 1000.0) for r in range(ROUNDS)]

    def times(left, right):
        out = []
        for w in range(workers):
            total = None
            for j in range(workers):
                term = left[w][j : j + 1, :] * right[j]
                total = term if total is None else total + term
            out.append(total)
        return out

    for h in range(2):
        first = rows_of(spread(table(0), packed_ref[h : h + 1, :]))
        now, total, total_t = first, None, None
        for r in range(ROUNDS):
            factor = [radius[r] / jnp.maximum(jnp.sqrt(d), radius[r]) for d in now]
            step = [s * f for s, f in zip(share, factor)]
            step = [a + e * (1.0 - jnp.sum(a, axis=0, keepdims=True)) for a, e in zip(step, eye)]
            total = step if total is None else times(step, total)
            if r + 1 < ROUNDS:
                step_t = [s * f for s, f in zip(share_t, factor)]
                keep = 1.0 - functools.reduce(lambda a, b: a + b, step_t)
                step_t = [a + e * keep for a, e in zip(step_t, eye)]
                total_t = step_t if total_t is None else times(total_t, step_t)
                inner = times(times(total, first), total_t)
                diag = functools.reduce(lambda a, b: a + b, [i * e for i, e in zip(inner, eye)])
                now = [
                    jnp.maximum(i - 0.5 * (diag + diag[w : w + 1, :]), 0.0) for w, i in enumerate(inner)
                ]
        for w in range(workers):
            at = h * size + w * workers
            matrix_ref[at : at + workers, :] = total[w]


def mix_kernel(workers, half, counts, masks, first, me_ref, *rest):
    if first:
        clip_ref, packed_ref, select_ref, *rest = rest
        matrix_ref, *rest = rest[-1:] + rest[:-1]
        fill_matrices(workers, clip_ref, packed_ref, select_ref, matrix_ref)
    else:
        matrix_ref, *rest = rest
    chunks = []
    for count in counts:
        chunks.append(rest[:count])
        rest = rest[count:]
    me = me_ref[0]
    for k, refs in enumerate(chunks):
        for lane in range(CHUNKS[k] // LANES):
            start = STARTS[k] + lane * LANES
            base = start // half * workers * workers
            old = pieces_of(refs, slice(lane * LANES, (lane + 1) * LANES))
            for mask, out in zip(masks, rest):
                value = None
                for other, rows in enumerate(old):
                    share = matrix_ref[pl.ds(base + (me ^ mask) * workers + (me ^ other), 1), :]
                    value = share * rows if value is None else value + share * rows
                out[:, start : start + LANES] = value


def mix(masks, me, matrix, clip_radius, packed, chunks, workers, rows, width):
    first = matrix is None
    table = jax.ShapeDtypeStruct((2 * workers * workers, LANES), jnp.float32)
    piece = jax.ShapeDtypeStruct((rows, width), jnp.float32)
    head = (clip_radius, packed, selectors(workers)) if first else (matrix,)
    counts = [len(chunk) for chunk in chunks]
    return pl.pallas_call(
        functools.partial(mix_kernel, workers, width // 2, counts, masks, first),
        in_specs=[SMEM] + ([SMEM] if first else []) + [VMEM] * (len(head) - first + sum(counts)),
        out_specs=[VMEM] * (len(masks) + first),
        out_shape=[piece] * len(masks) + [table] * first,
        compiler_params=pltpu.CompilerParams(vmem_limit_bytes=16 << 20),
        name="mix",
    )(me, *head, *[piece for chunk in chunks for piece in chunk])


def per_device(inputs, cotangent, weights, momentum, mix_weights, clip_radius):
    tokens = lax.axis_size("tok")
    workers = lax.axis_size("worker")
    group = workers // 2
    tok, me = lax.axis_index("tok"), lax.axis_index("worker")
    here = me.reshape(1)
    rows, width = weights.shape[1:]
    piece = rows // workers
    half = width // 2
    h_of = [tuple((start + lane) // half for lane in range(0, size, LANES)) for start, size in zip(STARTS, CHUNKS)]
    levels = tokens.bit_length() - 1
    order = [None]

    last = 1 << (levels - 1)
    index = lambda offset: (tok ^ offset).reshape(1)
    leaves = {}
    for offset in [*range(last, tokens, 2), *range(0, last, 2)]:
        at = index(offset) if order[0] is None else after(index(offset), order[0])
        leaves[offset + 1], leaves[offset] = multiply(at, inputs, cotangent, rows, order[0] is None)
        order[0] = leaves[offset][0]

    def arrived(offset, level, k):
        terms = []
        for step in range(1, level + 1):
            mask = 1 << (step - 1)
            away = reduced(offset ^ mask, step - 1, k)
            terms.append(flip(away, "tok", mask))
        return terms

    def reduced(offset, level, k):
        return sum(arrived(offset, level, k), leaves[offset][k])

    def send_terms(k, *gates):
        leaves[last][k] = after(leaves[last][k], *gates)
        away = reduced(last, levels - 1, k)
        return flip(away, "tok", last), away

    aways, away = [], leaves[last][0]
    for k in range(EARLY):
        moved, away = send_terms(k, away)
        aways.append(moved)
    extras = [arrived(0, levels - 1, k) for k in range(COUNT)]
    velocity, chunks, sums = None, [], []
    for k in range(COUNT):
        grouped = k < COUNT - 1
        away = after(aways[k], gradient) if k else aways[k]
        terms = [leaves[0][k], *extras[k], away]
        gradient, outs = update(here, terms, momentum[0], weights[0], k, group, grouped)
        if grouped:
            got = flip(outs[1], "worker", group)
            pieces = list(regroup(here, outs[0], got, group))
            for mask in range(1, group):
                pieces[mask] = flip(pieces[mask], "worker", mask)
            sums.append(squares(pieces, workers, h_of[k]))
        else:
            pieces = list(outs)
            for mask in [*range(group, workers), *range(1, group)]:
                pieces[mask] = flip(pieces[mask], "worker", mask)
        chunks.append(pieces)
        if len(aways) < COUNT:
            moved, _ = send_terms(len(aways), gradient)
            aways.append(moved)
        velocity = velocity_chunk(gradient, momentum[0], velocity, k)
    packed = pack(sums, chunks[-1], mix_weights, here, workers, tokens, h_of[-1])
    for axis, size in (("tok", tokens), ("worker", workers)):
        mask = 1
        while mask < size:
            packed = packed + flip(packed, axis, mask)
            mask *= 2
    news = {}
    far = tuple(range(group, workers))
    *pieces, matrix = mix(far, here, None, clip_radius, packed, chunks, workers, piece, width)
    for mask, value in zip(far, pieces):
        news[mask] = flip(value, "worker", mask)
    near = tuple(range(group))
    pieces = mix(near, here, matrix, clip_radius, packed, chunks, workers, piece, width)
    news[0] = pieces[0]
    for mask in near[1:]:
        news[mask] = flip(pieces[mask], "worker", mask)
    new = jnp.zeros((rows, width), jnp.float32)
    for mask in [*near, *far]:
        new = lax.dynamic_update_slice_in_dim(new, news[mask], (me ^ mask) * piece, 0)
    return new[None], velocity[None]


def solution(mesh):
    placed = (
        P("worker", "tok", None),
        P("worker", "tok", None),
        P("worker", "tok", None),
        P("worker", "tok", None),
        P("worker", None),
        P(),
    )

    return jax.shard_map(
        per_device,
        mesh=mesh,
        in_specs=placed,
        out_specs=(P("worker", "tok", None), P("worker", "tok", None)),
        check_vma=False,
    )
```

time: 334 us -> 195 us (0.58)
  the two profiles are of different devices: /device:TPU:0 before, /device:TPU:12 now
where the time goes in v3:
time: 195 us; the launch traced here: 194 us
  waiting for transfers between devices  102 us (52%)
  starting transfers between devices  46.2 us (24%)
  Pallas kernels  23.9 us (12%)
  local copies, waits for them, and re-layouts  17.6 us (9%)
  other arithmetic  4.06 us (2%)
    ppermute x43, waiting for transfers between devices, flip(): return lax.ppermute(value, axis, pairs)  102 us
    ppermute x43, starting transfers between devices, flip(): return lax.ppermute(value, axis, pairs)  46.2 us
    unnamed x78, local copies, waits for them, and re-layouts  16.3 us
    pallas_call x1, Pallas kernels, multiply(): pl.pallas_call(functools.partial(first_kernel, rows, cuts), in_specs=[SME...  7.48 us
    add x4, other arithmetic, reduced(): return sum(arrived(offset, level, k), leaves[offset][k])  4.05 us
    pallas_call x1, Pallas kernels, multiply(): pl.pallas_call(functools.partial(second_kernel, rows), in_specs=[SMEM, VM...  3.92 us
  transfers between devices with their start and end apart: 43, of which 23 were waited for; matrix products, arithmetic and copies ran while one was open for 3% of the time, Pallas kernels for 6%

profile of v3, /device:TPU:12, one launch (start us, length us, event | category | flops | bytes accessed | tf_op | source)
XLA Modules:
  0.0 194.2 jit_solution(2033877437304234402)
XLA Ops:
  0.6 7.5 %first.1 = (f32[512,256]{1,0:T(8,128)}, f32[512,256]{1,0:T(8,128)}, f32[512,256]{1,0:T(8,128)}, f32[512,256]{1,0:T(8,128)}, f32[512,256]{1,0:T(8,128)}, /*index=...) custom-call(s32[1]{0:T(128)} %bitcast.2.at_ref, bf16[1,1536,2048]{2,1,0:T(8,128)(2,1)} %features_hbm.1, ...), custom_call_target="tpu_custom_call" | custom-call | tf_op jit(solution)/shard_map/first/pallas_call | solution.py:100
  8.7 2.8 %copy-done.3 = bf16[1,1536,2048]{2,1,0:T(8,128)(2,1)S(1)} copy-done((bf16[1,1536,2048]{2,1,0:T(8,128)(2,1)S(1)}, bf16[1,1536,2048]{2,1,0:T(8,128)(2,1)}, u32[]{:S(2)}) %copy-start.3) | copy-done | bytes 6291480
  11.5 3.9 %second.1 = (f32[512,256]{1,0:T(8,128)S(1)}, f32[512,256]{1,0:T(8,128)}, f32[512,256]{1,0:T(8,128)S(1)}, f32[512,256]{1,0:T(8,128)S(1)}, f32[512,256]{1,0:T(8,12...) custom-call(s32[1]{0:T(128)} %bitcast.1.at_ref, bf16[1536,2048]{1,0:T(8,128)(2,1)S(1)} %bitcast.36, ...), custom_call_target="tpu_custom_call" | custom-call | tf_op jit(solution)/shard_map/second/pallas_call | solution.py:87
  23.2 10.7 %collective-permute-done.2.rest_2_ = f32[512,256]{1,0:T(8,128)} collective-permute-done((f32[512,256]{1,0:T(8,128)}, f32[512,256]{1,0:T(8,128)}, u32[]{:S(2)}, u32[]{:S(2)}) %collective-permute-start.2) | collective-permute-done | bytes 524320 | tf_op jit(solution)/shard_map/ppermute | solution.py:31
  40.8 4.4 %collective-permute-done.9.rest_2_ = f32[512,256]{1,0:T(8,128)} collective-permute-done((f32[512,256]{1,0:T(8,128)}, f32[512,256]{1,0:T(8,128)}, u32[]{:S(2)}, u32[]{:S(2)}) %collective-permute-start.9) | collective-permute-done | bytes 524320 | tf_op jit(solution)/shard_map/ppermute | solution.py:31
  47.5 2.6 %collective-permute-start.10 = (f32[256,256]{1,0:T(8,128)S(1)}, f32[256,256]{1,0:T(8,128)S(1)}, u32[]{:S(2)}, u32[]{:S(2)}) collective-permute-start(f32[256,256]{1,0:T(8,128)S(1)} %get-tuple-element.85), channel_id=1, source_target_pairs={{0,16},{4,20},{8,24},{12,28},{16,0},{20,4},{24,8},{28,12},{1,17},{... | collective-permute-start | bytes 786440 | tf_op jit(solution)/shard_map/ppermute | solution.py:31
  51.8 4.5 %collective-permute-done.16.rest_2_ = f32[512,256]{1,0:T(8,128)S(1)} collective-permute-done((f32[512,256]{1,0:T(8,128)S(1)}, f32[512,256]{1,0:T(8,128)S(1)}, u32[]{:S(2)}, u32[]{:S(2)}) %collective-permute-start.16) | collective-permute-done | bytes 524320 | tf_op jit(solution)/shard_map/ppermute | solution.py:31
  56.3 2.6 %collective-permute-start.3 = (f32[256,256]{1,0:T(8,128)S(1)}, f32[256,256]{1,0:T(8,128)S(1)}, u32[]{:S(2)}, u32[]{:S(2)}) collective-permute-start(f32[256,256]{1,0:T(8,128)S(1)} %get-tuple-element.72), channel_id=1, source_target_pairs={{0,16},{4,20},{8,24},{12,28},{16,0},{20,4},{24,8},{28,12},{1,17},{... | collective-permute-start | bytes 786440 | tf_op jit(solution)/shard_map/ppermute | solution.py:31
  60.2 12.9 %collective-permute-done.10.got_ref = f32[256,256]{1,0:T(8,128)S(1)} collective-permute-done((f32[256,256]{1,0:T(8,128)S(1)}, f32[256,256]{1,0:T(8,128)S(1)}, u32[]{:S(2)}, u32[]{:S(2)}) %collective-permute-start.10) | collective-permute-done | bytes 262176 | tf_op jit(solution)/shard_map/ppermute | solution.py:31
  74.7 4.0 %collective-permute-done.3.got_ref = f32[256,256]{1,0:T(8,128)S(1)} collective-permute-done((f32[256,256]{1,0:T(8,128)S(1)}, f32[256,256]{1,0:T(8,128)S(1)}, u32[]{:S(2)}, u32[]{:S(2)}) %collective-permute-start.3) | collective-permute-done | bytes 262176 | tf_op jit(solution)/shard_map/ppermute | solution.py:31
  82.4 3.7 %collective-permute-done.12.rest_2_.rest_9_.rest_7_ = f32[2,64,256]{2,1,0:T(8,128)S(1)} collective-permute-done((f32[2,64,256]{2,1,0:T(8,128)S(1)}, f32[2,64,256]{2,1,0:T(8,128)S(1)}, u32[]{:S(2)}, u32[]{:S(2)}) %collective-permute-start.12) | collective-permute-done | bytes 131104 | tf_op jit(solution)/shard_map/ppermute | solution.py:31
  101.0 3.3 %collective-permute-start.26 = (f32[64,256]{1,0:T(8,128)S(1)}, f32[64,256]{1,0:T(8,128)S(1)}, u32[]{:S(2)}, u32[]{:S(2)}) collective-permute-start(f32[64,256]{1,0:T(8,128)S(1)} %get-tuple-element.113), channel_id=1, source_target_pairs={{0,12},{4,8},{8,4},{12,0},{16,28},{20,24},{24,20},{28,16},{1,13},{... | collective-permute-start | bytes 196616 | tf_op jit(solution)/shard_map/ppermute | solution.py:31
  108.2 2.6 %collective-permute-start.29 = (f32[64,256]{1,0:T(8,128)S(1)}, f32[64,256]{1,0:T(8,128)S(1)}, u32[]{:S(2)}, u32[]{:S(2)}) collective-permute-start(f32[64,256]{1,0:T(8,128)S(1)} %get-tuple-element.116), channel_id=1, source_target_pairs={{0,24},{4,28},{8,16},{12,20},{16,8},{20,12},{24,0},{28,4},{1,25},{... | collective-permute-start | bytes 196616 | tf_op jit(solution)/shard_map/ppermute | solution.py:31
  121.9 3.1 %collective-permute-done.32 = f32[8,128]{1,0:T(8,128)S(1)} collective-permute-done((f32[8,128]{1,0:T(8,128)S(1)}, f32[8,128]{1,0:T(8,128)S(1)}, u32[]{:S(2)}, u32[]{:S(2)}) %collective-permute-start.32) | collective-permute-done | bytes 4128 | tf_op jit(solution)/shard_map/ppermute | solution.py:31
  125.6 3.1 %collective-permute-done.33 = f32[8,128]{1,0:T(8,128)S(1)} collective-permute-done((f32[8,128]{1,0:T(8,128)S(1)}, f32[8,128]{1,0:T(8,128)S(1)}, u32[]{:S(2)}, u32[]{:S(2)}) %collective-permute-start.33) | collective-permute-done | bytes 4128 | tf_op jit(solution)/shard_map/ppermute | solution.py:31
  128.7 3.6 %collective-permute-done.34 = f32[8,128]{1,0:T(8,128)S(1)} collective-permute-done((f32[8,128]{1,0:T(8,128)S(1)}, f32[8,128]{1,0:T(8,128)S(1)}, u32[]{:S(2)}, u32[]{:S(2)}) %collective-permute-start.34) | collective-permute-done | bytes 4128 | tf_op jit(solution)/shard_map/ppermute | solution.py:31
  132.6 4.2 %collective-permute-done.35 = f32[8,128]{1,0:T(8,128)S(1)} collective-permute-done((f32[8,128]{1,0:T(8,128)S(1)}, f32[8,128]{1,0:T(8,128)S(1)}, u32[]{:S(2)}, u32[]{:S(2)}) %collective-permute-start.35) | collective-permute-done | bytes 4128 | tf_op jit(solution)/shard_map/ppermute | solution.py:31
  147.9 2.7 %collective-permute-start.38 = (f32[64,1024]{1,0:T(8,128)S(1)}, f32[64,1024]{1,0:T(8,128)S(1)}, u32[]{:S(2)}, u32[]{:S(2)}) collective-permute-start(f32[64,1024]{1,0:T(8,128)S(1)} %copy-done.31), channel_id=1, source_target_pairs={{0,12},{4,8},{8,4},{12,0},{16,28},{20,24},{24,20},{28,16},{1,13},{... | collective-permute-start | bytes 786440 | tf_op jit(solution)/shard_map/ppermute | solution.py:31
  156.3 2.6 %collective-permute-done.37 = f32[64,1024]{1,0:T(8,128)S(1)} collective-permute-done((f32[64,1024]{1,0:T(8,128)S(1)}, f32[64,1024]{1,0:T(8,128)S(1)}, u32[]{:S(2)}, u32[]{:S(2)}) %collective-permute-start.37) | collective-permute-done | bytes 262176 | tf_op jit(solution)/shard_map/ppermute | solution.py:31
  160.9 2.5 %collective-permute-done.38 = f32[64,1024]{1,0:T(8,128)S(1)} collective-permute-done((f32[64,1024]{1,0:T(8,128)S(1)}, f32[64,1024]{1,0:T(8,128)S(1)}, u32[]{:S(2)}, u32[]{:S(2)}) %collective-permute-start.38) | collective-permute-done | bytes 262176 | tf_op jit(solution)/shard_map/ppermute | solution.py:31
  163.4 15.9 %collective-permute-done.39 = f32[64,1024]{1,0:T(8,128)S(1)} collective-permute-done((f32[64,1024]{1,0:T(8,128)S(1)}, f32[64,1024]{1,0:T(8,128)S(1)}, u32[]{:S(2)}, u32[]{:S(2)}) %collective-permute-start.39) | collective-permute-done | bytes 262176 | tf_op jit(solution)/shard_map/ppermute | solution.py:31
  179.3 5.6 %collective-permute-done.40 = f32[64,1024]{1,0:T(8,128)S(1)} collective-permute-done((f32[64,1024]{1,0:T(8,128)S(1)}, f32[64,1024]{1,0:T(8,128)S(1)}, u32[]{:S(2)}, u32[]{:S(2)}) %collective-permute-start.40) | collective-permute-done | bytes 262176 | tf_op jit(solution)/shard_map/ppermute | solution.py:31
  184.9 5.2 %collective-permute-done.41 = f32[64,1024]{1,0:T(8,128)S(1)} collective-permute-done((f32[64,1024]{1,0:T(8,128)S(1)}, f32[64,1024]{1,0:T(8,128)S(1)}, u32[]{:S(2)}, u32[]{:S(2)}) %collective-permute-start.41) | collective-permute-done | bytes 262176 | tf_op jit(solution)/shard_map/ppermute | solution.py:31
  190.1 2.8 %collective-permute-done.42 = f32[64,1024]{1,0:T(8,128)S(1)} collective-permute-done((f32[64,1024]{1,0:T(8,128)S(1)}, f32[64,1024]{1,0:T(8,128)S(1)}, u32[]{:S(2)}, u32[]{:S(2)}) %collective-permute-start.42) | collective-permute-done | bytes 262176 | tf_op jit(solution)/shard_map/ppermute | solution.py:31
  (177 shorter events, 76.5 us)
Async XLA Ops:
  8.2 11.3 %collective-permute-start.8 = (f32[512,256]{1,0:T(8,128)}, f32[512,256]{1,0:T(8,128)S(1)}, u32[]{:S(2)}, u32[]{:S(2)}) collective-permute-start(f32[512,256]{1,0:T(8,128)} %get-tuple-element.81), channel_id=1, source_target_pairs={{0,1},{1,0},{2,3},{3,2},{4,5},{5,4},{6,7},{7,6},{8,9},{9,8},{10,11... | collective-permute-start | bytes 1572872 | tf_op jit(solution)/shard_map/ppermute | solution.py:31
  18.8 15.1 %collective-permute-start.2 = (f32[512,256]{1,0:T(8,128)}, f32[512,256]{1,0:T(8,128)}, u32[]{:S(2)}, u32[]{:S(2)}) collective-permute-start(f32[512,256]{1,0:T(8,128)} %add.51), channel_id=1, source_target_pairs={{0,2},{1,3},{2,0},{3,1},{4,6},{5,7},{6,4},{7,5},{8,10},{9,11},{10,... | collective-permute-start | bytes 1572872 | tf_op jit(solution)/shard_map/ppermute | solution.py:31
  19.3 19.7 %collective-permute-start.15 = (f32[512,256]{1,0:T(8,128)}, f32[512,256]{1,0:T(8,128)}, u32[]{:S(2)}, u32[]{:S(2)}) collective-permute-start(f32[512,256]{1,0:T(8,128)} %get-tuple-element.94), channel_id=1, source_target_pairs={{0,1},{1,0},{2,3},{3,2},{4,5},{5,4},{6,7},{7,6},{8,9},{9,8},{10,11... | collective-permute-start | bytes 1572872 | tf_op jit(solution)/shard_map/ppermute | solution.py:31
  20.4 24.8 %collective-permute-start.9 = (f32[512,256]{1,0:T(8,128)}, f32[512,256]{1,0:T(8,128)}, u32[]{:S(2)}, u32[]{:S(2)}) collective-permute-start(f32[512,256]{1,0:T(8,128)} %add.52), channel_id=1, source_target_pairs={{0,2},{1,3},{2,0},{3,1},{4,6},{5,7},{6,4},{7,5},{8,10},{9,11},{10,... | collective-permute-start | bytes 1572872 | tf_op jit(solution)/shard_map/ppermute | solution.py:31
  21.9 23.3 %collective-permute-start.7 = (f32[512,256]{1,0:T(8,128)}, f32[512,256]{1,0:T(8,128)}, u32[]{:S(2)}, u32[]{:S(2)}) collective-permute-start(f32[512,256]{1,0:T(8,128)} %get-tuple-element.78), channel_id=1, source_target_pairs={{0,1},{1,0},{2,3},{3,2},{4,5},{5,4},{6,7},{7,6},{8,9},{9,8},{10,11... | collective-permute-start | bytes 1572872 | tf_op jit(solution)/shard_map/ppermute | solution.py:31
  22.8 27.4 %collective-permute-start.22 = (f32[512,256]{1,0:T(8,128)}, f32[512,256]{1,0:T(8,128)}, u32[]{:S(2)}, u32[]{:S(2)}) collective-permute-start(f32[512,256]{1,0:T(8,128)} %get-tuple-element.107), channel_id=1, source_target_pairs={{0,1},{1,0},{2,3},{3,2},{4,5},{5,4},{6,7},{7,6},{8,9},{9,8},{10,11... | collective-permute-start | bytes 1572872 | tf_op jit(solution)/shard_map/ppermute | solution.py:31
  40.2 16.1 %collective-permute-start.16 = (f32[512,256]{1,0:T(8,128)S(1)}, f32[512,256]{1,0:T(8,128)S(1)}, u32[]{:S(2)}, u32[]{:S(2)}) collective-permute-start(f32[512,256]{1,0:T(8,128)S(1)} %add.53), channel_id=1, source_target_pairs={{0,2},{1,3},{2,0},{3,1},{4,6},{5,7},{6,4},{7,5},{8,10},{9,11},{10,... | collective-permute-start | bytes 1572872 | tf_op jit(solution)/shard_map/ppermute | solution.py:31
  40.8 18.1 %collective-permute-start.14 = (f32[512,256]{1,0:T(8,128)S(1)}, f32[512,256]{1,0:T(8,128)S(1)}, u32[]{:S(2)}, u32[]{:S(2)}) collective-permute-start(f32[512,256]{1,0:T(8,128)S(1)} %copy-done.25), channel_id=1, source_target_pairs={{0,1},{1,0},{2,3},{3,2},{4,5},{5,4},{6,7},{7,6},{8,9},{9,8},{10,11... | collective-permute-start | bytes 1572872 | tf_op jit(solution)/shard_map/ppermute | solution.py:31
  45.2 35.4 %collective-permute-start.21 = (f32[512,256]{1,0:T(8,128)S(1)}, f32[512,256]{1,0:T(8,128)S(1)}, u32[]{:S(2)}, u32[]{:S(2)}) collective-permute-start(f32[512,256]{1,0:T(8,128)S(1)} %copy-done.23), channel_id=1, source_target_pairs={{0,1},{1,0},{2,3},{3,2},{4,5},{5,4},{6,7},{7,6},{8,9},{9,8},{10,11... | collective-permute-start | bytes 1572872 | tf_op jit(solution)/shard_map/ppermute | solution.py:31
  47.5 25.6 %collective-permute-start.10 = (f32[256,256]{1,0:T(8,128)S(1)}, f32[256,256]{1,0:T(8,128)S(1)}, u32[]{:S(2)}, u32[]{:S(2)}) collective-permute-start(f32[256,256]{1,0:T(8,128)S(1)} %get-tuple-element.85), channel_id=1, source_target_pairs={{0,16},{4,20},{8,24},{12,28},{16,0},{20,4},{24,8},{28,12},{1,17},{... | collective-permute-start | bytes 786440 | tf_op jit(solution)/shard_map/ppermute | solution.py:31
  51.3 41.6 %collective-permute-start.23 = (f32[512,256]{1,0:T(8,128)S(1)}, f32[512,256]{1,0:T(8,128)S(1)}, u32[]{:S(2)}, u32[]{:S(2)}) collective-permute-start(f32[512,256]{1,0:T(8,128)S(1)} %add.54), channel_id=1, source_target_pairs={{0,2},{1,3},{2,0},{3,1},{4,6},{5,7},{6,4},{7,5},{8,10},{9,11},{10,... | collective-permute-start | bytes 1572872 | tf_op jit(solution)/shard_map/ppermute | solution.py:31
  56.3 22.4 %collective-permute-start.3 = (f32[256,256]{1,0:T(8,128)S(1)}, f32[256,256]{1,0:T(8,128)S(1)}, u32[]{:S(2)}, u32[]{:S(2)}) collective-permute-start(f32[256,256]{1,0:T(8,128)S(1)} %get-tuple-element.72), channel_id=1, source_target_pairs={{0,16},{4,20},{8,24},{12,28},{16,0},{20,4},{24,8},{28,12},{1,17},{... | collective-permute-start | bytes 786440 | tf_op jit(solution)/shard_map/ppermute | solution.py:31
  59.9 28.7 %collective-permute-start.17 = (f32[256,256]{1,0:T(8,128)S(1)}, f32[256,256]{1,0:T(8,128)S(1)}, u32[]{:S(2)}, u32[]{:S(2)}) collective-permute-start(f32[256,256]{1,0:T(8,128)S(1)} %get-tuple-element.98), channel_id=1, source_target_pairs={{0,16},{4,20},{8,24},{12,28},{16,0},{20,4},{24,8},{28,12},{1,17},{... | collective-permute-start | bytes 786440 | tf_op jit(solution)/shard_map/ppermute | solution.py:31
  89.6 16.8 %collective-permute-start.18 = (f32[2,64,256]{2,1,0:T(8,128)S(1)}, f32[2,64,256]{2,1,0:T(8,128)S(1)}, u32[]{:S(2)}, u32[]{:S(2)}) collective-permute-start(f32[2,64,256]{2,1,0:T(8,128)S(1)} %get-tuple-element.100), channel_id=1, source_target_pairs={{0,4},{4,0},{8,12},{12,8},{16,20},{20,16},{24,28},{28,24},{1,5},{5... | collective-permute-start | bytes 393224 | tf_op jit(solution)/shard_map/ppermute | solution.py:31
  90.4 17.8 %collective-permute-start.19 = (f32[2,64,256]{2,1,0:T(8,128)S(1)}, f32[2,64,256]{2,1,0:T(8,128)S(1)}, u32[]{:S(2)}, u32[]{:S(2)}) collective-permute-start(f32[2,64,256]{2,1,0:T(8,128)S(1)} %get-tuple-element.101), channel_id=1, source_target_pairs={{0,8},{4,12},{8,0},{12,4},{16,24},{20,28},{24,16},{28,20},{1,9},{5... | collective-permute-start | bytes 393224 | tf_op jit(solution)/shard_map/ppermute | solution.py:31
  92.9 17.9 %collective-permute-start.20 = (f32[2,64,256]{2,1,0:T(8,128)S(1)}, f32[2,64,256]{2,1,0:T(8,128)S(1)}, u32[]{:S(2)}, u32[]{:S(2)}) collective-permute-start(f32[2,64,256]{2,1,0:T(8,128)S(1)} %get-tuple-element.102), channel_id=1, source_target_pairs={{0,12},{4,8},{8,4},{12,0},{16,28},{20,24},{24,20},{28,16},{1,13},{... | collective-permute-start | bytes 393224 | tf_op jit(solution)/shard_map/ppermute | solution.py:31
  101.0 10.6 %collective-permute-start.26 = (f32[64,256]{1,0:T(8,128)S(1)}, f32[64,256]{1,0:T(8,128)S(1)}, u32[]{:S(2)}, u32[]{:S(2)}) collective-permute-start(f32[64,256]{1,0:T(8,128)S(1)} %get-tuple-element.113), channel_id=1, source_target_pairs={{0,12},{4,8},{8,4},{12,0},{16,28},{20,24},{24,20},{28,16},{1,13},{... | collective-permute-start | bytes 196616 | tf_op jit(solution)/shard_map/ppermute | solution.py:31
  142.5 11.3 %collective-permute-start.36 = (f32[64,1024]{1,0:T(8,128)}, f32[64,1024]{1,0:T(8,128)}, u32[]{:S(2)}, u32[]{:S(2)}) collective-permute-start(f32[64,1024]{1,0:T(8,128)} %get-tuple-element.120), channel_id=1, source_target_pairs={{0,4},{4,0},{8,12},{12,8},{16,20},{20,16},{24,28},{28,24},{1,5},{5... | collective-permute-start | bytes 786440 | tf_op jit(solution)/shard_map/ppermute | solution.py:31
  147.7 11.2 %collective-permute-start.37 = (f32[64,1024]{1,0:T(8,128)S(1)}, f32[64,1024]{1,0:T(8,128)S(1)}, u32[]{:S(2)}, u32[]{:S(2)}) collective-permute-start(f32[64,1024]{1,0:T(8,128)S(1)} %copy-done.33), channel_id=1, source_target_pairs={{0,8},{4,12},{8,0},{12,4},{16,24},{20,28},{24,16},{28,20},{1,9},{5... | collective-permute-start | bytes 786440 | tf_op jit(solution)/shard_map/ppermute | solution.py:31
  147.9 15.5 %collective-permute-start.38 = (f32[64,1024]{1,0:T(8,128)S(1)}, f32[64,1024]{1,0:T(8,128)S(1)}, u32[]{:S(2)}, u32[]{:S(2)}) collective-permute-start(f32[64,1024]{1,0:T(8,128)S(1)} %copy-done.31), channel_id=1, source_target_pairs={{0,12},{4,8},{8,4},{12,0},{16,28},{20,24},{24,20},{28,16},{1,13},{... | collective-permute-start | bytes 786440 | tf_op jit(solution)/shard_map/ppermute | solution.py:31
  150.6 28.6 %collective-permute-start.39 = (f32[64,1024]{1,0:T(8,128)S(1)}, f32[64,1024]{1,0:T(8,128)S(1)}, u32[]{:S(2)}, u32[]{:S(2)}) collective-permute-start(f32[64,1024]{1,0:T(8,128)S(1)} %copy-done.29), channel_id=1, source_target_pairs={{0,16},{4,20},{8,24},{12,28},{16,0},{20,4},{24,8},{28,12},{1,17},{... | collective-permute-start | bytes 786440 | tf_op jit(solution)/shard_map/ppermute | solution.py:31
  151.2 33.7 %collective-permute-start.40 = (f32[64,1024]{1,0:T(8,128)S(1)}, f32[64,1024]{1,0:T(8,128)S(1)}, u32[]{:S(2)}, u32[]{:S(2)}) collective-permute-start(f32[64,1024]{1,0:T(8,128)S(1)} %copy-done.27), channel_id=1, source_target_pairs={{0,20},{4,16},{8,28},{12,24},{16,4},{20,0},{24,12},{28,8},{1,21},{... | collective-permute-start | bytes 786440 | tf_op jit(solution)/shard_map/ppermute | solution.py:31
  153.8 36.3 %collective-permute-start.41 = (f32[64,1024]{1,0:T(8,128)S(1)}, f32[64,1024]{1,0:T(8,128)S(1)}, u32[]{:S(2)}, u32[]{:S(2)}) collective-permute-start(f32[64,1024]{1,0:T(8,128)S(1)} %get-tuple-element.125), channel_id=1, source_target_pairs={{0,24},{4,28},{8,16},{12,20},{16,8},{20,12},{24,0},{28,4},{1,25},{... | collective-permute-start | bytes 786440 | tf_op jit(solution)/shard_map/ppermute | solution.py:31
  158.9 34.0 %collective-permute-start.42 = (f32[64,1024]{1,0:T(8,128)S(1)}, f32[64,1024]{1,0:T(8,128)S(1)}, u32[]{:S(2)}, u32[]{:S(2)}) collective-permute-start(f32[64,1024]{1,0:T(8,128)S(1)} %get-tuple-element.126), channel_id=1, source_target_pairs={{0,28},{4,24},{8,20},{12,16},{16,12},{20,8},{24,4},{28,0},{1,29},{... | collective-permute-start | bytes 786440 | tf_op jit(solution)/shard_map/ppermute | solution.py:31
  (58 other events, 387.9 us)

commit v4 on v3

--- a/solution.py
+++ b/solution.py
@@ -20,6 +20,8 @@
 STARTS = tuple(sum(CHUNKS[:k]) for k in range(len(CHUNKS)))
 COUNT = len(CHUNKS)
 EARLY = 2
+BITS = (-1, 0, 0, 0)
+SHARED = 3
 
 
 SMEM = pl.BlockSpec(memory_space=pltpu.SMEM)
@@ -89,7 +91,7 @@
             in_specs=[SMEM, VMEM, VMEM],
             out_specs=[VMEM] * len(outs),
             out_shape=outs,
-            compiler_params=pltpu.CompilerParams(vmem_limit_bytes=24 << 20),
+            compiler_params=pltpu.CompilerParams(vmem_limit_bytes=54 << 20),
             name="second",
         )(at, features[0], upstream[0])
         return list(outs[:COUNT]), list(outs[COUNT:])
@@ -107,106 +109,106 @@
             pltpu.VMEM(upstream.shape[1:], upstream.dtype),
             pltpu.SemaphoreType.DMA((2 * len(cuts),)),
         ],
-        compiler_params=pltpu.CompilerParams(vmem_limit_bytes=60 << 20),
+        compiler_params=pltpu.CompilerParams(vmem_limit_bytes=59 << 20),
         name="first",
     )(at, features, upstream)
     return list(outs[:COUNT]), list(outs[COUNT:])
 
 
-def velocity_kernel(gradient_ref, momentum_ref, *rest):
-    rest[-1][...] = 0.5 * momentum_ref[...] + gradient_ref[...]
+def velocity_kernel(cut, gradient_ref, momentum_ref, *rest):
+    out_ref, scratch_ref, sem = rest[-3:]
+    scratch_ref[...] = 0.5 * momentum_ref[:, cut] + gradient_ref[...]
+    copy = pltpu.make_async_copy(scratch_ref, out_ref.at[:, cut], sem)
+    copy.start()
+    copy.wait()
 
 
 def velocity_chunk(gradient, momentum, velocity, k):
-    rows, width = gradient.shape
-    narrow = pl.BlockSpec((rows, width), lambda i: (0, 0))
-    wide = pl.BlockSpec((rows, width), lambda i: (0, STARTS[k] // width))
-    args, specs, alias = [gradient, momentum], [narrow, wide], {}
-    if velocity is not None:
-        args.append(velocity)
-        specs.append(pl.BlockSpec(memory_space=pl.ANY))
-        alias = {2: 0}
-    return pl.pallas_call(
-        velocity_kernel,
-        grid=(1,),
-        in_specs=specs,
-        out_specs=wide,
+    hbm = pl.BlockSpec(memory_space=pl.ANY)
+    cut = slice(STARTS[k], STARTS[k] + CHUNKS[k])
+    more = () if velocity is None else (velocity,)
+    return pl.pallas_call(
+        functools.partial(velocity_kernel, cut),
+        in_specs=[VMEM, VMEM] + [hbm] * len(more),
+        out_specs=hbm,
         out_shape=jax.ShapeDtypeStruct(momentum.shape, jnp.float32),
-        input_output_aliases=alias,
+        scratch_shapes=[pltpu.VMEM(gradient.shape, jnp.float32), pltpu.SemaphoreType.DMA],
+        input_output_aliases={2: 0} if more else {},
         compiler_params=pltpu.CompilerParams(vmem_limit_bytes=8 << 20),
         name="velocity",
-    )(*args)
-
-
-def update_kernel(k, count, grouped, me_ref, *rest):
-    terms, (momentum_ref, weights_ref, gradient_ref, *outs) = rest[:count], rest[count:]
-    me = me_ref[0]
-    rows = gradient_ref.shape[0]
+    )(gradient, momentum, *more)
+
+
+def without(value, bit):
+    return (value >> (bit + 1)) << bit | value & ((1 << bit) - 1)
+
+
+def spread_bits(value, bit):
+    return (value >> bit) << (bit + 1) | value & ((1 << bit) - 1)
+
+
+def update_kernel(k, count, bit, me_ref, *rest):
+    terms, (momentum_ref, weights_ref, gradient_ref, keep_ref, send_ref) = rest[:count], rest[count:]
     cut = slice(STARTS[k], STARTS[k] + CHUNKS[k])
     gradient = terms[0][...]
     for term in terms[1:]:
         gradient = gradient + term[...]
     gradient_ref[...] = gradient
     current = weights_ref[:, cut] - LEARNING_RATE * (0.5 * momentum_ref[:, cut] + gradient)
-    size = outs[0].shape[0]
-    parts = rows // size
-    for place in range(parts):
-        if grouped:
-            for mask, out in enumerate(outs):
-
-                @pl.when((me >= grouped) == ((place ^ mask) == 1))
-                def _(out=out, place=place):
-                    out[...] = current[place * size : (place + 1) * size]
-
-        else:
-            for mask, out in enumerate(outs):
-
-                @pl.when((me ^ mask) == place)
-                def _(out=out, place=place):
-                    out[...] = current[place * size : (place + 1) * size]
-
-
-def update(me, terms, momentum, weights, k, group, grouped):
+    side = (me_ref[0] >> bit) & 1
+    slots, size, _ = keep_ref.shape
+    for worker in range(2 * slots):
+        piece = current[worker * size : (worker + 1) * size]
+        for out, mine in ((keep_ref, worker >> bit & 1), (send_ref, 1 - (worker >> bit & 1))):
+
+            @pl.when(side == mine)
+            def _(out=out, piece=piece, slot=without(worker, bit)):
+                out[slot] = piece
+
+
+def update(me, terms, momentum, weights, k, workers, bit):
     rows = terms[0].shape[0]
-    parts = 2 if grouped else 2 * group
     full = jax.ShapeDtypeStruct(terms[0].shape, jnp.float32)
-    cut = jax.ShapeDtypeStruct((rows // parts, CHUNKS[k]), jnp.float32)
-    gradient, *outs = pl.pallas_call(
-        functools.partial(update_kernel, k, len(terms), group if grouped else 0),
+    part = jax.ShapeDtypeStruct((workers // 2, rows // workers, CHUNKS[k]), jnp.float32)
+    return pl.pallas_call(
+        functools.partial(update_kernel, k, len(terms), bit),
         in_specs=[SMEM] + [VMEM] * (len(terms) + 2),
-        out_specs=[VMEM] * (1 + parts),
-        out_shape=[full] + [cut] * parts,
+        out_specs=[VMEM] * 3,
+        out_shape=[full, part, part],
         compiler_params=pltpu.CompilerParams(vmem_limit_bytes=8 << 20),
         name="update",
     )(me, *terms, momentum, weights)
-    return gradient, outs
-
-
-def regroup_kernel(group, me_ref, keep_ref, got_ref, *outs):
-    rank = me_ref[0] % group
-    size = outs[0].shape[1]
-    for mask, out in enumerate(outs):
-        cut = pl.ds(pl.multiple_of((rank ^ mask) * size, 8), size)
-        out[0] = keep_ref[cut, :]
-        out[1] = got_ref[cut, :]
-
-
-def regroup(me, keep, got, group):
-    rows, width = keep.shape
-    return pl.pallas_call(
-        functools.partial(regroup_kernel, group),
-        in_specs=[SMEM, VMEM, VMEM],
+
+
+def regroup_kernel(bit, turn, me_ref, *rest):
+    group = rest[0].shape[0]
+    parts, outs = rest[:-group], rest[-group:]
+    rank = without(me_ref[0], bit) ^ turn
+    for i, out in enumerate(outs):
+        start = 0
+        for place in range(0, len(parts), 2):
+            width = parts[place].shape[2]
+            for side in range(2):
+                out[side, :, start : start + width] = parts[place + side][rank ^ i]
+            start += width
+
+
+def regroup(me, parts, bit, turn=0):
+    group, rows, _ = parts[0].shape
+    width = sum(part.shape[2] for part in parts[::2])
+    return pl.pallas_call(
+        functools.partial(regroup_kernel, bit, turn),
+        in_specs=[SMEM] + [VMEM] * len(parts),
         out_specs=[VMEM] * group,
-        out_shape=[jax.ShapeDtypeStruct((2, rows // group, width), jnp.float32)] * group,
+        out_shape=[jax.ShapeDtypeStruct((2, rows, width), jnp.float32)] * group,
         compiler_params=pltpu.CompilerParams(vmem_limit_bytes=8 << 20),
         name="regroup",
-    )(me, keep, got)
-
-
-def pieces_of(refs, cut):
-    if len(refs[0].shape) == 2:
-        return [ref[:, cut] for ref in refs]
-    return [ref[half, :, cut] for half in range(2) for ref in refs]
+    )(me, *parts)
+
+
+def pieces_of(refs, bit, cut):
+    masks = range(2 * len(refs))
+    return [refs[without(mask, bit)][mask >> bit & 1, :, cut] for mask in masks]
 
 
 def gap_row(left, right):
@@ -214,23 +216,23 @@
     return jnp.sum(gap * gap, axis=0, keepdims=True)
 
 
-def add_squares(refs, h_of, rows, sums_ref):
+def add_squares(refs, bit, h_of, rows, sums_ref):
     for lane, h in enumerate(h_of):
-        old = pieces_of(refs, slice(lane * LANES, (lane + 1) * LANES))
+        old = pieces_of(refs, bit, slice(lane * LANES, (lane + 1) * LANES))
         for place, (a, b) in enumerate(pair_list(len(old))):
             at = slice(h * rows + place, h * rows + place + 1)
             sums_ref[at, :] = sums_ref[at, :] + gap_row(old[a], old[b])
 
 
-def squares_kernel(h_of, *rest):
+def squares_kernel(bit, h_of, *rest):
     refs, sums_ref = rest[:-1], rest[-1]
     sums_ref[...] = jnp.zeros_like(sums_ref)
-    add_squares(refs, h_of, sums_ref.shape[0] // 2, sums_ref)
-
-
-def squares(pieces, workers, h_of):
-    return pl.pallas_call(
-        functools.partial(squares_kernel, h_of),
+    add_squares(refs, bit, h_of, sums_ref.shape[0] // 2, sums_ref)
+
+
+def squares(pieces, workers, bit, h_of):
+    return pl.pallas_call(
+        functools.partial(squares_kernel, bit, h_of),
         in_specs=[VMEM] * len(pieces),
         out_specs=VMEM,
         out_shape=jax.ShapeDtypeStruct((2 * pair_rows(workers), LANES), jnp.float32),
@@ -244,7 +246,7 @@
     return lax.dot_general(ones, sums, (((1,), (1,)), ((), ())), precision=HIGH, preferred_element_type=jnp.float32)
 
 
-def pack_kernel(workers, tokens, parts, h_of, me_ref, mix_ref, *rest):
+def pack_kernel(workers, tokens, parts, bit, h_of, me_ref, mix_ref, *rest):
     rows = pair_rows(workers)
     sums, refs = rest[:parts], rest[parts:-3]
     packed_ref, table_ref, total_ref = rest[-3:]
@@ -253,7 +255,7 @@
     for part in sums[1:]:
         total = total + part[...]
     total_ref[...] = total
-    add_squares(refs, h_of, rows, total_ref)
+    add_squares(refs, bit, h_of, rows, total_ref)
     packed_ref[...] = jnp.zeros_like(packed_ref)
     for h in range(2):
         for place, (a, b) in enumerate(pair_list(workers)):
@@ -272,9 +274,9 @@
     packed_ref[2:3, :] = row
 
 
-def pack(sums, pieces, mix_weights, me, workers, tokens, h_of):
-    return pl.pallas_call(
-        functools.partial(pack_kernel, workers, tokens, len(sums), h_of),
+def pack(sums, pieces, mix_weights, me, workers, tokens, bit, h_of):
+    return pl.pallas_call(
+        functools.partial(pack_kernel, workers, tokens, len(sums), bit, h_of),
         in_specs=[SMEM, SMEM] + [VMEM] * (len(sums) + len(pieces)),
         out_specs=VMEM,
         out_shape=jax.ShapeDtypeStruct((8, LANES), jnp.float32),
@@ -349,45 +351,65 @@
             matrix_ref[at : at + workers, :] = total[w]
 
 
-def mix_kernel(workers, half, counts, masks, first, me_ref, *rest):
+def mix_kernel(workers, half, layout, masks, first, me_ref, *rest):
     if first:
         clip_ref, packed_ref, select_ref, *rest = rest
         matrix_ref, *rest = rest[-1:] + rest[:-1]
         fill_matrices(workers, clip_ref, packed_ref, select_ref, matrix_ref)
     else:
         matrix_ref, *rest = rest
-    chunks = []
-    for count in counts:
-        chunks.append(rest[:count])
-        rest = rest[count:]
     me = me_ref[0]
-    for k, refs in enumerate(chunks):
-        for lane in range(CHUNKS[k] // LANES):
-            start = STARTS[k] + lane * LANES
-            base = start // half * workers * workers
-            old = pieces_of(refs, slice(lane * LANES, (lane + 1) * LANES))
-            for mask, out in zip(masks, rest):
+    for bit, start, into in layout:
+        refs, rest = rest[: workers // 2], rest[workers // 2 :]
+        for lane in range(0, refs[0].shape[2], LANES):
+            base = (start + lane) // half * workers * workers
+            old = pieces_of(refs, bit, slice(lane, lane + LANES))
+            for mask, out in zip(masks, rest[-len(masks) :]):
                 value = None
                 for other, rows in enumerate(old):
                     share = matrix_ref[pl.ds(base + (me ^ mask) * workers + (me ^ other), 1), :]
                     value = share * rows if value is None else value + share * rows
-                out[:, start : start + LANES] = value
-
-
-def mix(masks, me, matrix, clip_radius, packed, chunks, workers, rows, width):
+                out[:, into + lane : into + lane + LANES] = value
+
+
+def mix(masks, me, matrix, head, chunks, layout, workers, half):
     first = matrix is None
+    rows = chunks[0][0].shape[1]
+    width = sum(chunk[0].shape[2] for chunk in chunks)
     table = jax.ShapeDtypeStruct((2 * workers * workers, LANES), jnp.float32)
-    piece = jax.ShapeDtypeStruct((rows, width), jnp.float32)
-    head = (clip_radius, packed, selectors(workers)) if first else (matrix,)
-    counts = [len(chunk) for chunk in chunks]
-    return pl.pallas_call(
-        functools.partial(mix_kernel, workers, width // 2, counts, masks, first),
-        in_specs=[SMEM] + ([SMEM] if first else []) + [VMEM] * (len(head) - first + sum(counts)),
+    head = (*head, selectors(workers)) if first else (matrix,)
+    return pl.pallas_call(
+        functools.partial(mix_kernel, workers, half, layout, masks, first),
+        in_specs=[SMEM] * (1 + first) + [VMEM] * (len(head) - first + sum(len(chunk) for chunk in chunks)),
         out_specs=[VMEM] * (len(masks) + first),
-        out_shape=[piece] * len(masks) + [table] * first,
+        out_shape=[jax.ShapeDtypeStruct((rows, width), jnp.float32)] * len(masks) + [table] * first,
         compiler_params=pltpu.CompilerParams(vmem_limit_bytes=16 << 20),
         name="mix",
     )(me, *head, *[piece for chunk in chunks for piece in chunk])
+
+
+def place_kernel(spots, me_ref, *rest):
+    pieces, out_ref, sems = rest[:-2], rest[-2], rest[-1]
+    copies = []
+    for i, (mask, start) in enumerate(spots):
+        rows, width = pieces[i].shape
+        at = pl.ds(pl.multiple_of((me_ref[0] ^ mask) * rows, 8), rows)
+        copies.append(pltpu.make_async_copy(pieces[i], out_ref.at[at, start : start + width], sems.at[i]))
+        copies[i].start()
+    for copy in copies:
+        copy.wait()
+
+
+def place(me, pieces, spots, rows, width):
+    return pl.pallas_call(
+        functools.partial(place_kernel, spots),
+        in_specs=[SMEM] + [pl.BlockSpec(memory_space=pl.ANY)] * len(pieces),
+        out_specs=pl.BlockSpec(memory_space=pl.ANY),
+        out_shape=jax.ShapeDtypeStruct((rows, width), jnp.float32),
+        scratch_shapes=[pltpu.SemaphoreType.DMA((len(pieces),))],
+        compiler_params=pltpu.CompilerParams(vmem_limit_bytes=4 << 20),
+        name="place",
+    )(me, *pieces)
 
 
 def per_device(inputs, cotangent, weights, momentum, mix_weights, clip_radius):
@@ -397,7 +419,6 @@
     tok, me = lax.axis_index("tok"), lax.axis_index("worker")
     here = me.reshape(1)
     rows, width = weights.shape[1:]
-    piece = rows // workers
     half = width // 2
     h_of = [tuple((start + lane) // half for lane in range(0, size, LANES)) for start, size in zip(STARTS, CHUNKS)]
     levels = tokens.bit_length() - 1
@@ -433,45 +454,59 @@
         aways.append(moved)
     extras = [arrived(0, levels - 1, k) for k in range(COUNT)]
     velocity, chunks, sums = None, [], []
+    bits = [bit % (workers.bit_length() - 1) for bit in BITS]
+    held = []
     for k in range(COUNT):
-        grouped = k < COUNT - 1
         away = after(aways[k], gradient) if k else aways[k]
         terms = [leaves[0][k], *extras[k], away]
-        gradient, outs = update(here, terms, momentum[0], weights[0], k, group, grouped)
-        if grouped:
-            got = flip(outs[1], "worker", group)
-            pieces = list(regroup(here, outs[0], got, group))
-            for mask in range(1, group):
-                pieces[mask] = flip(pieces[mask], "worker", mask)
-            sums.append(squares(pieces, workers, h_of[k]))
-        else:
-            pieces = list(outs)
-            for mask in [*range(group, workers), *range(1, group)]:
-                pieces[mask] = flip(pieces[mask], "worker", mask)
+        gradient, keep, send = update(here, terms, momentum[0], weights[0], k, workers, bits[k])
+        got = flip(send, "worker", 1 << bits[k])
+        pieces = list(regroup(here, (keep, got), bits[k]))
+        if k >= SHARED:
+            held += [keep, got]
+        for i in reversed(range(1, group)):
+            pieces[i] = flip(pieces[i], "worker", spread_bits(i, bits[k]))
         chunks.append(pieces)
-        if len(aways) < COUNT:
+        if k < COUNT - 1:
+            sums.append(squares(pieces, workers, bits[k], h_of[k]))
+        if k == 0:
             moved, _ = send_terms(len(aways), gradient)
             aways.append(moved)
         velocity = velocity_chunk(gradient, momentum[0], velocity, k)
-    packed = pack(sums, chunks[-1], mix_weights, here, workers, tokens, h_of[-1])
+        if 0 < k and len(aways) < COUNT:
+            moved, _ = send_terms(len(aways), velocity)
+            aways.append(moved)
+    packed = pack(sums, chunks[-1], mix_weights, here, workers, tokens, bits[-1], h_of[-1])
+    bit = bits[SHARED]
+    mirror = list(regroup(here, held, bit, without(group, bit)))
+    later = [*range(group // 2, group), *range(1, group // 2)]
     for axis, size in (("tok", tokens), ("worker", workers)):
         mask = 1
         while mask < size:
             packed = packed + flip(packed, axis, mask)
+            if later:
+                i = later.pop(0)
+                mirror[i] = flip(after(mirror[i], packed), "worker", spread_bits(i, bit))
             mask *= 2
-    news = {}
-    far = tuple(range(group, workers))
-    *pieces, matrix = mix(far, here, None, clip_radius, packed, chunks, workers, piece, width)
-    for mask, value in zip(far, pieces):
-        news[mask] = flip(value, "worker", mask)
-    near = tuple(range(group))
-    pieces = mix(near, here, matrix, clip_radius, packed, chunks, workers, piece, width)
-    news[0] = pieces[0]
-    for mask in near[1:]:
-        news[mask] = flip(pieces[mask], "worker", mask)
-    new = jnp.zeros((rows, width), jnp.float32)
-    for mask in [*near, *far]:
-        new = lax.dynamic_update_slice_in_dim(new, news[mask], (me ^ mask) * piece, 0)
+    for i in later:
+        mirror[i] = flip(mirror[i], "worker", spread_bits(i, bit))
+    split = STARTS[SHARED]
+    layout = tuple((bit, start, start) for bit, start in zip(bits, STARTS))
+    near, far = tuple(range(group)), tuple(range(group, workers))
+    pieces, spots = [], []
+    *out, matrix = mix(far, here, None, (clip_radius, packed), chunks[:SHARED], layout[:SHARED], workers, half)
+    for mask, value in zip(far, out):
+        pieces.append(flip(value, "worker", mask))
+        spots.append((mask, 0))
+    out = mix(near, here, matrix, (), chunks, layout, workers, half)
+    for mask, value in zip(near, out):
+        pieces.append(flip(value, "worker", mask) if mask else value)
+        spots.append((mask, 0))
+    out = mix(near, here, matrix, (), [mirror], ((bit, split, 0),), workers, half)
+    for mask, value in zip(near, out):
+        pieces.append(flip(value, "worker", mask) if mask else value)
+        spots.append((mask ^ group, split))
+    new = place(here, pieces, tuple(spots), rows, width)
     return new[None], velocity[None]
 
 

time: 195 us -> 182 us (0.933)
  the two profiles are of different devices: /device:TPU:12 before, /device:TPU:0 now
where the time goes in v4:
time: 182 us
  waiting for transfers between devices  81.4 us (45%)
  starting transfers between devices  63.1 us (35%)
  Pallas kernels  28.2 us (15%)
  other arithmetic  4.02 us (2%)
  local copies, waits for them, and re-layouts  3.76 us (2%)
    ppermute x46, waiting for transfers between devices, flip(): return lax.ppermute(value, axis, pairs)  81.4 us
    ppermute x46, starting transfers between devices, flip(): return lax.ppermute(value, axis, pairs)  63.1 us
    pallas_call x1, Pallas kernels, multiply(): pl.pallas_call(functools.partial(second_kernel, rows), in_specs=[SMEM, VM...  8.21 us
    pallas_call x1, Pallas kernels, multiply(): pl.pallas_call(functools.partial(first_kernel, rows, cuts), in_specs=[SME...  7.31 us
    add x4, other arithmetic, reduced(): return sum(arrived(offset, level, k), leaves[offset][k])  4.01 us
    unnamed x34, local copies, waits for them, and re-layouts  3.76 us
  transfers between devices with their start and end apart: 46, of which 18 were waited for; matrix products, arithmetic and copies ran while one was open for 2% of the time, Pallas kernels for 10%

profile of v4, /device:TPU:0, one launch (start us, length us, event | category | flops | bytes accessed | tf_op | source)
XLA Modules:
  0.0 181.7 jit_solution(637616197506521822)
XLA Ops:
  0.6 7.3 %first.1 = (f32[512,256]{1,0:T(8,128)}, f32[512,256]{1,0:T(8,128)}, f32[512,256]{1,0:T(8,128)}, f32[512,256]{1,0:T(8,128)}, f32[512,256]{1,0:T(8,128)}, /*index=...) custom-call(s32[1]{0:T(128)} %bitcast.2.at_ref, bf16[1,1536,2048]{2,1,0:T(8,128)(2,1)} %features_hbm.1, ...), custom_call_target="tpu_custom_call" | custom-call | tf_op jit(solution)/shard_map/first/pallas_call | solution.py:102
  8.6 8.2 %second.1 = (f32[512,256]{1,0:T(8,128)}, f32[512,256]{1,0:T(8,128)}, f32[512,256]{1,0:T(8,128)}, f32[512,256]{1,0:T(8,128)}, f32[512,256]{1,0:T(8,128)}, /*index...) custom-call(s32[1]{0:T(128)} %bitcast.1.at_ref, bf16[1536,2048]{1,0:T(8,128)(2,1)} %bitcast.22, ...), custom_call_target="tpu_custom_call" | custom-call | tf_op jit(solution)/shard_map/second/pallas_call | solution.py:89
  18.2 2.6 %collective-permute-start.2 = (f32[512,256]{1,0:T(8,128)}, f32[512,256]{1,0:T(8,128)}, u32[]{:S(2)}, u32[]{:S(2)}) collective-permute-start(f32[512,256]{1,0:T(8,128)} %add.27), channel_id=1, source_target_pairs={{0,2},{1,3},{2,0},{3,1},{4,6},{5,7},{6,4},{7,5},{8,10},{9,11},{10,... | collective-permute-start | bytes 1572872 | tf_op jit(solution)/shard_map/ppermute | solution.py:33
  23.1 10.7 %collective-permute-done.2.rest_2_ = f32[512,256]{1,0:T(8,128)} collective-permute-done((f32[512,256]{1,0:T(8,128)}, f32[512,256]{1,0:T(8,128)}, u32[]{:S(2)}, u32[]{:S(2)}) %collective-permute-start.2) | collective-permute-done | bytes 524320 | tf_op jit(solution)/shard_map/ppermute | solution.py:33
  38.7 6.0 %collective-permute-done.9.rest_2_ = f32[512,256]{1,0:T(8,128)S(1)} collective-permute-done((f32[512,256]{1,0:T(8,128)}, f32[512,256]{1,0:T(8,128)S(1)}, u32[]{:S(2)}, u32[]{:S(2)}) %collective-permute-start.9) | collective-permute-done | bytes 524320 | tf_op jit(solution)/shard_map/ppermute | solution.py:33
  51.6 2.8 %collective-permute-start.3 = (f32[4,64,256]{2,1,0:T(8,128)S(1)}, f32[4,64,256]{2,1,0:T(8,128)S(1)}, u32[]{:S(2)}, u32[]{:S(2)}) collective-permute-start(f32[4,64,256]{2,1,0:T(8,128)S(1)} %get-tuple-element.81), channel_id=1, source_target_pairs={{0,16},{4,20},{8,24},{12,28},{16,0},{20,4},{24,8},{28,12},{1,17},{... | collective-permute-start | bytes 786440 | tf_op jit(solution)/shard_map/ppermute | solution.py:33
  54.4 6.3 %collective-permute-done.16.rest_2_ = f32[512,256]{1,0:T(8,128)S(1)} collective-permute-done((f32[512,256]{1,0:T(8,128)S(1)}, f32[512,256]{1,0:T(8,128)S(1)}, u32[]{:S(2)}, u32[]{:S(2)}) %collective-permute-start.16) | collective-permute-done | bytes 524320 | tf_op jit(solution)/shard_map/ppermute | solution.py:33
  63.0 7.8 %collective-permute-done.23.rest_2_ = f32[512,256]{1,0:T(8,128)S(1)} collective-permute-done((f32[512,256]{1,0:T(8,128)S(1)}, f32[512,256]{1,0:T(8,128)S(1)}, u32[]{:S(2)}, u32[]{:S(2)}) %collective-permute-start.23) | collective-permute-done | bytes 524320 | tf_op jit(solution)/shard_map/ppermute | solution.py:33
  78.1 6.1 %collective-permute-done.4.rest_1_.rest_4_.rest_2_ = f32[2,64,256]{2,1,0:T(8,128)S(1)} collective-permute-done((f32[2,64,256]{2,1,0:T(8,128)S(1)}, f32[2,64,256]{2,1,0:T(8,128)S(1)}, u32[]{:S(2)}, u32[]{:S(2)}) %collective-permute-start.4) | collective-permute-done | bytes 131104 | tf_op jit(solution)/shard_map/ppermute | solution.py:33
  84.2 2.2 %collective-permute-start.12 = (f32[2,64,256]{2,1,0:T(8,128)S(1)}, f32[2,64,256]{2,1,0:T(8,128)S(1)}, u32[]{:S(2)}, u32[]{:S(2)}) collective-permute-start(f32[2,64,256]{2,1,0:T(8,128)S(1)} %get-tuple-element.97), channel_id=1, source_target_pairs={{0,16},{4,20},{8,24},{12,28},{16,0},{20,4},{24,8},{28,12},{1,17},{... | collective-permute-start | bytes 393224 | tf_op jit(solution)/shard_map/ppermute | solution.py:33
  88.1 2.8 %collective-permute-start.19 = (f32[2,64,256]{2,1,0:T(8,128)S(1)}, f32[2,64,256]{2,1,0:T(8,128)S(1)}, u32[]{:S(2)}, u32[]{:S(2)}) collective-permute-start(f32[2,64,256]{2,1,0:T(8,128)S(1)} %get-tuple-element.110), channel_id=1, source_target_pairs={{0,16},{4,20},{8,24},{12,28},{16,0},{20,4},{24,8},{28,12},{1,17},{... | collective-permute-start | bytes 393224 | tf_op jit(solution)/shard_map/ppermute | solution.py:33
  92.3 4.8 %collective-permute-done.12.rest_2_.rest_9_.rest_7_ = f32[2,64,256]{2,1,0:T(8,128)S(1)} collective-permute-done((f32[2,64,256]{2,1,0:T(8,128)S(1)}, f32[2,64,256]{2,1,0:T(8,128)S(1)}, u32[]{:S(2)}, u32[]{:S(2)}) %collective-permute-start.12) | collective-permute-done | bytes 131104 | tf_op jit(solution)/shard_map/ppermute | solution.py:33
  97.3 10.3 %collective-permute-start.26 = (f32[2,64,256]{2,1,0:T(8,128)S(1)}, f32[2,64,256]{2,1,0:T(8,128)S(1)}, u32[]{:S(2)}, u32[]{:S(2)}) collective-permute-start(f32[2,64,256]{2,1,0:T(8,128)S(1)} %get-tuple-element.123), channel_id=1, source_target_pairs={{0,16},{4,20},{8,24},{12,28},{16,0},{20,4},{24,8},{28,12},{1,17},{... | collective-permute-start | bytes 393224 | tf_op jit(solution)/shard_map/ppermute | solution.py:33
  109.2 7.6 %collective-permute-done.26.rest_5_.rest_15_ = f32[2,64,256]{2,1,0:T(8,128)S(1)} collective-permute-done((f32[2,64,256]{2,1,0:T(8,128)S(1)}, f32[2,64,256]{2,1,0:T(8,128)S(1)}, u32[]{:S(2)}, u32[]{:S(2)}) %collective-permute-start.26) | collective-permute-done | bytes 131104 | tf_op jit(solution)/shard_map/ppermute | solution.py:33
  120.1 2.4 %collective-permute-done.29 = f32[8,128]{1,0:T(8,128)S(1)} collective-permute-done((f32[8,128]{1,0:T(8,128)S(1)}, f32[8,128]{1,0:T(8,128)S(1)}, u32[]{:S(2)}, u32[]{:S(2)}) %collective-permute-start.29) | collective-permute-done | bytes 4128 | tf_op jit(solution)/shard_map/ppermute | solution.py:33
  124.4 3.6 %collective-permute-start.41 = (f32[2,64,256]{2,1,0:T(8,128)S(1)}, f32[2,64,256]{2,1,0:T(8,128)S(1)}, u32[]{:S(2)}, u32[]{:S(2)}) collective-permute-start(f32[2,64,256]{2,1,0:T(8,128)S(1)} %get-tuple-element.138), channel_id=1, source_target_pairs={{0,16},{4,20},{8,24},{12,28},{16,0},{20,4},{24,8},{28,12},{1,17},{... | collective-permute-start | bytes 393224 | tf_op jit(solution)/shard_map/ppermute | solution.py:33
  130.8 6.6 %collective-permute-done.31 = f32[8,128]{1,0:T(8,128)S(1)} collective-permute-done((f32[8,128]{1,0:T(8,128)S(1)}, f32[8,128]{1,0:T(8,128)S(1)}, u32[]{:S(2)}, u32[]{:S(2)}) %collective-permute-start.31) | collective-permute-done | bytes 4128 | tf_op jit(solution)/shard_map/ppermute | solution.py:33
  138.1 3.9 %collective-permute-done.32 = f32[8,128]{1,0:T(8,128)S(1)} collective-permute-done((f32[8,128]{1,0:T(8,128)S(1)}, f32[8,128]{1,0:T(8,128)S(1)}, u32[]{:S(2)}, u32[]{:S(2)}) %collective-permute-start.32) | collective-permute-done | bytes 4128 | tf_op jit(solution)/shard_map/ppermute | solution.py:33
  142.0 2.1 %mix.3 = (f32[64,768]{1,0:T(8,128)S(1)}, f32[64,768]{1,0:T(8,128)S(1)}, f32[64,768]{1,0:T(8,128)S(1)}, f32[64,768]{1,0:T(8,128)S(1)}, f32[128,128]{1,0:T(8,128)S(1)}) custom-call(s32[1]{0:T(128)} %bitcast.me_ref, s32[2]{0:T(128)S(1)} %copy-done.11, f32[8,128]{1,0:T(8,128)S(1)} %add.35.rest_1_, f32[320,128]{1,0:T(8,128)S(1)} %copy-done.9, ...), custom_call_target="tpu_custom_call" | custom-call | tf_op jit(solution)/shard_map/mix/pallas_call | solution.py:381
  154.5 2.4 %collective-permute-start.38 = (f32[64,1024]{1,0:T(8,128)S(1)}, f32[64,1024]{1,0:T(8,128)S(1)}, u32[]{:S(2)}, u32[]{:S(2)}) collective-permute-start(f32[64,1024]{1,0:T(8,128)S(1)} %get-tuple-element.132), channel_id=1, source_target_pairs={{0,8},{4,12},{8,0},{12,4},{16,24},{20,28},{24,16},{28,20},{1,9},{5... | collective-permute-start | bytes 786440 | tf_op jit(solution)/shard_map/ppermute | solution.py:33
  156.9 4.6 %collective-permute-done.45.rest_11_ = f32[64,256]{1,0:T(8,128)S(1)} collective-permute-done((f32[64,256]{1,0:T(8,128)S(1)}, f32[64,256]{1,0:T(8,128)S(1)}, u32[]{:S(2)}, u32[]{:S(2)}) %collective-permute-start.45) | collective-permute-done | bytes 65568 | tf_op jit(solution)/shard_map/ppermute | solution.py:33
  161.8 5.1 %collective-permute-start.36 = (f32[64,768]{1,0:T(8,128)S(1)}, f32[64,768]{1,0:T(8,128)S(1)}, u32[]{:S(2)}, u32[]{:S(2)}) collective-permute-start(f32[64,768]{1,0:T(8,128)S(1)} %get-tuple-element.128), channel_id=1, source_target_pairs={{0,28},{4,24},{8,20},{12,16},{16,12},{20,8},{24,4},{28,0},{1,29},{... | collective-permute-start | bytes 589832 | tf_op jit(solution)/shard_map/ppermute | solution.py:33
  168.6 4.5 %collective-permute-done.35.rest_2_ = f32[64,768]{1,0:T(8,128)S(1)} collective-permute-done((f32[64,768]{1,0:T(8,128)S(1)}, f32[64,768]{1,0:T(8,128)S(1)}, u32[]{:S(2)}, u32[]{:S(2)}) %collective-permute-start.35) | collective-permute-done | bytes 196640 | tf_op jit(solution)/shard_map/ppermute | solution.py:33
  176.2 3.9 %collective-permute-done.39.rest_7_ = f32[64,1024]{1,0:T(8,128)S(1)} collective-permute-done((f32[64,1024]{1,0:T(8,128)S(1)}, f32[64,1024]{1,0:T(8,128)S(1)}, u32[]{:S(2)}, u32[]{:S(2)}) %collective-permute-start.39) | collective-permute-done | bytes 262176 | tf_op jit(solution)/shard_map/ppermute | solution.py:33
  (134 shorter events, 55.8 us)
Async XLA Ops:
  18.2 15.7 %collective-permute-start.2 = (f32[512,256]{1,0:T(8,128)}, f32[512,256]{1,0:T(8,128)}, u32[]{:S(2)}, u32[]{:S(2)}) collective-permute-start(f32[512,256]{1,0:T(8,128)} %add.27), channel_id=1, source_target_pairs={{0,2},{1,3},{2,0},{3,1},{4,6},{5,7},{6,4},{7,5},{8,10},{9,11},{10,... | collective-permute-start | bytes 1572872 | tf_op jit(solution)/shard_map/ppermute | solution.py:33
  21.7 23.1 %collective-permute-start.9 = (f32[512,256]{1,0:T(8,128)}, f32[512,256]{1,0:T(8,128)S(1)}, u32[]{:S(2)}, u32[]{:S(2)}) collective-permute-start(f32[512,256]{1,0:T(8,128)} %add.28), channel_id=1, source_target_pairs={{0,2},{1,3},{2,0},{3,1},{4,6},{5,7},{6,4},{7,5},{8,10},{9,11},{10,... | collective-permute-start | bytes 1572872 | tf_op jit(solution)/shard_map/ppermute | solution.py:33
  21.7 23.1 %collective-permute-start.15 = (f32[512,256]{1,0:T(8,128)}, f32[512,256]{1,0:T(8,128)}, u32[]{:S(2)}, u32[]{:S(2)}) collective-permute-start(f32[512,256]{1,0:T(8,128)} %get-tuple-element.103), channel_id=1, source_target_pairs={{0,1},{1,0},{2,3},{3,2},{4,5},{5,4},{6,7},{7,6},{8,9},{9,8},{10,11... | collective-permute-start | bytes 1572872 | tf_op jit(solution)/shard_map/ppermute | solution.py:33
  21.8 25.8 %collective-permute-start.7 = (f32[512,256]{1,0:T(8,128)}, f32[512,256]{1,0:T(8,128)}, u32[]{:S(2)}, u32[]{:S(2)}) collective-permute-start(f32[512,256]{1,0:T(8,128)} %get-tuple-element.87), channel_id=1, source_target_pairs={{0,1},{1,0},{2,3},{3,2},{4,5},{5,4},{6,7},{7,6},{8,9},{9,8},{10,11... | collective-permute-start | bytes 1572872 | tf_op jit(solution)/shard_map/ppermute | solution.py:33
  23.0 26.8 %collective-permute-start.22 = (f32[512,256]{1,0:T(8,128)}, f32[512,256]{1,0:T(8,128)}, u32[]{:S(2)}, u32[]{:S(2)}) collective-permute-start(f32[512,256]{1,0:T(8,128)} %get-tuple-element.116), channel_id=1, source_target_pairs={{0,1},{1,0},{2,3},{3,2},{4,5},{5,4},{6,7},{7,6},{8,9},{9,8},{10,11... | collective-permute-start | bytes 1572872 | tf_op jit(solution)/shard_map/ppermute | solution.py:33
  33.9 28.5 %collective-permute-start.14 = (f32[512,256]{1,0:T(8,128)}, f32[512,256]{1,0:T(8,128)S(1)}, u32[]{:S(2)}, u32[]{:S(2)}) collective-permute-start(f32[512,256]{1,0:T(8,128)} %get-tuple-element.100), channel_id=1, source_target_pairs={{0,1},{1,0},{2,3},{3,2},{4,5},{5,4},{6,7},{7,6},{8,9},{9,8},{10,11... | collective-permute-start | bytes 1572872 | tf_op jit(solution)/shard_map/ppermute | solution.py:33
  45.9 14.9 %collective-permute-start.16 = (f32[512,256]{1,0:T(8,128)S(1)}, f32[512,256]{1,0:T(8,128)S(1)}, u32[]{:S(2)}, u32[]{:S(2)}) collective-permute-start(f32[512,256]{1,0:T(8,128)S(1)} %add.29), channel_id=1, source_target_pairs={{0,2},{1,3},{2,0},{3,1},{4,6},{5,7},{6,4},{7,5},{8,10},{9,11},{10,... | collective-permute-start | bytes 1572872 | tf_op jit(solution)/shard_map/ppermute | solution.py:33
  51.2 19.6 %collective-permute-start.23 = (f32[512,256]{1,0:T(8,128)S(1)}, f32[512,256]{1,0:T(8,128)S(1)}, u32[]{:S(2)}, u32[]{:S(2)}) collective-permute-start(f32[512,256]{1,0:T(8,128)S(1)} %add.30), channel_id=1, source_target_pairs={{0,2},{1,3},{2,0},{3,1},{4,6},{5,7},{6,4},{7,5},{8,10},{9,11},{10,... | collective-permute-start | bytes 1572872 | tf_op jit(solution)/shard_map/ppermute | solution.py:33
  51.6 19.3 %collective-permute-start.21 = (f32[512,256]{1,0:T(8,128)S(1)}, f32[512,256]{1,0:T(8,128)S(1)}, u32[]{:S(2)}, u32[]{:S(2)}) collective-permute-start(f32[512,256]{1,0:T(8,128)S(1)} %copy-done.16), channel_id=1, source_target_pairs={{0,1},{1,0},{2,3},{3,2},{4,5},{5,4},{6,7},{7,6},{8,9},{9,8},{10,11... | collective-permute-start | bytes 1572872 | tf_op jit(solution)/shard_map/ppermute | solution.py:33
  51.6 21.2 %collective-permute-start.3 = (f32[4,64,256]{2,1,0:T(8,128)S(1)}, f32[4,64,256]{2,1,0:T(8,128)S(1)}, u32[]{:S(2)}, u32[]{:S(2)}) collective-permute-start(f32[4,64,256]{2,1,0:T(8,128)S(1)} %get-tuple-element.81), channel_id=1, source_target_pairs={{0,16},{4,20},{8,24},{12,28},{16,0},{20,4},{24,8},{28,12},{1,17},{... | collective-permute-start | bytes 786440 | tf_op jit(solution)/shard_map/ppermute | solution.py:33
  71.3 16.5 %collective-permute-start.24 = (f32[4,64,256]{2,1,0:T(8,128)S(1)}, f32[4,64,256]{2,1,0:T(8,128)S(1)}, u32[]{:S(2)}, u32[]{:S(2)}) collective-permute-start(f32[4,64,256]{2,1,0:T(8,128)S(1)} %get-tuple-element.120), channel_id=1, source_target_pairs={{0,4},{4,0},{8,12},{12,8},{16,20},{20,16},{24,28},{28,24},{1,5},{5... | collective-permute-start | bytes 786440 | tf_op jit(solution)/shard_map/ppermute | solution.py:33
  76.4 14.5 %collective-permute-start.11 = (f32[2,64,256]{2,1,0:T(8,128)S(1)}, f32[2,64,256]{2,1,0:T(8,128)S(1)}, u32[]{:S(2)}, u32[]{:S(2)}) collective-permute-start(f32[2,64,256]{2,1,0:T(8,128)S(1)} %get-tuple-element.96), channel_id=1, source_target_pairs={{0,8},{4,12},{8,0},{12,4},{16,24},{20,28},{24,16},{28,20},{1,9},{5... | collective-permute-start | bytes 393224 | tf_op jit(solution)/shard_map/ppermute | solution.py:33
  87.7 19.9 %collective-permute-start.18 = (f32[2,64,256]{2,1,0:T(8,128)S(1)}, f32[2,64,256]{2,1,0:T(8,128)S(1)}, u32[]{:S(2)}, u32[]{:S(2)}) collective-permute-start(f32[2,64,256]{2,1,0:T(8,128)S(1)} %get-tuple-element.109), channel_id=1, source_target_pairs={{0,8},{4,12},{8,0},{12,4},{16,24},{20,28},{24,16},{28,20},{1,9},{5... | collective-permute-start | bytes 393224 | tf_op jit(solution)/shard_map/ppermute | solution.py:33
  88.1 20.9 %collective-permute-start.19 = (f32[2,64,256]{2,1,0:T(8,128)S(1)}, f32[2,64,256]{2,1,0:T(8,128)S(1)}, u32[]{:S(2)}, u32[]{:S(2)}) collective-permute-start(f32[2,64,256]{2,1,0:T(8,128)S(1)} %get-tuple-element.110), channel_id=1, source_target_pairs={{0,16},{4,20},{8,24},{12,28},{16,0},{20,4},{24,8},{28,12},{1,17},{... | collective-permute-start | bytes 393224 | tf_op jit(solution)/shard_map/ppermute | solution.py:33
  90.9 18.0 %collective-permute-start.20 = (f32[2,64,256]{2,1,0:T(8,128)S(1)}, f32[2,64,256]{2,1,0:T(8,128)S(1)}, u32[]{:S(2)}, u32[]{:S(2)}) collective-permute-start(f32[2,64,256]{2,1,0:T(8,128)S(1)} %get-tuple-element.111), channel_id=1, source_target_pairs={{0,24},{4,28},{8,16},{12,20},{16,8},{20,12},{24,0},{28,4},{1,25},{... | collective-permute-start | bytes 393224 | tf_op jit(solution)/shard_map/ppermute | solution.py:33
  97.3 19.5 %collective-permute-start.26 = (f32[2,64,256]{2,1,0:T(8,128)S(1)}, f32[2,64,256]{2,1,0:T(8,128)S(1)}, u32[]{:S(2)}, u32[]{:S(2)}) collective-permute-start(f32[2,64,256]{2,1,0:T(8,128)S(1)} %get-tuple-element.123), channel_id=1, source_target_pairs={{0,16},{4,20},{8,24},{12,28},{16,0},{20,4},{24,8},{28,12},{1,17},{... | collective-permute-start | bytes 393224 | tf_op jit(solution)/shard_map/ppermute | solution.py:33
  124.4 22.4 %collective-permute-start.41 = (f32[2,64,256]{2,1,0:T(8,128)S(1)}, f32[2,64,256]{2,1,0:T(8,128)S(1)}, u32[]{:S(2)}, u32[]{:S(2)}) collective-permute-start(f32[2,64,256]{2,1,0:T(8,128)S(1)} %get-tuple-element.138), channel_id=1, source_target_pairs={{0,16},{4,20},{8,24},{12,28},{16,0},{20,4},{24,8},{28,12},{1,17},{... | collective-permute-start | bytes 393224 | tf_op jit(solution)/shard_map/ppermute | solution.py:33
  128.0 18.8 %collective-permute-start.42 = (f32[2,64,256]{2,1,0:T(8,128)S(1)}, f32[2,64,256]{2,1,0:T(8,128)S(1)}, u32[]{:S(2)}, u32[]{:S(2)}) collective-permute-start(f32[2,64,256]{2,1,0:T(8,128)S(1)} %get-tuple-element.140), channel_id=1, source_target_pairs={{0,24},{4,28},{8,16},{12,20},{16,8},{20,12},{24,0},{28,4},{1,25},{... | collective-permute-start | bytes 393224 | tf_op jit(solution)/shard_map/ppermute | solution.py:33
  128.8 18.0 %collective-permute-start.40 = (f32[2,64,256]{2,1,0:T(8,128)S(1)}, f32[2,64,256]{2,1,0:T(8,128)S(1)}, u32[]{:S(2)}, u32[]{:S(2)}) collective-permute-start(f32[2,64,256]{2,1,0:T(8,128)S(1)} %get-tuple-element.136), channel_id=1, source_target_pairs={{0,8},{4,12},{8,0},{12,4},{16,24},{20,28},{24,16},{28,20},{1,9},{5... | collective-permute-start | bytes 393224 | tf_op jit(solution)/shard_map/ppermute | solution.py:33
  144.1 17.5 %collective-permute-start.33 = (f32[64,768]{1,0:T(8,128)S(1)}, f32[64,768]{1,0:T(8,128)S(1)}, u32[]{:S(2)}, u32[]{:S(2)}) collective-permute-start(f32[64,768]{1,0:T(8,128)S(1)} %get-tuple-element.125), channel_id=1, source_target_pairs={{0,16},{4,20},{8,24},{12,28},{16,0},{20,4},{24,8},{28,12},{1,17},{... | collective-permute-start | bytes 589832 | tf_op jit(solution)/shard_map/ppermute | solution.py:33
  144.8 17.0 %collective-permute-start.34 = (f32[64,768]{1,0:T(8,128)S(1)}, f32[64,768]{1,0:T(8,128)S(1)}, u32[]{:S(2)}, u32[]{:S(2)}) collective-permute-start(f32[64,768]{1,0:T(8,128)S(1)} %get-tuple-element.126), channel_id=1, source_target_pairs={{0,20},{4,16},{8,28},{12,24},{16,4},{20,0},{24,12},{28,8},{1,21},{... | collective-permute-start | bytes 589832 | tf_op jit(solution)/shard_map/ppermute | solution.py:33
  152.0 23.1 %collective-permute-start.37 = (f32[64,1024]{1,0:T(8,128)S(1)}, f32[64,1024]{1,0:T(8,128)S(1)}, u32[]{:S(2)}, u32[]{:S(2)}) collective-permute-start(f32[64,1024]{1,0:T(8,128)S(1)} %get-tuple-element.131), channel_id=1, source_target_pairs={{0,4},{4,0},{8,12},{12,8},{16,20},{20,16},{24,28},{28,24},{1,5},{5... | collective-permute-start | bytes 786440 | tf_op jit(solution)/shard_map/ppermute | solution.py:33
  154.5 21.7 %collective-permute-start.38 = (f32[64,1024]{1,0:T(8,128)S(1)}, f32[64,1024]{1,0:T(8,128)S(1)}, u32[]{:S(2)}, u32[]{:S(2)}) collective-permute-start(f32[64,1024]{1,0:T(8,128)S(1)} %get-tuple-element.132), channel_id=1, source_target_pairs={{0,8},{4,12},{8,0},{12,4},{16,24},{20,28},{24,16},{28,20},{1,9},{5... | collective-permute-start | bytes 786440 | tf_op jit(solution)/shard_map/ppermute | solution.py:33
  161.5 18.6 %collective-permute-start.39 = (f32[64,1024]{1,0:T(8,128)S(1)}, f32[64,1024]{1,0:T(8,128)S(1)}, u32[]{:S(2)}, u32[]{:S(2)}) collective-permute-start(f32[64,1024]{1,0:T(8,128)S(1)} %get-tuple-element.133), channel_id=1, source_target_pairs={{0,12},{4,8},{8,4},{12,0},{16,28},{20,24},{24,20},{28,16},{1,13},{... | collective-permute-start | bytes 786440 | tf_op jit(solution)/shard_map/ppermute | solution.py:33
  (39 other events, 497.2 us)

commit v5 on v4

--- a/solution.py
+++ b/solution.py
@@ -19,9 +19,9 @@
 CHUNKS = (256, 256, 256, 256)
 STARTS = tuple(sum(CHUNKS[:k]) for k in range(len(CHUNKS)))
 COUNT = len(CHUNKS)
-EARLY = 2
+EARLY = 1
 BITS = (-1, 0, 0, 0)
-SHARED = 3
+SHARED = 640
 
 
 SMEM = pl.BlockSpec(memory_space=pltpu.SMEM)
@@ -71,10 +71,18 @@
         copies.append(pltpu.make_async_copy(upstream_hbm.at[0, cut], upstream_ref.at[cut], sems.at[2 * i + 1]))
     for copy in copies:
         copy.start()
-    for copy in copies:
-        copy.wait()
     side = at % 2
-    blocks_of(left_ref, upstream_ref, rows, (1 - side, side), outs)
+    left = pl.ds(pl.multiple_of((1 - side) * rows, LANES), rows)
+    early = len(cuts) // 2
+    for part in range(2):
+        mine = cuts[early:] if part else cuts[:early]
+        for copy in copies[2 * early * part :][: 2 * len(mine)]:
+            copy.wait()
+        down = slice(mine[0].start, mine[-1].stop)
+        for k in range(COUNT):
+            value = product(left_ref[down, left], upstream_ref[down, STARTS[k] : STARTS[k] + CHUNKS[k]])
+            outs[k][...] = outs[k][...] + value if part else value
+    blocks_of(left_ref, upstream_ref, rows, (side,), outs[COUNT:])
 
 
 def second_kernel(rows, at_ref, features_ref, upstream_ref, *outs):
@@ -97,7 +105,7 @@
         return list(outs[:COUNT]), list(outs[COUNT:])
     hbm = pl.BlockSpec(memory_space=pltpu.HBM)
     tokens = features.shape[1]
-    step = tokens // 6 if tokens % 96 == 0 else tokens
+    step = tokens // 6 if tokens % 96 == 0 else tokens // 2
     cuts = [slice(start, start + step) for start in range(0, tokens, step)]
     outs = pl.pallas_call(
         functools.partial(first_kernel, rows, cuts),
@@ -115,6 +123,39 @@
     return list(outs[:COUNT]), list(outs[COUNT:])
 
 
+def base_kernel(weights_ref, momentum_ref, out_ref):
+    out_ref[...] = weights_ref[...] - (0.5 * LEARNING_RATE) * momentum_ref[...]
+
+
+def base(weights, momentum):
+    return pl.pallas_call(
+        base_kernel,
+        in_specs=[VMEM, VMEM],
+        out_specs=VMEM,
+        out_shape=jax.ShapeDtypeStruct(weights.shape, jnp.float32),
+        compiler_params=pltpu.CompilerParams(vmem_limit_bytes=8 << 20),
+        name="base",
+    )(weights, momentum)
+
+
+def add_kernel(*refs):
+    value = refs[0][...]
+    for ref in refs[1:-1]:
+        value = value + ref[...]
+    refs[-1][...] = value
+
+
+def add(*terms):
+    return pl.pallas_call(
+        add_kernel,
+        in_specs=[VMEM] * len(terms),
+        out_specs=VMEM,
+        out_shape=jax.ShapeDtypeStruct(terms[0].shape, terms[0].dtype),
+        compiler_params=pltpu.CompilerParams(vmem_limit_bytes=8 << 20),
+        name="add",
+    )(*terms)
+
+
 def velocity_kernel(cut, gradient_ref, momentum_ref, *rest):
     out_ref, scratch_ref, sem = rest[-3:]
     scratch_ref[...] = 0.5 * momentum_ref[:, cut] + gradient_ref[...]
@@ -148,13 +189,13 @@
 
 
 def update_kernel(k, count, bit, me_ref, *rest):
-    terms, (momentum_ref, weights_ref, gradient_ref, keep_ref, send_ref) = rest[:count], rest[count:]
+    terms, (base_ref, gradient_ref, keep_ref, send_ref) = rest[:count], rest[count:]
     cut = slice(STARTS[k], STARTS[k] + CHUNKS[k])
     gradient = terms[0][...]
     for term in terms[1:]:
         gradient = gradient + term[...]
     gradient_ref[...] = gradient
-    current = weights_ref[:, cut] - LEARNING_RATE * (0.5 * momentum_ref[:, cut] + gradient)
+    current = base_ref[:, cut] - LEARNING_RATE * gradient
     side = (me_ref[0] >> bit) & 1
     slots, size, _ = keep_ref.shape
     for worker in range(2 * slots):
@@ -166,38 +207,39 @@
                 out[slot] = piece
 
 
-def update(me, terms, momentum, weights, k, workers, bit):
+def update(me, terms, start, k, workers, bit):
     rows = terms[0].shape[0]
     full = jax.ShapeDtypeStruct(terms[0].shape, jnp.float32)
     part = jax.ShapeDtypeStruct((workers // 2, rows // workers, CHUNKS[k]), jnp.float32)
     return pl.pallas_call(
         functools.partial(update_kernel, k, len(terms), bit),
-        in_specs=[SMEM] + [VMEM] * (len(terms) + 2),
+        in_specs=[SMEM] + [VMEM] * (len(terms) + 1),
         out_specs=[VMEM] * 3,
         out_shape=[full, part, part],
         compiler_params=pltpu.CompilerParams(vmem_limit_bytes=8 << 20),
         name="update",
-    )(me, *terms, momentum, weights)
-
-
-def regroup_kernel(bit, turn, me_ref, *rest):
+    )(me, *terms, start)
+
+
+def regroup_kernel(bit, turn, skips, me_ref, *rest):
     group = rest[0].shape[0]
     parts, outs = rest[:-group], rest[-group:]
     rank = without(me_ref[0], bit) ^ turn
     for i, out in enumerate(outs):
         start = 0
         for place in range(0, len(parts), 2):
-            width = parts[place].shape[2]
+            skip = skips[place // 2]
+            width = parts[place].shape[2] - skip
             for side in range(2):
-                out[side, :, start : start + width] = parts[place + side][rank ^ i]
+                out[side, :, start : start + width] = parts[place + side][rank ^ i, :, skip:]
             start += width
 
 
-def regroup(me, parts, bit, turn=0):
+def regroup(me, parts, bit, turn=0, skips=(0,)):
     group, rows, _ = parts[0].shape
-    width = sum(part.shape[2] for part in parts[::2])
-    return pl.pallas_call(
-        functools.partial(regroup_kernel, bit, turn),
+    width = sum(part.shape[2] - skip for part, skip in zip(parts[::2], skips))
+    return pl.pallas_call(
+        functools.partial(regroup_kernel, bit, turn, skips),
         in_specs=[SMEM] + [VMEM] * len(parts),
         out_specs=[VMEM] * group,
         out_shape=[jax.ShapeDtypeStruct((2, rows, width), jnp.float32)] * group,
@@ -359,9 +401,9 @@
     else:
         matrix_ref, *rest = rest
     me = me_ref[0]
-    for bit, start, into in layout:
+    for bit, start, into, size in layout:
         refs, rest = rest[: workers // 2], rest[workers // 2 :]
-        for lane in range(0, refs[0].shape[2], LANES):
+        for lane in range(0, size, LANES):
             base = (start + lane) // half * workers * workers
             old = pieces_of(refs, bit, slice(lane, lane + LANES))
             for mask, out in zip(masks, rest[-len(masks) :]):
@@ -375,7 +417,7 @@
 def mix(masks, me, matrix, head, chunks, layout, workers, half):
     first = matrix is None
     rows = chunks[0][0].shape[1]
-    width = sum(chunk[0].shape[2] for chunk in chunks)
+    width = sum(size for _, _, _, size in layout)
     table = jax.ShapeDtypeStruct((2 * workers * workers, LANES), jnp.float32)
     head = (*head, selectors(workers)) if first else (matrix,)
     return pl.pallas_call(
@@ -429,7 +471,7 @@
     leaves = {}
     for offset in [*range(last, tokens, 2), *range(0, last, 2)]:
         at = index(offset) if order[0] is None else after(index(offset), order[0])
-        leaves[offset + 1], leaves[offset] = multiply(at, inputs, cotangent, rows, order[0] is None)
+        leaves[offset + 1], leaves[offset] = multiply(at, inputs, cotangent, rows, True)
         order[0] = leaves[offset][0]
 
     def arrived(offset, level, k):
@@ -441,7 +483,7 @@
         return terms
 
     def reduced(offset, level, k):
-        return sum(arrived(offset, level, k), leaves[offset][k])
+        return add(leaves[offset][k], *arrived(offset, level, k)) if level else leaves[offset][k]
 
     def send_terms(k, *gates):
         leaves[last][k] = after(leaves[last][k], *gates)
@@ -453,17 +495,21 @@
         moved, away = send_terms(k, away)
         aways.append(moved)
     extras = [arrived(0, levels - 1, k) for k in range(COUNT)]
+    moved, away = send_terms(1, away, leaves[0][0])
+    aways.append(moved)
+    start = base(weights[0], momentum[0])
     velocity, chunks, sums = None, [], []
     bits = [bit % (workers.bit_length() - 1) for bit in BITS]
-    held = []
+    held, skips = [], ()
     for k in range(COUNT):
         away = after(aways[k], gradient) if k else aways[k]
         terms = [leaves[0][k], *extras[k], away]
-        gradient, keep, send = update(here, terms, momentum[0], weights[0], k, workers, bits[k])
+        gradient, keep, send = update(here, terms, start, k, workers, bits[k])
         got = flip(send, "worker", 1 << bits[k])
         pieces = list(regroup(here, (keep, got), bits[k]))
-        if k >= SHARED:
+        if STARTS[k] + CHUNKS[k] > SHARED:
             held += [keep, got]
+            skips += (max(SHARED - STARTS[k], 0),)
         for i in reversed(range(1, group)):
             pieces[i] = flip(pieces[i], "worker", spread_bits(i, bits[k]))
         chunks.append(pieces)
@@ -477,35 +523,34 @@
             moved, _ = send_terms(len(aways), velocity)
             aways.append(moved)
     packed = pack(sums, chunks[-1], mix_weights, here, workers, tokens, bits[-1], h_of[-1])
-    bit = bits[SHARED]
-    mirror = list(regroup(here, held, bit, without(group, bit)))
+    bit = bits[-1]
+    mirror = list(regroup(here, held, bit, without(group, bit), skips))
     later = [*range(group // 2, group), *range(1, group // 2)]
-    for axis, size in (("tok", tokens), ("worker", workers)):
-        mask = 1
-        while mask < size:
-            packed = packed + flip(packed, axis, mask)
-            if later:
-                i = later.pop(0)
-                mirror[i] = flip(after(mirror[i], packed), "worker", spread_bits(i, bit))
-            mask *= 2
+    rounds = [("worker", [2 * i for i in range(1, group)]), ("worker", [1])]
+    rounds += [("tok", [1 << level]) for level in range(levels)]
+    for axis, masks in rounds:
+        packed = sum([flip(packed, axis, mask) for mask in masks], packed)
+        if later:
+            i = later.pop(0)
+            mirror[i] = flip(after(mirror[i], packed), "worker", spread_bits(i, bit))
     for i in later:
         mirror[i] = flip(mirror[i], "worker", spread_bits(i, bit))
-    split = STARTS[SHARED]
-    layout = tuple((bit, start, start) for bit, start in zip(bits, STARTS))
+    layout = tuple((bit, start, start, size) for bit, start, size in zip(bits, STARTS, CHUNKS))
+    apart = tuple((bit, start, start, min(size, SHARED - start)) for bit, start, _, size in layout if start < SHARED)
     near, far = tuple(range(group)), tuple(range(group, workers))
     pieces, spots = [], []
-    *out, matrix = mix(far, here, None, (clip_radius, packed), chunks[:SHARED], layout[:SHARED], workers, half)
+    *out, matrix = mix(near, here, None, (clip_radius, packed), chunks, layout, workers, half)
+    for mask, value in zip(near, out):
+        pieces.append(flip(value, "worker", mask) if mask else value)
+        spots.append((mask, 0))
+    out = mix(far, here, matrix, (), chunks[: len(apart)], apart, workers, half)
     for mask, value in zip(far, out):
         pieces.append(flip(value, "worker", mask))
         spots.append((mask, 0))
-    out = mix(near, here, matrix, (), chunks, layout, workers, half)
+    out = mix(near, here, matrix, (), [mirror], ((bit, SHARED, 0, width - SHARED),), workers, half)
     for mask, value in zip(near, out):
         pieces.append(flip(value, "worker", mask) if mask else value)
-        spots.append((mask, 0))
-    out = mix(near, here, matrix, (), [mirror], ((bit, split, 0),), workers, half)
-    for mask, value in zip(near, out):
-        pieces.append(flip(value, "worker", mask) if mask else value)
-        spots.append((mask ^ group, split))
+        spots.append((mask ^ group, SHARED))
     new = place(here, pieces, tuple(spots), rows, width)
     return new[None], velocity[None]
 

time: 182 us -> 197 us (1.082)
  waiting for transfers between devices: 81.4 us -> 97.6 us
  other arithmetic: 4.02 us -> 0.01 us
  starting transfers between devices: 63.1 us -> 66.7 us
    ppermute x46 -> x47, waiting for transfers between devices: 81.4 us -> 97.6 us  [flip(): return lax.ppermute(value, axis, pairs)]
    pallas_call x6 -> x10, Pallas kernels: 8.39 us -> 2.5 us  [the longest x4 2.09 us: add(): pl.pallas_call(add_kernel, in_specs=[VMEM] * len(terms), out_specs=VMEM,...]
    pallas_call x1 -> x2, Pallas kernels: 7.31 us -> 13.2 us  [multiply(): pl.pallas_call(functools.partial(first_kernel, rows, cuts), in_specs=[SME...]
    add x9 -> x4, other arithmetic: 4.02 us -> 0.01 us  [per_device(): packed = sum([flip(packed, axis, mask) for mask in masks], packed)]
    ppermute x46 -> x47, starting transfers between devices: 63.1 us -> 66.7 us  [flip(): return lax.ppermute(value, axis, pairs)]
  transfers between devices with their start and end apart: 46 -> 47, of which waited for: 18 -> 19; matrix products, arithmetic and copies ran while one was open for 2% -> 0% of each run, Pallas kernels for 10% -> 9%
where the time goes in v5:
time: 197 us
  waiting for transfers between devices  97.6 us (50%)
  starting transfers between devices  66.7 us (34%)
  Pallas kernels  28.3 us (14%)
  local copies, waits for them, and re-layouts  2.73 us (1%)
    ppermute x47, waiting for transfers between devices, flip(): return lax.ppermute(value, axis, pairs)  97.6 us
    ppermute x47, starting transfers between devices, flip(): return lax.ppermute(value, axis, pairs)  66.7 us
    pallas_call x2, Pallas kernels, multiply(): pl.pallas_call(functools.partial(first_kernel, rows, cuts), in_specs=[SME...  13.2 us
  transfers between devices with their start and end apart: 47, of which 19 were waited for; matrix products, arithmetic and copies ran while one was open for 0% of the time, Pallas kernels for 9%

profile of v5, /device:TPU:0, one launch (start us, length us, event | category | flops | bytes accessed | tf_op | source)
XLA Modules:
  0.0 196.6 jit_solution(17397057624358179437)
XLA Ops:
  0.6 6.6 %first.2 = (f32[512,256]{1,0:T(8,128)}, f32[512,256]{1,0:T(8,128)}, f32[512,256]{1,0:T(8,128)}, f32[512,256]{1,0:T(8,128)}, f32[512,256]{1,0:T(8,128)}, /*index=...) custom-call(s32[1]{0:T(128)} %bitcast.2.at_ref, bf16[1,1536,2048]{2,1,0:T(8,128)(2,1)} %features_hbm.3, ...), custom_call_target="tpu_custom_call" | custom-call | tf_op jit(solution)/shard_map/first/pallas_call | solution.py:110
  7.8 6.6 %first.3 = (f32[512,256]{1,0:T(8,128)}, f32[512,256]{1,0:T(8,128)}, f32[512,256]{1,0:T(8,128)}, f32[512,256]{1,0:T(8,128)}, f32[512,256]{1,0:T(8,128)}, /*index=...) custom-call(s32[1]{0:T(128)} %bitcast.1.at_ref, bf16[1,1536,2048]{2,1,0:T(8,128)(2,1)} %features_hbm.3, ...), custom_call_target="tpu_custom_call" | custom-call | tf_op jit(solution)/shard_map/first/pallas_call | solution.py:110
  15.8 2.6 %collective-permute-start.2 = (f32[512,256]{1,0:T(8,128)}, f32[512,256]{1,0:T(8,128)}, u32[]{:S(2)}, u32[]{:S(2)}) collective-permute-start(f32[512,256]{1,0:T(8,128)} %add.31), channel_id=1, source_target_pairs={{0,2},{1,3},{2,0},{3,1},{4,6},{5,7},{6,4},{7,5},{8,10},{9,11},{10,... | collective-permute-start | bytes 1572872 | tf_op jit(solution)/shard_map/ppermute | solution.py:33
  22.0 9.6 %collective-permute-done.2.rest_2_ = f32[512,256]{1,0:T(8,128)} collective-permute-done((f32[512,256]{1,0:T(8,128)}, f32[512,256]{1,0:T(8,128)}, u32[]{:S(2)}, u32[]{:S(2)}) %collective-permute-start.2) | collective-permute-done | bytes 524320 | tf_op jit(solution)/shard_map/ppermute | solution.py:33
  33.7 8.8 %collective-permute-done.9.rest_2_ = f32[512,256]{1,0:T(8,128)} collective-permute-done((f32[512,256]{1,0:T(8,128)S(1)}, f32[512,256]{1,0:T(8,128)}, u32[]{:S(2)}, u32[]{:S(2)}) %collective-permute-start.9) | collective-permute-done | bytes 524320 | tf_op jit(solution)/shard_map/ppermute | solution.py:33
  48.4 2.8 %collective-permute-start.3 = (f32[4,64,256]{2,1,0:T(8,128)S(1)}, f32[4,64,256]{2,1,0:T(8,128)S(1)}, u32[]{:S(2)}, u32[]{:S(2)}) collective-permute-start(f32[4,64,256]{2,1,0:T(8,128)S(1)} %get-tuple-element.81), channel_id=1, source_target_pairs={{0,16},{4,20},{8,24},{12,28},{16,0},{20,4},{24,8},{28,12},{1,17},{... | collective-permute-start | bytes 786440 | tf_op jit(solution)/shard_map/ppermute | solution.py:33
  51.2 7.3 %collective-permute-done.16.rest_2_ = f32[512,256]{1,0:T(8,128)S(1)} collective-permute-done((f32[512,256]{1,0:T(8,128)S(1)}, f32[512,256]{1,0:T(8,128)S(1)}, u32[]{:S(2)}, u32[]{:S(2)}) %collective-permute-start.16) | collective-permute-done | bytes 524320 | tf_op jit(solution)/shard_map/ppermute | solution.py:33
  60.8 7.8 %collective-permute-done.23.rest_2_ = f32[512,256]{1,0:T(8,128)S(1)} collective-permute-done((f32[512,256]{1,0:T(8,128)S(1)}, f32[512,256]{1,0:T(8,128)S(1)}, u32[]{:S(2)}, u32[]{:S(2)}) %collective-permute-start.23) | collective-permute-done | bytes 524320 | tf_op jit(solution)/shard_map/ppermute | solution.py:33
  75.9 6.1 %collective-permute-done.4.rest_1_.rest_4_.rest_2_ = f32[2,64,256]{2,1,0:T(8,128)S(1)} collective-permute-done((f32[2,64,256]{2,1,0:T(8,128)S(1)}, f32[2,64,256]{2,1,0:T(8,128)S(1)}, u32[]{:S(2)}, u32[]{:S(2)}) %collective-permute-start.4) | collective-permute-done | bytes 131104 | tf_op jit(solution)/shard_map/ppermute | solution.py:33
  85.9 2.8 %collective-permute-start.19 = (f32[2,64,256]{2,1,0:T(8,128)S(1)}, f32[2,64,256]{2,1,0:T(8,128)S(1)}, u32[]{:S(2)}, u32[]{:S(2)}) collective-permute-start(f32[2,64,256]{2,1,0:T(8,128)S(1)} %get-tuple-element.110), channel_id=1, source_target_pairs={{0,16},{4,20},{8,24},{12,28},{16,0},{20,4},{24,8},{28,12},{1,17},{... | collective-permute-start | bytes 393224 | tf_op jit(solution)/shard_map/ppermute | solution.py:33
  90.0 4.8 %collective-permute-done.12.rest_2_.rest_9_.rest_7_ = f32[2,64,256]{2,1,0:T(8,128)S(1)} collective-permute-done((f32[2,64,256]{2,1,0:T(8,128)S(1)}, f32[2,64,256]{2,1,0:T(8,128)S(1)}, u32[]{:S(2)}, u32[]{:S(2)}) %collective-permute-start.12) | collective-permute-done | bytes 131104 | tf_op jit(solution)/shard_map/ppermute | solution.py:33
  95.0 10.3 %collective-permute-start.26 = (f32[2,64,256]{2,1,0:T(8,128)S(1)}, f32[2,64,256]{2,1,0:T(8,128)S(1)}, u32[]{:S(2)}, u32[]{:S(2)}) collective-permute-start(f32[2,64,256]{2,1,0:T(8,128)S(1)} %get-tuple-element.123), channel_id=1, source_target_pairs={{0,16},{4,20},{8,24},{12,28},{16,0},{20,4},{24,8},{28,12},{1,17},{... | collective-permute-start | bytes 393224 | tf_op jit(solution)/shard_map/ppermute | solution.py:33
  107.0 7.5 %collective-permute-done.26.rest_5_.rest_17_ = f32[2,64,256]{2,1,0:T(8,128)S(1)} collective-permute-done((f32[2,64,256]{2,1,0:T(8,128)S(1)}, f32[2,64,256]{2,1,0:T(8,128)S(1)}, u32[]{:S(2)}, u32[]{:S(2)}) %collective-permute-start.26) | collective-permute-done | bytes 131104 | tf_op jit(solution)/shard_map/ppermute | solution.py:33
  115.5 2.9 %collective-permute-start.30 = (f32[8,128]{1,0:T(8,128)S(1)}, f32[8,128]{1,0:T(8,128)S(1)}, u32[]{:S(2)}, u32[]{:S(2)}) collective-permute-start(f32[8,128]{1,0:T(8,128)S(1)} %pack.1), channel_id=1, source_target_pairs={{0,24},{4,28},{8,16},{12,20},{16,8},{20,12},{24,0},{28,4},{1,25},{... | collective-permute-start | bytes 12296 | tf_op jit(solution)/shard_map/ppermute | solution.py:33
  137.2 2.4 %collective-permute-start.43 = (f32[2,64,384]{2,1,0:T(8,128)S(1)}, f32[2,64,384]{2,1,0:T(8,128)S(1)}, u32[]{:S(2)}, u32[]{:S(2)}) collective-permute-start(f32[2,64,384]{2,1,0:T(8,128)S(1)} %get-tuple-element.140), channel_id=1, source_target_pairs={{0,24},{4,28},{8,16},{12,20},{16,8},{20,12},{24,0},{28,4},{1,25},{... | collective-permute-start | bytes 589832 | tf_op jit(solution)/shard_map/ppermute | solution.py:33
  139.7 3.1 %collective-permute-start.38 = (f32[64,640]{1,0:T(8,128)S(1)}, f32[64,640]{1,0:T(8,128)S(1)}, u32[]{:S(2)}, u32[]{:S(2)}) collective-permute-start(f32[64,640]{1,0:T(8,128)S(1)} %get-tuple-element.131), channel_id=1, source_target_pairs={{0,20},{4,16},{8,28},{12,24},{16,4},{20,0},{24,12},{28,8},{1,21},{... | collective-permute-start | bytes 491528 | tf_op jit(solution)/shard_map/ppermute | solution.py:33
  142.8 11.2 %collective-permute-done.37.rest_4_ = f32[64,640]{1,0:T(8,128)S(1)} collective-permute-done((f32[64,640]{1,0:T(8,128)S(1)}, f32[64,640]{1,0:T(8,128)S(1)}, u32[]{:S(2)}, u32[]{:S(2)}) %collective-permute-start.37) | collective-permute-done | bytes 163872 | tf_op jit(solution)/shard_map/ppermute | solution.py:33
  155.9 12.9 %collective-permute-done.38.rest_5_ = f32[64,640]{1,0:T(8,128)S(1)} collective-permute-done((f32[64,640]{1,0:T(8,128)S(1)}, f32[64,640]{1,0:T(8,128)S(1)}, u32[]{:S(2)}, u32[]{:S(2)}) %collective-permute-start.38) | collective-permute-done | bytes 163872 | tf_op jit(solution)/shard_map/ppermute | solution.py:33
  168.8 2.5 %collective-permute-start.39 = (f32[64,640]{1,0:T(8,128)S(1)}, f32[64,640]{1,0:T(8,128)S(1)}, u32[]{:S(2)}, u32[]{:S(2)}) collective-permute-start(f32[64,640]{1,0:T(8,128)S(1)} %get-tuple-element.132), channel_id=1, source_target_pairs={{0,24},{4,28},{8,16},{12,20},{16,8},{20,12},{24,0},{28,4},{1,25},{... | collective-permute-start | bytes 491528 | tf_op jit(solution)/shard_map/ppermute | solution.py:33
  172.3 3.2 %collective-permute-start.36 = (f32[64,1024]{1,0:T(8,128)S(1)}, f32[64,1024]{1,0:T(8,128)S(1)}, u32[]{:S(2)}, u32[]{:S(2)}) collective-permute-start(f32[64,1024]{1,0:T(8,128)S(1)} %get-tuple-element.128), channel_id=1, source_target_pairs={{0,12},{4,8},{8,4},{12,0},{16,28},{20,24},{24,20},{28,16},{1,13},{... | collective-permute-start | bytes 786440 | tf_op jit(solution)/shard_map/ppermute | solution.py:33
  177.9 3.3 %collective-permute-done.40.rest_7_ = f32[64,640]{1,0:T(8,128)S(1)} collective-permute-done((f32[64,640]{1,0:T(8,128)S(1)}, f32[64,640]{1,0:T(8,128)S(1)}, u32[]{:S(2)}, u32[]{:S(2)}) %collective-permute-start.40) | collective-permute-done | bytes 163872 | tf_op jit(solution)/shard_map/ppermute | solution.py:33
  181.1 4.0 %collective-permute-start.45 = (f32[64,384]{1,0:T(8,128)S(1)}, f32[64,384]{1,0:T(8,128)S(1)}, u32[]{:S(2)}, u32[]{:S(2)}) collective-permute-start(f32[64,384]{1,0:T(8,128)S(1)} %get-tuple-element.143), channel_id=1, source_target_pairs={{0,8},{4,12},{8,0},{12,4},{16,24},{20,28},{24,16},{28,20},{1,9},{5... | collective-permute-start | bytes 294920 | tf_op jit(solution)/shard_map/ppermute | solution.py:33
  186.9 4.0 %collective-permute-done.36.rest_3_ = f32[64,1024]{1,0:T(8,128)S(1)} collective-permute-done((f32[64,1024]{1,0:T(8,128)S(1)}, f32[64,1024]{1,0:T(8,128)S(1)}, u32[]{:S(2)}, u32[]{:S(2)}) %collective-permute-start.36) | collective-permute-done | bytes 262176 | tf_op jit(solution)/shard_map/ppermute | solution.py:33
  190.9 2.3 %collective-permute-done.45.rest_10_ = f32[64,384]{1,0:T(8,128)S(1)} collective-permute-done((f32[64,384]{1,0:T(8,128)S(1)}, f32[64,384]{1,0:T(8,128)S(1)}, u32[]{:S(2)}, u32[]{:S(2)}) %collective-permute-start.45) | collective-permute-done | bytes 98336 | tf_op jit(solution)/shard_map/ppermute | solution.py:33
  (136 shorter events, 59.9 us)
Async XLA Ops:
  15.8 15.7 %collective-permute-start.2 = (f32[512,256]{1,0:T(8,128)}, f32[512,256]{1,0:T(8,128)}, u32[]{:S(2)}, u32[]{:S(2)}) collective-permute-start(f32[512,256]{1,0:T(8,128)} %add.31), channel_id=1, source_target_pairs={{0,2},{1,3},{2,0},{3,1},{4,6},{5,7},{6,4},{7,5},{8,10},{9,11},{10,... | collective-permute-start | bytes 1572872 | tf_op jit(solution)/shard_map/ppermute | solution.py:33
  18.5 24.0 %collective-permute-start.9 = (f32[512,256]{1,0:T(8,128)S(1)}, f32[512,256]{1,0:T(8,128)}, u32[]{:S(2)}, u32[]{:S(2)}) collective-permute-start(f32[512,256]{1,0:T(8,128)S(1)} %add.32), channel_id=1, source_target_pairs={{0,2},{1,3},{2,0},{3,1},{4,6},{5,7},{6,4},{7,5},{8,10},{9,11},{10,... | collective-permute-start | bytes 1572872 | tf_op jit(solution)/shard_map/ppermute | solution.py:33
  18.6 23.9 %collective-permute-start.15 = (f32[512,256]{1,0:T(8,128)}, f32[512,256]{1,0:T(8,128)}, u32[]{:S(2)}, u32[]{:S(2)}) collective-permute-start(f32[512,256]{1,0:T(8,128)} %get-tuple-element.103), channel_id=1, source_target_pairs={{0,1},{1,0},{2,3},{3,2},{4,5},{5,4},{6,7},{7,6},{8,9},{9,8},{10,11... | collective-permute-start | bytes 1572872 | tf_op jit(solution)/shard_map/ppermute | solution.py:33
  18.8 26.6 %collective-permute-start.7 = (f32[512,256]{1,0:T(8,128)}, f32[512,256]{1,0:T(8,128)}, u32[]{:S(2)}, u32[]{:S(2)}) collective-permute-start(f32[512,256]{1,0:T(8,128)} %get-tuple-element.87), channel_id=1, source_target_pairs={{0,1},{1,0},{2,3},{3,2},{4,5},{5,4},{6,7},{7,6},{8,9},{9,8},{10,11... | collective-permute-start | bytes 1572872 | tf_op jit(solution)/shard_map/ppermute | solution.py:33
  20.0 27.8 %collective-permute-start.22 = (f32[512,256]{1,0:T(8,128)}, f32[512,256]{1,0:T(8,128)S(1)}, u32[]{:S(2)}, u32[]{:S(2)}) collective-permute-start(f32[512,256]{1,0:T(8,128)} %get-tuple-element.116), channel_id=1, source_target_pairs={{0,1},{1,0},{2,3},{3,2},{4,5},{5,4},{6,7},{7,6},{8,9},{9,8},{10,11... | collective-permute-start | bytes 1572872 | tf_op jit(solution)/shard_map/ppermute | solution.py:33
  31.5 28.6 %collective-permute-start.14 = (f32[512,256]{1,0:T(8,128)S(1)}, f32[512,256]{1,0:T(8,128)S(1)}, u32[]{:S(2)}, u32[]{:S(2)}) collective-permute-start(f32[512,256]{1,0:T(8,128)S(1)} %copy-done.16), channel_id=1, source_target_pairs={{0,1},{1,0},{2,3},{3,2},{4,5},{5,4},{6,7},{7,6},{8,9},{9,8},{10,11... | collective-permute-start | bytes 1572872 | tf_op jit(solution)/shard_map/ppermute | solution.py:33
  43.6 14.9 %collective-permute-start.16 = (f32[512,256]{1,0:T(8,128)S(1)}, f32[512,256]{1,0:T(8,128)S(1)}, u32[]{:S(2)}, u32[]{:S(2)}) collective-permute-start(f32[512,256]{1,0:T(8,128)S(1)} %add.33), channel_id=1, source_target_pairs={{0,2},{1,3},{2,0},{3,1},{4,6},{5,7},{6,4},{7,5},{8,10},{9,11},{10,... | collective-permute-start | bytes 1572872 | tf_op jit(solution)/shard_map/ppermute | solution.py:33
  48.1 20.5 %collective-permute-start.23 = (f32[512,256]{1,0:T(8,128)S(1)}, f32[512,256]{1,0:T(8,128)S(1)}, u32[]{:S(2)}, u32[]{:S(2)}) collective-permute-start(f32[512,256]{1,0:T(8,128)S(1)} %add.34), channel_id=1, source_target_pairs={{0,2},{1,3},{2,0},{3,1},{4,6},{5,7},{6,4},{7,5},{8,10},{9,11},{10,... | collective-permute-start | bytes 1572872 | tf_op jit(solution)/shard_map/ppermute | solution.py:33
  48.4 20.2 %collective-permute-start.21 = (f32[512,256]{1,0:T(8,128)S(1)}, f32[512,256]{1,0:T(8,128)S(1)}, u32[]{:S(2)}, u32[]{:S(2)}) collective-permute-start(f32[512,256]{1,0:T(8,128)S(1)} %copy-done.15), channel_id=1, source_target_pairs={{0,1},{1,0},{2,3},{3,2},{4,5},{5,4},{6,7},{7,6},{8,9},{9,8},{10,11... | collective-permute-start | bytes 1572872 | tf_op jit(solution)/shard_map/ppermute | solution.py:33
  48.4 22.1 %collective-permute-start.3 = (f32[4,64,256]{2,1,0:T(8,128)S(1)}, f32[4,64,256]{2,1,0:T(8,128)S(1)}, u32[]{:S(2)}, u32[]{:S(2)}) collective-permute-start(f32[4,64,256]{2,1,0:T(8,128)S(1)} %get-tuple-element.81), channel_id=1, source_target_pairs={{0,16},{4,20},{8,24},{12,28},{16,0},{20,4},{24,8},{28,12},{1,17},{... | collective-permute-start | bytes 786440 | tf_op jit(solution)/shard_map/ppermute | solution.py:33
  69.0 16.5 %collective-permute-start.24 = (f32[4,64,256]{2,1,0:T(8,128)S(1)}, f32[4,64,256]{2,1,0:T(8,128)S(1)}, u32[]{:S(2)}, u32[]{:S(2)}) collective-permute-start(f32[4,64,256]{2,1,0:T(8,128)S(1)} %get-tuple-element.120), channel_id=1, source_target_pairs={{0,4},{4,0},{8,12},{12,8},{16,20},{20,16},{24,28},{28,24},{1,5},{5... | collective-permute-start | bytes 786440 | tf_op jit(solution)/shard_map/ppermute | solution.py:33
  74.2 14.5 %collective-permute-start.11 = (f32[2,64,256]{2,1,0:T(8,128)S(1)}, f32[2,64,256]{2,1,0:T(8,128)S(1)}, u32[]{:S(2)}, u32[]{:S(2)}) collective-permute-start(f32[2,64,256]{2,1,0:T(8,128)S(1)} %get-tuple-element.96), channel_id=1, source_target_pairs={{0,8},{4,12},{8,0},{12,4},{16,24},{20,28},{24,16},{28,20},{1,9},{5... | collective-permute-start | bytes 393224 | tf_op jit(solution)/shard_map/ppermute | solution.py:33
  85.5 19.9 %collective-permute-start.18 = (f32[2,64,256]{2,1,0:T(8,128)S(1)}, f32[2,64,256]{2,1,0:T(8,128)S(1)}, u32[]{:S(2)}, u32[]{:S(2)}) collective-permute-start(f32[2,64,256]{2,1,0:T(8,128)S(1)} %get-tuple-element.109), channel_id=1, source_target_pairs={{0,8},{4,12},{8,0},{12,4},{16,24},{20,28},{24,16},{28,20},{1,9},{5... | collective-permute-start | bytes 393224 | tf_op jit(solution)/shard_map/ppermute | solution.py:33
  85.9 20.8 %collective-permute-start.19 = (f32[2,64,256]{2,1,0:T(8,128)S(1)}, f32[2,64,256]{2,1,0:T(8,128)S(1)}, u32[]{:S(2)}, u32[]{:S(2)}) collective-permute-start(f32[2,64,256]{2,1,0:T(8,128)S(1)} %get-tuple-element.110), channel_id=1, source_target_pairs={{0,16},{4,20},{8,24},{12,28},{16,0},{20,4},{24,8},{28,12},{1,17},{... | collective-permute-start | bytes 393224 | tf_op jit(solution)/shard_map/ppermute | solution.py:33
  88.7 18.0 %collective-permute-start.20 = (f32[2,64,256]{2,1,0:T(8,128)S(1)}, f32[2,64,256]{2,1,0:T(8,128)S(1)}, u32[]{:S(2)}, u32[]{:S(2)}) collective-permute-start(f32[2,64,256]{2,1,0:T(8,128)S(1)} %get-tuple-element.111), channel_id=1, source_target_pairs={{0,24},{4,28},{8,16},{12,20},{16,8},{20,12},{24,0},{28,4},{1,25},{... | collective-permute-start | bytes 393224 | tf_op jit(solution)/shard_map/ppermute | solution.py:33
  95.0 19.5 %collective-permute-start.26 = (f32[2,64,256]{2,1,0:T(8,128)S(1)}, f32[2,64,256]{2,1,0:T(8,128)S(1)}, u32[]{:S(2)}, u32[]{:S(2)}) collective-permute-start(f32[2,64,256]{2,1,0:T(8,128)S(1)} %get-tuple-element.123), channel_id=1, source_target_pairs={{0,16},{4,20},{8,24},{12,28},{16,0},{20,4},{24,8},{28,12},{1,17},{... | collective-permute-start | bytes 393224 | tf_op jit(solution)/shard_map/ppermute | solution.py:33
  134.1 19.9 %collective-permute-start.37 = (f32[64,640]{1,0:T(8,128)S(1)}, f32[64,640]{1,0:T(8,128)S(1)}, u32[]{:S(2)}, u32[]{:S(2)}) collective-permute-start(f32[64,640]{1,0:T(8,128)S(1)} %get-tuple-element.130), channel_id=1, source_target_pairs={{0,16},{4,20},{8,24},{12,28},{16,0},{20,4},{24,8},{28,12},{1,17},{... | collective-permute-start | bytes 491528 | tf_op jit(solution)/shard_map/ppermute | solution.py:33
  136.2 35.2 %collective-permute-start.42 = (f32[2,64,384]{2,1,0:T(8,128)S(1)}, f32[2,64,384]{2,1,0:T(8,128)S(1)}, u32[]{:S(2)}, u32[]{:S(2)}) collective-permute-start(f32[2,64,384]{2,1,0:T(8,128)S(1)} %get-tuple-element.138), channel_id=1, source_target_pairs={{0,16},{4,20},{8,24},{12,28},{16,0},{20,4},{24,8},{28,12},{1,17},{... | collective-permute-start | bytes 589832 | tf_op jit(solution)/shard_map/ppermute | solution.py:33
  137.2 35.1 %collective-permute-start.43 = (f32[2,64,384]{2,1,0:T(8,128)S(1)}, f32[2,64,384]{2,1,0:T(8,128)S(1)}, u32[]{:S(2)}, u32[]{:S(2)}) collective-permute-start(f32[2,64,384]{2,1,0:T(8,128)S(1)} %get-tuple-element.140), channel_id=1, source_target_pairs={{0,24},{4,28},{8,16},{12,20},{16,8},{20,12},{24,0},{28,4},{1,25},{... | collective-permute-start | bytes 589832 | tf_op jit(solution)/shard_map/ppermute | solution.py:33
  139.6 32.7 %collective-permute-start.41 = (f32[2,64,384]{2,1,0:T(8,128)S(1)}, f32[2,64,384]{2,1,0:T(8,128)S(1)}, u32[]{:S(2)}, u32[]{:S(2)}) collective-permute-start(f32[2,64,384]{2,1,0:T(8,128)S(1)} %get-tuple-element.136), channel_id=1, source_target_pairs={{0,8},{4,12},{8,0},{12,4},{16,24},{20,28},{24,16},{28,20},{1,9},{5... | collective-permute-start | bytes 589832 | tf_op jit(solution)/shard_map/ppermute | solution.py:33
  139.7 29.1 %collective-permute-start.38 = (f32[64,640]{1,0:T(8,128)S(1)}, f32[64,640]{1,0:T(8,128)S(1)}, u32[]{:S(2)}, u32[]{:S(2)}) collective-permute-start(f32[64,640]{1,0:T(8,128)S(1)} %get-tuple-element.131), channel_id=1, source_target_pairs={{0,20},{4,16},{8,28},{12,24},{16,4},{20,0},{24,12},{28,8},{1,21},{... | collective-permute-start | bytes 491528 | tf_op jit(solution)/shard_map/ppermute | solution.py:33
  154.0 31.1 %collective-permute-start.34 = (f32[64,1024]{1,0:T(8,128)S(1)}, f32[64,1024]{1,0:T(8,128)S(1)}, u32[]{:S(2)}, u32[]{:S(2)}) collective-permute-start(f32[64,1024]{1,0:T(8,128)S(1)} %get-tuple-element.126), channel_id=1, source_target_pairs={{0,4},{4,0},{8,12},{12,8},{16,20},{20,16},{24,28},{28,24},{1,5},{5... | collective-permute-start | bytes 786440 | tf_op jit(solution)/shard_map/ppermute | solution.py:33
  172.3 14.5 %collective-permute-start.35 = (f32[64,1024]{1,0:T(8,128)S(1)}, f32[64,1024]{1,0:T(8,128)S(1)}, u32[]{:S(2)}, u32[]{:S(2)}) collective-permute-start(f32[64,1024]{1,0:T(8,128)S(1)} %get-tuple-element.127), channel_id=1, source_target_pairs={{0,8},{4,12},{8,0},{12,4},{16,24},{20,28},{24,16},{28,20},{1,9},{5... | collective-permute-start | bytes 786440 | tf_op jit(solution)/shard_map/ppermute | solution.py:33
  172.3 18.5 %collective-permute-start.36 = (f32[64,1024]{1,0:T(8,128)S(1)}, f32[64,1024]{1,0:T(8,128)S(1)}, u32[]{:S(2)}, u32[]{:S(2)}) collective-permute-start(f32[64,1024]{1,0:T(8,128)S(1)} %get-tuple-element.128), channel_id=1, source_target_pairs={{0,12},{4,8},{8,4},{12,0},{16,28},{20,24},{24,20},{28,16},{1,13},{... | collective-permute-start | bytes 786440 | tf_op jit(solution)/shard_map/ppermute | solution.py:33
  (40 other events, 491.3 us)

commit v6 on v5

--- a/solution.py
+++ b/solution.py
@@ -121,6 +121,21 @@
         name="first",
     )(at, features, upstream)
     return list(outs[:COUNT]), list(outs[COUNT:])
+
+
+def tick_kernel(in_ref, out_ref):
+    out_ref[...] = in_ref[...]
+
+
+def tick(value):
+    return pl.pallas_call(
+        tick_kernel,
+        in_specs=[VMEM],
+        out_specs=VMEM,
+        out_shape=jax.ShapeDtypeStruct(value.shape, value.dtype),
+        compiler_params=pltpu.CompilerParams(vmem_limit_bytes=4 << 20),
+        name="tick",
+    )(value)
 
 
 def base_kernel(weights_ref, momentum_ref, out_ref):
@@ -526,10 +541,16 @@
     bit = bits[-1]
     mirror = list(regroup(here, held, bit, without(group, bit), skips))
     later = [*range(group // 2, group), *range(1, group // 2)]
+    i = later.pop(0)
+    mirror[i] = flip(after(mirror[i], packed), "worker", spread_bits(i, bit))
+    mark = tick(packed)
     rounds = [("worker", [2 * i for i in range(1, group)]), ("worker", [1])]
     rounds += [("tok", [1 << level]) for level in range(levels)]
     for axis, masks in rounds:
-        packed = sum([flip(packed, axis, mask) for mask in masks], packed)
+        terms = [packed]
+        for mask in masks:
+            terms.append(flip(packed, axis, mask))
+        packed = sum(terms[1:], terms[0])
         if later:
             i = later.pop(0)
             mirror[i] = flip(after(mirror[i], packed), "worker", spread_bits(i, bit))
@@ -551,7 +572,7 @@
     for mask, value in zip(near, out):
         pieces.append(flip(value, "worker", mask) if mask else value)
         spots.append((mask ^ group, SHARED))
-    new = place(here, pieces, tuple(spots), rows, width)
+    new = place(here, [*pieces, mark], tuple(spots), rows, width)
     return new[None], velocity[None]
 
 

time: 197 us -> 197 us (level)
  no operation moved by 1% of the time
where the time goes in v6:
time: 197 us
  waiting for transfers between devices  97.6 us (50%)
  starting transfers between devices  66.7 us (34%)
  Pallas kernels  28.3 us (14%)
  local copies, waits for them, and re-layouts  2.73 us (1%)
    ppermute x47, waiting for transfers between devices, flip(): return lax.ppermute(value, axis, pairs)  97.6 us
    ppermute x47, starting transfers between devices, flip(): return lax.ppermute(value, axis, pairs)  66.7 us
    pallas_call x2, Pallas kernels, multiply(): pl.pallas_call(functools.partial(first_kernel, rows, cuts), in_specs=[SME...  13.2 us
  transfers between devices with their start and end apart: 47, of which 19 were waited for; matrix products, arithmetic and copies ran while one was open for 0% of the time, Pallas kernels for 9%

profile of v6, /device:TPU:0, one launch (start us, length us, event | category | flops | bytes accessed | tf_op | source)
XLA Modules:
  0.0 196.6 jit_solution(525931117102815600)
XLA Ops:
  0.6 6.6 %first.2 = (f32[512,256]{1,0:T(8,128)}, f32[512,256]{1,0:T(8,128)}, f32[512,256]{1,0:T(8,128)}, f32[512,256]{1,0:T(8,128)}, f32[512,256]{1,0:T(8,128)}, /*index=...) custom-call(s32[1]{0:T(128)} %bitcast.2.at_ref, bf16[1,1536,2048]{2,1,0:T(8,128)(2,1)} %features_hbm.3, ...), custom_call_target="tpu_custom_call" | custom-call | tf_op jit(solution)/shard_map/first/pallas_call | solution.py:110
  7.8 6.6 %first.3 = (f32[512,256]{1,0:T(8,128)}, f32[512,256]{1,0:T(8,128)}, f32[512,256]{1,0:T(8,128)}, f32[512,256]{1,0:T(8,128)}, f32[512,256]{1,0:T(8,128)}, /*index=...) custom-call(s32[1]{0:T(128)} %bitcast.1.at_ref, bf16[1,1536,2048]{2,1,0:T(8,128)(2,1)} %features_hbm.3, ...), custom_call_target="tpu_custom_call" | custom-call | tf_op jit(solution)/shard_map/first/pallas_call | solution.py:110
  15.8 2.6 %collective-permute-start.2 = (f32[512,256]{1,0:T(8,128)}, f32[512,256]{1,0:T(8,128)}, u32[]{:S(2)}, u32[]{:S(2)}) collective-permute-start(f32[512,256]{1,0:T(8,128)} %add.31), channel_id=1, source_target_pairs={{0,2},{1,3},{2,0},{3,1},{4,6},{5,7},{6,4},{7,5},{8,10},{9,11},{10,... | collective-permute-start | bytes 1572872 | tf_op jit(solution)/shard_map/ppermute | solution.py:33
  22.0 9.6 %collective-permute-done.2.rest_2_ = f32[512,256]{1,0:T(8,128)} collective-permute-done((f32[512,256]{1,0:T(8,128)}, f32[512,256]{1,0:T(8,128)}, u32[]{:S(2)}, u32[]{:S(2)}) %collective-permute-start.2) | collective-permute-done | bytes 524320 | tf_op jit(solution)/shard_map/ppermute | solution.py:33
  33.7 8.8 %collective-permute-done.9.rest_2_ = f32[512,256]{1,0:T(8,128)} collective-permute-done((f32[512,256]{1,0:T(8,128)S(1)}, f32[512,256]{1,0:T(8,128)}, u32[]{:S(2)}, u32[]{:S(2)}) %collective-permute-start.9) | collective-permute-done | bytes 524320 | tf_op jit(solution)/shard_map/ppermute | solution.py:33
  48.4 2.8 %collective-permute-start.3 = (f32[4,64,256]{2,1,0:T(8,128)S(1)}, f32[4,64,256]{2,1,0:T(8,128)S(1)}, u32[]{:S(2)}, u32[]{:S(2)}) collective-permute-start(f32[4,64,256]{2,1,0:T(8,128)S(1)} %get-tuple-element.81), channel_id=1, source_target_pairs={{0,16},{4,20},{8,24},{12,28},{16,0},{20,4},{24,8},{28,12},{1,17},{... | collective-permute-start | bytes 786440 | tf_op jit(solution)/shard_map/ppermute | solution.py:33
  51.2 7.3 %collective-permute-done.16.rest_2_ = f32[512,256]{1,0:T(8,128)S(1)} collective-permute-done((f32[512,256]{1,0:T(8,128)S(1)}, f32[512,256]{1,0:T(8,128)S(1)}, u32[]{:S(2)}, u32[]{:S(2)}) %collective-permute-start.16) | collective-permute-done | bytes 524320 | tf_op jit(solution)/shard_map/ppermute | solution.py:33
  60.8 7.8 %collective-permute-done.23.rest_2_ = f32[512,256]{1,0:T(8,128)S(1)} collective-permute-done((f32[512,256]{1,0:T(8,128)S(1)}, f32[512,256]{1,0:T(8,128)S(1)}, u32[]{:S(2)}, u32[]{:S(2)}) %collective-permute-start.23) | collective-permute-done | bytes 524320 | tf_op jit(solution)/shard_map/ppermute | solution.py:33
  75.9 6.1 %collective-permute-done.4.rest_1_.rest_4_.rest_2_ = f32[2,64,256]{2,1,0:T(8,128)S(1)} collective-permute-done((f32[2,64,256]{2,1,0:T(8,128)S(1)}, f32[2,64,256]{2,1,0:T(8,128)S(1)}, u32[]{:S(2)}, u32[]{:S(2)}) %collective-permute-start.4) | collective-permute-done | bytes 131104 | tf_op jit(solution)/shard_map/ppermute | solution.py:33
  85.9 2.8 %collective-permute-start.19 = (f32[2,64,256]{2,1,0:T(8,128)S(1)}, f32[2,64,256]{2,1,0:T(8,128)S(1)}, u32[]{:S(2)}, u32[]{:S(2)}) collective-permute-start(f32[2,64,256]{2,1,0:T(8,128)S(1)} %get-tuple-element.110), channel_id=1, source_target_pairs={{0,16},{4,20},{8,24},{12,28},{16,0},{20,4},{24,8},{28,12},{1,17},{... | collective-permute-start | bytes 393224 | tf_op jit(solution)/shard_map/ppermute | solution.py:33
  90.0 4.8 %collective-permute-done.12.rest_2_.rest_9_.rest_7_ = f32[2,64,256]{2,1,0:T(8,128)S(1)} collective-permute-done((f32[2,64,256]{2,1,0:T(8,128)S(1)}, f32[2,64,256]{2,1,0:T(8,128)S(1)}, u32[]{:S(2)}, u32[]{:S(2)}) %collective-permute-start.12) | collective-permute-done | bytes 131104 | tf_op jit(solution)/shard_map/ppermute | solution.py:33
  95.0 10.3 %collective-permute-start.26 = (f32[2,64,256]{2,1,0:T(8,128)S(1)}, f32[2,64,256]{2,1,0:T(8,128)S(1)}, u32[]{:S(2)}, u32[]{:S(2)}) collective-permute-start(f32[2,64,256]{2,1,0:T(8,128)S(1)} %get-tuple-element.123), channel_id=1, source_target_pairs={{0,16},{4,20},{8,24},{12,28},{16,0},{20,4},{24,8},{28,12},{1,17},{... | collective-permute-start | bytes 393224 | tf_op jit(solution)/shard_map/ppermute | solution.py:33
  107.0 7.5 %collective-permute-done.26.rest_5_.rest_17_ = f32[2,64,256]{2,1,0:T(8,128)S(1)} collective-permute-done((f32[2,64,256]{2,1,0:T(8,128)S(1)}, f32[2,64,256]{2,1,0:T(8,128)S(1)}, u32[]{:S(2)}, u32[]{:S(2)}) %collective-permute-start.26) | collective-permute-done | bytes 131104 | tf_op jit(solution)/shard_map/ppermute | solution.py:33
  115.5 2.9 %collective-permute-start.30 = (f32[8,128]{1,0:T(8,128)S(1)}, f32[8,128]{1,0:T(8,128)S(1)}, u32[]{:S(2)}, u32[]{:S(2)}) collective-permute-start(f32[8,128]{1,0:T(8,128)S(1)} %pack.1.in_ref), channel_id=1, source_target_pairs={{0,24},{4,28},{8,16},{12,20},{16,8},{20,12},{24,0},{28,4},{1,25},{... | collective-permute-start | bytes 12296 | tf_op jit(solution)/shard_map/ppermute | solution.py:33
  137.2 2.4 %collective-permute-start.43 = (f32[2,64,384]{2,1,0:T(8,128)S(1)}, f32[2,64,384]{2,1,0:T(8,128)S(1)}, u32[]{:S(2)}, u32[]{:S(2)}) collective-permute-start(f32[2,64,384]{2,1,0:T(8,128)S(1)} %get-tuple-element.140), channel_id=1, source_target_pairs={{0,24},{4,28},{8,16},{12,20},{16,8},{20,12},{24,0},{28,4},{1,25},{... | collective-permute-start | bytes 589832 | tf_op jit(solution)/shard_map/ppermute | solution.py:33
  139.7 3.1 %collective-permute-start.38 = (f32[64,640]{1,0:T(8,128)S(1)}, f32[64,640]{1,0:T(8,128)S(1)}, u32[]{:S(2)}, u32[]{:S(2)}) collective-permute-start(f32[64,640]{1,0:T(8,128)S(1)} %get-tuple-element.131), channel_id=1, source_target_pairs={{0,20},{4,16},{8,28},{12,24},{16,4},{20,0},{24,12},{28,8},{1,21},{... | collective-permute-start | bytes 491528 | tf_op jit(solution)/shard_map/ppermute | solution.py:33
  142.8 11.2 %collective-permute-done.37.rest_4_ = f32[64,640]{1,0:T(8,128)S(1)} collective-permute-done((f32[64,640]{1,0:T(8,128)S(1)}, f32[64,640]{1,0:T(8,128)S(1)}, u32[]{:S(2)}, u32[]{:S(2)}) %collective-permute-start.37) | collective-permute-done | bytes 163872 | tf_op jit(solution)/shard_map/ppermute | solution.py:33
  155.9 12.9 %collective-permute-done.38.rest_5_ = f32[64,640]{1,0:T(8,128)S(1)} collective-permute-done((f32[64,640]{1,0:T(8,128)S(1)}, f32[64,640]{1,0:T(8,128)S(1)}, u32[]{:S(2)}, u32[]{:S(2)}) %collective-permute-start.38) | collective-permute-done | bytes 163872 | tf_op jit(solution)/shard_map/ppermute | solution.py:33
  168.8 2.5 %collective-permute-start.39 = (f32[64,640]{1,0:T(8,128)S(1)}, f32[64,640]{1,0:T(8,128)S(1)}, u32[]{:S(2)}, u32[]{:S(2)}) collective-permute-start(f32[64,640]{1,0:T(8,128)S(1)} %get-tuple-element.132), channel_id=1, source_target_pairs={{0,24},{4,28},{8,16},{12,20},{16,8},{20,12},{24,0},{28,4},{1,25},{... | collective-permute-start | bytes 491528 | tf_op jit(solution)/shard_map/ppermute | solution.py:33
  172.3 3.2 %collective-permute-start.36 = (f32[64,1024]{1,0:T(8,128)S(1)}, f32[64,1024]{1,0:T(8,128)S(1)}, u32[]{:S(2)}, u32[]{:S(2)}) collective-permute-start(f32[64,1024]{1,0:T(8,128)S(1)} %get-tuple-element.128), channel_id=1, source_target_pairs={{0,12},{4,8},{8,4},{12,0},{16,28},{20,24},{24,20},{28,16},{1,13},{... | collective-permute-start | bytes 786440 | tf_op jit(solution)/shard_map/ppermute | solution.py:33
  177.9 3.2 %collective-permute-done.40.rest_7_ = f32[64,640]{1,0:T(8,128)S(1)} collective-permute-done((f32[64,640]{1,0:T(8,128)S(1)}, f32[64,640]{1,0:T(8,128)S(1)}, u32[]{:S(2)}, u32[]{:S(2)}) %collective-permute-start.40) | collective-permute-done | bytes 163872 | tf_op jit(solution)/shard_map/ppermute | solution.py:33
  181.1 4.0 %collective-permute-start.45 = (f32[64,384]{1,0:T(8,128)S(1)}, f32[64,384]{1,0:T(8,128)S(1)}, u32[]{:S(2)}, u32[]{:S(2)}) collective-permute-start(f32[64,384]{1,0:T(8,128)S(1)} %get-tuple-element.143), channel_id=1, source_target_pairs={{0,8},{4,12},{8,0},{12,4},{16,24},{20,28},{24,16},{28,20},{1,9},{5... | collective-permute-start | bytes 294920 | tf_op jit(solution)/shard_map/ppermute | solution.py:33
  186.9 4.0 %collective-permute-done.36.rest_3_ = f32[64,1024]{1,0:T(8,128)S(1)} collective-permute-done((f32[64,1024]{1,0:T(8,128)S(1)}, f32[64,1024]{1,0:T(8,128)S(1)}, u32[]{:S(2)}, u32[]{:S(2)}) %collective-permute-start.36) | collective-permute-done | bytes 262176 | tf_op jit(solution)/shard_map/ppermute | solution.py:33
  190.9 2.3 %collective-permute-done.45.rest_10_ = f32[64,384]{1,0:T(8,128)S(1)} collective-permute-done((f32[64,384]{1,0:T(8,128)S(1)}, f32[64,384]{1,0:T(8,128)S(1)}, u32[]{:S(2)}, u32[]{:S(2)}) %collective-permute-start.45) | collective-permute-done | bytes 98336 | tf_op jit(solution)/shard_map/ppermute | solution.py:33
  (137 shorter events, 59.9 us)
Async XLA Ops:
  15.8 15.7 %collective-permute-start.2 = (f32[512,256]{1,0:T(8,128)}, f32[512,256]{1,0:T(8,128)}, u32[]{:S(2)}, u32[]{:S(2)}) collective-permute-start(f32[512,256]{1,0:T(8,128)} %add.31), channel_id=1, source_target_pairs={{0,2},{1,3},{2,0},{3,1},{4,6},{5,7},{6,4},{7,5},{8,10},{9,11},{10,... | collective-permute-start | bytes 1572872 | tf_op jit(solution)/shard_map/ppermute | solution.py:33
  18.5 24.0 %collective-permute-start.9 = (f32[512,256]{1,0:T(8,128)S(1)}, f32[512,256]{1,0:T(8,128)}, u32[]{:S(2)}, u32[]{:S(2)}) collective-permute-start(f32[512,256]{1,0:T(8,128)S(1)} %add.32), channel_id=1, source_target_pairs={{0,2},{1,3},{2,0},{3,1},{4,6},{5,7},{6,4},{7,5},{8,10},{9,11},{10,... | collective-permute-start | bytes 1572872 | tf_op jit(solution)/shard_map/ppermute | solution.py:33
  18.6 23.9 %collective-permute-start.15 = (f32[512,256]{1,0:T(8,128)}, f32[512,256]{1,0:T(8,128)}, u32[]{:S(2)}, u32[]{:S(2)}) collective-permute-start(f32[512,256]{1,0:T(8,128)} %get-tuple-element.103), channel_id=1, source_target_pairs={{0,1},{1,0},{2,3},{3,2},{4,5},{5,4},{6,7},{7,6},{8,9},{9,8},{10,11... | collective-permute-start | bytes 1572872 | tf_op jit(solution)/shard_map/ppermute | solution.py:33
  18.8 26.6 %collective-permute-start.7 = (f32[512,256]{1,0:T(8,128)}, f32[512,256]{1,0:T(8,128)}, u32[]{:S(2)}, u32[]{:S(2)}) collective-permute-start(f32[512,256]{1,0:T(8,128)} %get-tuple-element.87), channel_id=1, source_target_pairs={{0,1},{1,0},{2,3},{3,2},{4,5},{5,4},{6,7},{7,6},{8,9},{9,8},{10,11... | collective-permute-start | bytes 1572872 | tf_op jit(solution)/shard_map/ppermute | solution.py:33
  20.0 27.8 %collective-permute-start.22 = (f32[512,256]{1,0:T(8,128)}, f32[512,256]{1,0:T(8,128)S(1)}, u32[]{:S(2)}, u32[]{:S(2)}) collective-permute-start(f32[512,256]{1,0:T(8,128)} %get-tuple-element.116), channel_id=1, source_target_pairs={{0,1},{1,0},{2,3},{3,2},{4,5},{5,4},{6,7},{7,6},{8,9},{9,8},{10,11... | collective-permute-start | bytes 1572872 | tf_op jit(solution)/shard_map/ppermute | solution.py:33
  31.5 28.6 %collective-permute-start.14 = (f32[512,256]{1,0:T(8,128)S(1)}, f32[512,256]{1,0:T(8,128)S(1)}, u32[]{:S(2)}, u32[]{:S(2)}) collective-permute-start(f32[512,256]{1,0:T(8,128)S(1)} %copy-done.16), channel_id=1, source_target_pairs={{0,1},{1,0},{2,3},{3,2},{4,5},{5,4},{6,7},{7,6},{8,9},{9,8},{10,11... | collective-permute-start | bytes 1572872 | tf_op jit(solution)/shard_map/ppermute | solution.py:33
  43.6 14.9 %collective-permute-start.16 = (f32[512,256]{1,0:T(8,128)S(1)}, f32[512,256]{1,0:T(8,128)S(1)}, u32[]{:S(2)}, u32[]{:S(2)}) collective-permute-start(f32[512,256]{1,0:T(8,128)S(1)} %add.33), channel_id=1, source_target_pairs={{0,2},{1,3},{2,0},{3,1},{4,6},{5,7},{6,4},{7,5},{8,10},{9,11},{10,... | collective-permute-start | bytes 1572872 | tf_op jit(solution)/shard_map/ppermute | solution.py:33
  48.1 20.5 %collective-permute-start.23 = (f32[512,256]{1,0:T(8,128)S(1)}, f32[512,256]{1,0:T(8,128)S(1)}, u32[]{:S(2)}, u32[]{:S(2)}) collective-permute-start(f32[512,256]{1,0:T(8,128)S(1)} %add.34), channel_id=1, source_target_pairs={{0,2},{1,3},{2,0},{3,1},{4,6},{5,7},{6,4},{7,5},{8,10},{9,11},{10,... | collective-permute-start | bytes 1572872 | tf_op jit(solution)/shard_map/ppermute | solution.py:33
  48.4 20.2 %collective-permute-start.21 = (f32[512,256]{1,0:T(8,128)S(1)}, f32[512,256]{1,0:T(8,128)S(1)}, u32[]{:S(2)}, u32[]{:S(2)}) collective-permute-start(f32[512,256]{1,0:T(8,128)S(1)} %copy-done.15), channel_id=1, source_target_pairs={{0,1},{1,0},{2,3},{3,2},{4,5},{5,4},{6,7},{7,6},{8,9},{9,8},{10,11... | collective-permute-start | bytes 1572872 | tf_op jit(solution)/shard_map/ppermute | solution.py:33
  48.4 22.1 %collective-permute-start.3 = (f32[4,64,256]{2,1,0:T(8,128)S(1)}, f32[4,64,256]{2,1,0:T(8,128)S(1)}, u32[]{:S(2)}, u32[]{:S(2)}) collective-permute-start(f32[4,64,256]{2,1,0:T(8,128)S(1)} %get-tuple-element.81), channel_id=1, source_target_pairs={{0,16},{4,20},{8,24},{12,28},{16,0},{20,4},{24,8},{28,12},{1,17},{... | collective-permute-start | bytes 786440 | tf_op jit(solution)/shard_map/ppermute | solution.py:33
  69.0 16.5 %collective-permute-start.24 = (f32[4,64,256]{2,1,0:T(8,128)S(1)}, f32[4,64,256]{2,1,0:T(8,128)S(1)}, u32[]{:S(2)}, u32[]{:S(2)}) collective-permute-start(f32[4,64,256]{2,1,0:T(8,128)S(1)} %get-tuple-element.120), channel_id=1, source_target_pairs={{0,4},{4,0},{8,12},{12,8},{16,20},{20,16},{24,28},{28,24},{1,5},{5... | collective-permute-start | bytes 786440 | tf_op jit(solution)/shard_map/ppermute | solution.py:33
  74.2 14.5 %collective-permute-start.11 = (f32[2,64,256]{2,1,0:T(8,128)S(1)}, f32[2,64,256]{2,1,0:T(8,128)S(1)}, u32[]{:S(2)}, u32[]{:S(2)}) collective-permute-start(f32[2,64,256]{2,1,0:T(8,128)S(1)} %get-tuple-element.96), channel_id=1, source_target_pairs={{0,8},{4,12},{8,0},{12,4},{16,24},{20,28},{24,16},{28,20},{1,9},{5... | collective-permute-start | bytes 393224 | tf_op jit(solution)/shard_map/ppermute | solution.py:33
  85.5 19.9 %collective-permute-start.18 = (f32[2,64,256]{2,1,0:T(8,128)S(1)}, f32[2,64,256]{2,1,0:T(8,128)S(1)}, u32[]{:S(2)}, u32[]{:S(2)}) collective-permute-start(f32[2,64,256]{2,1,0:T(8,128)S(1)} %get-tuple-element.109), channel_id=1, source_target_pairs={{0,8},{4,12},{8,0},{12,4},{16,24},{20,28},{24,16},{28,20},{1,9},{5... | collective-permute-start | bytes 393224 | tf_op jit(solution)/shard_map/ppermute | solution.py:33
  85.9 20.8 %collective-permute-start.19 = (f32[2,64,256]{2,1,0:T(8,128)S(1)}, f32[2,64,256]{2,1,0:T(8,128)S(1)}, u32[]{:S(2)}, u32[]{:S(2)}) collective-permute-start(f32[2,64,256]{2,1,0:T(8,128)S(1)} %get-tuple-element.110), channel_id=1, source_target_pairs={{0,16},{4,20},{8,24},{12,28},{16,0},{20,4},{24,8},{28,12},{1,17},{... | collective-permute-start | bytes 393224 | tf_op jit(solution)/shard_map/ppermute | solution.py:33
  88.7 18.0 %collective-permute-start.20 = (f32[2,64,256]{2,1,0:T(8,128)S(1)}, f32[2,64,256]{2,1,0:T(8,128)S(1)}, u32[]{:S(2)}, u32[]{:S(2)}) collective-permute-start(f32[2,64,256]{2,1,0:T(8,128)S(1)} %get-tuple-element.111), channel_id=1, source_target_pairs={{0,24},{4,28},{8,16},{12,20},{16,8},{20,12},{24,0},{28,4},{1,25},{... | collective-permute-start | bytes 393224 | tf_op jit(solution)/shard_map/ppermute | solution.py:33
  95.0 19.5 %collective-permute-start.26 = (f32[2,64,256]{2,1,0:T(8,128)S(1)}, f32[2,64,256]{2,1,0:T(8,128)S(1)}, u32[]{:S(2)}, u32[]{:S(2)}) collective-permute-start(f32[2,64,256]{2,1,0:T(8,128)S(1)} %get-tuple-element.123), channel_id=1, source_target_pairs={{0,16},{4,20},{8,24},{12,28},{16,0},{20,4},{24,8},{28,12},{1,17},{... | collective-permute-start | bytes 393224 | tf_op jit(solution)/shard_map/ppermute | solution.py:33
  134.1 19.9 %collective-permute-start.37 = (f32[64,640]{1,0:T(8,128)S(1)}, f32[64,640]{1,0:T(8,128)S(1)}, u32[]{:S(2)}, u32[]{:S(2)}) collective-permute-start(f32[64,640]{1,0:T(8,128)S(1)} %get-tuple-element.130), channel_id=1, source_target_pairs={{0,16},{4,20},{8,24},{12,28},{16,0},{20,4},{24,8},{28,12},{1,17},{... | collective-permute-start | bytes 491528 | tf_op jit(solution)/shard_map/ppermute | solution.py:33
  136.2 35.2 %collective-permute-start.42 = (f32[2,64,384]{2,1,0:T(8,128)S(1)}, f32[2,64,384]{2,1,0:T(8,128)S(1)}, u32[]{:S(2)}, u32[]{:S(2)}) collective-permute-start(f32[2,64,384]{2,1,0:T(8,128)S(1)} %get-tuple-element.138), channel_id=1, source_target_pairs={{0,16},{4,20},{8,24},{12,28},{16,0},{20,4},{24,8},{28,12},{1,17},{... | collective-permute-start | bytes 589832 | tf_op jit(solution)/shard_map/ppermute | solution.py:33
  137.2 35.1 %collective-permute-start.43 = (f32[2,64,384]{2,1,0:T(8,128)S(1)}, f32[2,64,384]{2,1,0:T(8,128)S(1)}, u32[]{:S(2)}, u32[]{:S(2)}) collective-permute-start(f32[2,64,384]{2,1,0:T(8,128)S(1)} %get-tuple-element.140), channel_id=1, source_target_pairs={{0,24},{4,28},{8,16},{12,20},{16,8},{20,12},{24,0},{28,4},{1,25},{... | collective-permute-start | bytes 589832 | tf_op jit(solution)/shard_map/ppermute | solution.py:33
  139.6 32.7 %collective-permute-start.41 = (f32[2,64,384]{2,1,0:T(8,128)S(1)}, f32[2,64,384]{2,1,0:T(8,128)S(1)}, u32[]{:S(2)}, u32[]{:S(2)}) collective-permute-start(f32[2,64,384]{2,1,0:T(8,128)S(1)} %get-tuple-element.136), channel_id=1, source_target_pairs={{0,8},{4,12},{8,0},{12,4},{16,24},{20,28},{24,16},{28,20},{1,9},{5... | collective-permute-start | bytes 589832 | tf_op jit(solution)/shard_map/ppermute | solution.py:33
  139.7 29.1 %collective-permute-start.38 = (f32[64,640]{1,0:T(8,128)S(1)}, f32[64,640]{1,0:T(8,128)S(1)}, u32[]{:S(2)}, u32[]{:S(2)}) collective-permute-start(f32[64,640]{1,0:T(8,128)S(1)} %get-tuple-element.131), channel_id=1, source_target_pairs={{0,20},{4,16},{8,28},{12,24},{16,4},{20,0},{24,12},{28,8},{1,21},{... | collective-permute-start | bytes 491528 | tf_op jit(solution)/shard_map/ppermute | solution.py:33
  154.0 31.1 %collective-permute-start.34 = (f32[64,1024]{1,0:T(8,128)S(1)}, f32[64,1024]{1,0:T(8,128)S(1)}, u32[]{:S(2)}, u32[]{:S(2)}) collective-permute-start(f32[64,1024]{1,0:T(8,128)S(1)} %get-tuple-element.126), channel_id=1, source_target_pairs={{0,4},{4,0},{8,12},{12,8},{16,20},{20,16},{24,28},{28,24},{1,5},{5... | collective-permute-start | bytes 786440 | tf_op jit(solution)/shard_map/ppermute | solution.py:33
  172.3 14.5 %collective-permute-start.35 = (f32[64,1024]{1,0:T(8,128)S(1)}, f32[64,1024]{1,0:T(8,128)S(1)}, u32[]{:S(2)}, u32[]{:S(2)}) collective-permute-start(f32[64,1024]{1,0:T(8,128)S(1)} %get-tuple-element.127), channel_id=1, source_target_pairs={{0,8},{4,12},{8,0},{12,4},{16,24},{20,28},{24,16},{28,20},{1,9},{5... | collective-permute-start | bytes 786440 | tf_op jit(solution)/shard_map/ppermute | solution.py:33
  172.3 18.5 %collective-permute-start.36 = (f32[64,1024]{1,0:T(8,128)S(1)}, f32[64,1024]{1,0:T(8,128)S(1)}, u32[]{:S(2)}, u32[]{:S(2)}) collective-permute-start(f32[64,1024]{1,0:T(8,128)S(1)} %get-tuple-element.128), channel_id=1, source_target_pairs={{0,12},{4,8},{8,4},{12,0},{16,28},{20,24},{24,20},{28,16},{1,13},{... | collective-permute-start | bytes 786440 | tf_op jit(solution)/shard_map/ppermute | solution.py:33
  (40 other events, 491.3 us)
